TPU v7x, 32 devices: a whole 2x2x4 slice. The times are simulated.
32 devices in a mesh: comp: 4 (over y, core), tile: 8 (over z, x).
Axes of the slice: x: 2, y: 2, z: 4, core: 2. Of those that a mesh axis runs over, the one named last changes fastest.
Arguments:
- column_state: float32 [4, 8, 4, 16, 2048], P('comp', 'tile'), may hold values from -6 to 6
- mixing: float32 [2, 4, 16], replicated, may hold values from 0.02 to 0.24
- vertical: float32 [2, 16, 16], replicated, may hold values from -1.5 to 1.5
- flux_coef: float32 [2, 4], replicated, may hold values from 0.5 to 1.5
- atm_block: int32 [4, 8, 16], P('comp', 'tile'), may hold values from 0 to 15
- ocean_block: int32 [4, 8, 16], P('comp', 'tile'), may hold values from 0 to 15
- tile_offset: int32 [4, 8, 16], P('comp', 'tile'), may hold values from 0 to 6
- remap_weights: bfloat16 [4, 8, 16, 128, 128], P('comp', 'tile'), may hold values from 0 to 0.119628906
- ocean_mask: int32 [8, 2048], P('tile'), may hold values 0 or 1
Outputs:
- new_state: float32 [4, 8, 4, 16, 2048], P('comp', 'tile')
Inputs may be any that keep to these rules, and one draw needn't show every extreme that they name: `atm_block`: entries at comp index 3 are not read.
All inputs are finite; a program needn't handle non-finite values. No bound on the sum of `ocean_mask` on one device may be relied on, other than what follows from the above.
Results may differ from a plain program's by a relative error of at most 0.0003.
Values sent between devices are 32-bit elements; how exact they have to be, the bound alone decides.
No kernel may reach another device: no remote copies, remote signals or barrier semaphores. Data moves between devices by JAX's collectives and lax.ppermute only.
A program may use at most 64 MiB of HBM per device.

v0:
```python
import jax
import jax.numpy as jnp
from jax import lax
from jax.sharding import PartitionSpec as P

REACH = 3
SUB = 2


def extended(cells, sides, width):
    for axis, dim in sides:
        count = lax.axis_size(axis)
        head = lax.slice_in_dim(cells, 0, width, axis=dim)
        tail = lax.slice_in_dim(cells, cells.shape[dim] - width, cells.shape[dim], axis=dim)
        cells = jnp.concatenate(
            [
                lax.ppermute(tail, axis, [(i, (i + 1) % count) for i in range(count)]),
                cells,
                lax.ppermute(head, axis, [((i + 1) % count, i) for i in range(count)]),
            ],
            axis=dim,
        )
    return cells


def passed_along(value, axis, steps):
    count = lax.axis_size(axis)
    pairs = [(source, (source + steps) % count) for source in range(count)]
    return lax.ppermute(value, axis, pairs)


def local(
    column_state,
    mixing,
    vertical,
    flux_coef,
    atm_block,
    ocean_block,
    tile_offset,
    remap_weights,
    ocean_mask,
):
    fields = column_state[0, 0]
    cells = fields.shape[2]
    across = remap_weights.shape[3]
    ocean_cells = remap_weights.shape[4]
    oblocks = cells // ocean_cells
    spread = 2 * REACH + 1
    comp_index = lax.axis_index("comp")
    comp_count = lax.axis_size("comp")
    is_atmos = comp_index < comp_count - 1
    group = jnp.where(is_atmos, 0, 1).astype(jnp.int32)
    rates = lax.dynamic_index_in_dim(mixing, group, 0, keepdims=False)[:, :, None]
    operator = lax.dynamic_index_in_dim(vertical, group, 0, keepdims=False)
    for sweep in range(SUB):
        padded = extended(fields, (("tile", 2),), 1)
        fields = fields + rates * (padded[:, :, :-2] + padded[:, :, 2:] - 2.0 * fields)
    mixed = fields + jnp.einsum("lm,kmz->klz", operator, fields, precision=lax.Precision.HIGHEST)
    surface = jnp.tanh(flux_coef[0][:, None] * mixed[:, -1] + flux_coef[1][:, None] * mixed[:, -2])
    rounded = surface.astype(jnp.bfloat16)
    blocks = rounded.reshape(rounded.shape[0], cells // across, across)
    chosen = blocks[:, atm_block[0, 0], :]
    contrib = jnp.einsum(
        "knb,nbj->nkj", chosen, remap_weights[0, 0], preferred_element_type=jnp.float32
    )
    by_offset = (tile_offset[0, 0][:, None] == jnp.arange(spread, dtype=jnp.int32)[None, :]).astype(
        jnp.float32
    )
    by_block = (ocean_block[0, 0][:, None] == jnp.arange(oblocks, dtype=jnp.int32)[None, :]).astype(
        jnp.float32
    )
    buffers = jnp.einsum(
        "nd,no,nkj->dkoj", by_offset, by_block, contrib, precision=lax.Precision.HIGHEST
    )
    buffers = buffers.reshape(spread, rounded.shape[0], cells)
    buffers = jnp.where(is_atmos, buffers, 0.0)
    received = buffers[REACH]
    for offset in range(-REACH, REACH + 1):
        if offset != 0:
            received = received + passed_along(buffers[REACH + offset], "tile", offset)
    received = lax.psum(received, "comp")
    land = ocean_mask[0].astype(jnp.float32)
    atmosphere = mixed.at[:, -1].add(-0.5 * surface)
    ocean = mixed.at[:, 0].add(land[None, :] * received)
    result = jnp.where(is_atmos, atmosphere, ocean)
    return result[None, None]


def solution(mesh):
    placed = (
        P("comp", "tile", None, None, None),
        P(),
        P(),
        P(),
        P("comp", "tile", None),
        P("comp", "tile", None),
        P("comp", "tile", None),
        P("comp", "tile", None, None, None),
        P("tile", None),
    )
    return jax.shard_map(
        local,
        mesh=mesh,
        in_specs=placed,
        out_specs=P("comp", "tile", None, None, None),
        check_vma=False,
    )
```

profile of v0, /device:TPU:0, one launch (start us, length us, event | category | flops | bytes accessed | tf_op | source)
XLA Modules:
  0.0 47.1 jit_solution(6400851959491823201)
XLA Ops:
  0.0 0.0 copy-start
  0.0 1.4 %copy.46 = f32[1,1,4,16,2048]{4,2,3,1,0:T(4,128)S(1)} copy(f32[1,1,4,16,2048]{4,3,2,1,0:T(8,128)} %param.13) | data formatting | bytes 1048576 | tf_op args[0]
  1.4 0.1 fusion.36
  1.5 3.0 %collective-permute-start = (f32[4,16,1]{2,0,1:T(4,128)S(1)}, f32[4,16,1]{2,0,1:T(4,128)S(1)}, u32[]{:S(2)}, u32[]{:S(2)}) collective-permute-start(f32[4,16,1]{2,0,1:T(4,128)S(1)} %get-tuple-element.35), channel_id=1, source_target_pairs={{0,1},{1,2},{2,3},{3,4},{4,5},{5,6},{6,7},{7,0},{8,9},{9,10},{10,1... | collective-permute-start | bytes 776 | tf_op jit(solution)/shard_map/ppermute | solution.py:17
  4.5 3.1 %collective-permute-start.1 = (f32[4,16,1]{2,0,1:T(4,128)S(1)}, f32[4,16,1]{2,0,1:T(4,128)S(1)}, u32[]{:S(2)}, u32[]{:S(2)}) collective-permute-start(f32[4,16,1]{2,0,1:T(4,128)S(1)} %get-tuple-element.36), channel_id=1, source_target_pairs={{1,0},{2,1},{3,2},{4,3},{5,4},{6,5},{7,6},{0,7},{9,8},{10,9},{11,1... | collective-permute-start | bytes 776 | tf_op jit(solution)/shard_map/ppermute | solution.py:19
  7.6 0.0 copy-start.4
  7.6 0.7 %copy-done.4 = f32[2,4]{1,0:T(2,128)S(1)} copy-done((f32[2,4]{1,0:T(2,128)S(1)}, f32[2,4]{1,0:T(2,128)}, u32[]{:S(2)}) %copy-start.4) | copy-done | bytes 56
  8.3 0.0 copy-start.7
  8.3 0.6 %copy-done.7 = s32[1,1,16]{2,1,0:T(1,128)S(1)} copy-done((s32[1,1,16]{2,1,0:T(1,128)S(1)}, s32[1,1,16]{2,1,0:T(1,128)}, u32[]{:S(2)}) %copy-start.7) | copy-done | bytes 88
  9.0 0.0 copy-start.5
  9.0 0.7 %copy-done.5 = s32[1,1,16]{2,1,0:T(1,128)S(1)} copy-done((s32[1,1,16]{2,1,0:T(1,128)S(1)}, s32[1,1,16]{2,1,0:T(1,128)}, u32[]{:S(2)}) %copy-start.5) | copy-done | bytes 88
  9.6 0.7 %copy-done.6 = s32[1,1,16]{2,1,0:T(1,128)S(1)} copy-done((s32[1,1,16]{2,1,0:T(1,128)S(1)}, s32[1,1,16]{2,1,0:T(1,128)}, u32[]{:S(2)}) %copy-start.6) | copy-done | bytes 88
  10.3 0.7 %copy-done.3 = f32[2,4,16]{2,1,0:T(4,128)S(1)} copy-done((f32[2,4,16]{2,1,0:T(4,128)S(1)}, f32[2,4,16]{2,1,0:T(4,128)}, u32[]{:S(2)}) %copy-start.3) | copy-done | bytes 536
  11.0 0.1 copy.13
  11.1 0.0 collective-permute-done
  11.1 0.0 collective-permute-done.1
  11.1 0.6 %fusion.8 = f32[4,16,2048]{2,0,1:T(4,128)S(1)} fusion(f32[4,16,2048]{2,0,1:T(4,128)S(1)} %bitcast.114, f32[4,16,1]{2,0,1:T(4,128)S(1)} %collective-permute-done.1, f32[4,16,1]{2,0,1:T(4,128)S(1)} %collective-permute-done, f32[4,16]{0,1:T(8,128)S(1)} %copy.13), kind=kLoop, calls=%fused_computation.13 | loop fusion | flops 917504 | bytes 1049344 | tf_op jit(solution)/shard_map/add | solution.py:57
  11.7 0.1 fusion.35
  11.8 0.0 collective-permute-start.2
  11.8 4.7 %collective-permute-start.3 = (f32[4,16,1]{2,0,1:T(4,128)S(1)}, f32[4,16,1]{2,0,1:T(4,128)S(1)}, u32[]{:S(2)}, u32[]{:S(2)}) collective-permute-start(f32[4,16,1]{2,0,1:T(4,128)S(1)} %get-tuple-element.34), channel_id=1, source_target_pairs={{1,0},{2,1},{3,2},{4,3},{5,4},{6,5},{7,6},{0,7},{9,8},{10,9},{11,1... | collective-permute-start | bytes 776 | tf_op jit(solution)/shard_map/ppermute | solution.py:19
  16.5 1.9 %collective-permute-done.2 = f32[4,16,1]{2,0,1:T(4,128)S(1)} collective-permute-done((f32[4,16,1]{2,0,1:T(4,128)S(1)}, f32[4,16,1]{2,0,1:T(4,128)S(1)}, u32[]{:S(2)}, u32[]{:S(2)}) %collective-permute-start.2) | collective-permute-done | bytes 288 | tf_op jit(solution)/shard_map/ppermute | solution.py:17
  18.4 0.0 collective-permute-done.3
  18.4 0.6 %fusion.4 = f32[4,16,2048]{2,0,1:T(4,128)S(1)} fusion(f32[4,16,2048]{2,0,1:T(4,128)S(1)} %fusion.8, f32[4,16,1]{2,0,1:T(4,128)S(1)} %collective-permute-done.3, f32[4,16,1]{2,0,1:T(4,128)S(1)} %collective-permute-done.2, f32[4,16]{0,1:T(8,128)S(1)} %copy.13), kind=kLoop, calls=%fused_computation.7 | loop fusion | flops 917504 | bytes 1049344 | tf_op jit(solution)/shard_map/add | solution.py:57
  19.1 0.0 copy-done.2
  19.1 0.9 %fusion.11 = f32[4,2048,16]{1,2,0:T(8,128)S(1)} fusion(f32[4,16,2048]{2,0,1:T(4,128)S(1)} %fusion.4, f32[2,16,16]{2,1,0:T(8,128)S(1)} %copy-done.2, s32[]{:T(128)S(6)} %select_n.39), kind=kOutput, calls=%fused_computation.18 | convolution fusion | flops 25165824 | bytes 1056772 | tf_op jit(solution)/shard_map/lm,kmz->klz/dot_general | solution.py:58
  20.0 0.7 %bitcast_add_fusion = f32[4,16,2048]{2,0,1:T(4,128)S(1)} fusion(f32[4,2048,16]{1,2,0:T(8,128)S(1)} %fusion.11, f32[4,16,2048]{2,0,1:T(4,128)S(1)} %fusion.8, f32[4,16,1]{2,0,1:T(4,128)S(1)} %collective-permute-done.3, f32[4,16,1]{2,0,1:T(4,128)S(1)} %collective-permute-done.2, f32[4,16]{0,1:T(8,128)S(1)} %copy.13), kind=kLoop, calls=%fused_computation.17 | loop fusion | flops 1048576 | bytes 1573632 | tf_op jit(solution)/shard_map/add | solution.py:58
  20.7 0.1 fusion.22
  20.8 0.6 %gather_fusion = bf16[16,4,128]{2,1,0:T(4,128)(2,1)S(1)} fusion(bf16[4,16,128]{2,0,1:T(4,128)(2,1)S(1)} %copy.16, s32[1024]{0:T(1024)S(1)} %pad_clamp_fusion), kind=kCustom, calls=%fused_computation | custom fusion | bytes 32832 | tf_op jit(solution)/shard_map/gather | solution.py:62
  21.4 0.0 copy-done
  21.4 0.2 fusion.9
  21.6 0.3 fusion
  22.0 1.6 %collective-permute-start.4 = (f32[4,2048]{1,0:T(4,128)S(1)}, f32[4,2048]{1,0:T(4,128)S(1)}, u32[]{:S(2)}, u32[]{:S(2)}) collective-permute-start(f32[4,2048]{1,0:T(4,128)S(1)} %bitcast.117), channel_id=1, source_target_pairs={{0,5},{1,6},{2,7},{3,0},{4,1},{5,2},{6,3},{7,4},{8,13},{9,14},{10,... | collective-permute-start | bytes 98312 | tf_op jit(solution)/shard_map/ppermute | solution.py:29
  23.7 1.4 %collective-permute-start.5 = (f32[4,2048]{1,0:T(4,128)S(1)}, f32[4,2048]{1,0:T(4,128)S(1)}, u32[]{:S(2)}, u32[]{:S(2)}) collective-permute-start(f32[4,2048]{1,0:T(4,128)S(1)} %bitcast.115), channel_id=1, source_target_pairs={{0,6},{1,7},{2,0},{3,1},{4,2},{5,3},{6,4},{7,5},{8,14},{9,15},{10,... | collective-permute-start | bytes 98312 | tf_op jit(solution)/shard_map/ppermute | solution.py:29
  25.1 1.9 %collective-permute-start.6 = (f32[4,2048]{1,0:T(4,128)S(1)}, f32[4,2048]{1,0:T(4,128)S(1)}, u32[]{:S(2)}, u32[]{:S(2)}) collective-permute-start(f32[4,2048]{1,0:T(4,128)S(1)} %bitcast.116), channel_id=1, source_target_pairs={{0,7},{1,0},{2,1},{3,2},{4,3},{5,4},{6,5},{7,6},{8,15},{9,8},{10,9... | collective-permute-start | bytes 98312 | tf_op jit(solution)/shard_map/ppermute | solution.py:29
  27.0 0.6 %collective-permute-start.7 = (f32[4,2048]{1,0:T(4,128)S(1)}, f32[4,2048]{1,0:T(4,128)S(1)}, u32[]{:S(2)}, u32[]{:S(2)}) collective-permute-start(f32[4,2048]{1,0:T(4,128)S(1)} %bitcast.118), channel_id=1, source_target_pairs={{0,1},{1,2},{2,3},{3,4},{4,5},{5,6},{6,7},{7,0},{8,9},{9,10},{10,1... | collective-permute-start | bytes 98312 | tf_op jit(solution)/shard_map/ppermute | solution.py:29
  27.6 2.1 %collective-permute-start.8 = (f32[4,2048]{1,0:T(4,128)S(1)}, f32[4,2048]{1,0:T(4,128)S(1)}, u32[]{:S(2)}, u32[]{:S(2)}) collective-permute-start(f32[4,2048]{1,0:T(4,128)S(1)} %bitcast.119), channel_id=1, source_target_pairs={{0,2},{1,3},{2,4},{3,5},{4,6},{5,7},{6,0},{7,1},{8,10},{9,11},{10,... | collective-permute-start | bytes 98312 | tf_op jit(solution)/shard_map/ppermute | solution.py:29
  29.7 0.0 collective-permute-done.4
  29.7 1.5 %collective-permute-start.9 = (f32[4,2048]{1,0:T(4,128)S(1)}, f32[4,2048]{1,0:T(4,128)S(1)}, u32[]{:S(2)}, u32[]{:S(2)}) collective-permute-start(f32[4,2048]{1,0:T(4,128)S(1)} %bitcast.120), channel_id=1, source_target_pairs={{0,3},{1,4},{2,5},{3,6},{4,7},{5,0},{6,1},{7,2},{8,11},{9,12},{10,... | collective-permute-start | bytes 98312 | tf_op jit(solution)/shard_map/ppermute | solution.py:29
  31.2 0.0 copy-done.1
  31.3 0.0 collective-permute-done.5
  31.3 0.0 collective-permute-done.6
  31.3 2.3 %collective-permute-done.7 = f32[4,2048]{1,0:T(4,128)S(1)} collective-permute-done((f32[4,2048]{1,0:T(4,128)S(1)}, f32[4,2048]{1,0:T(4,128)S(1)}, u32[]{:S(2)}, u32[]{:S(2)}) %collective-permute-start.7) | collective-permute-done | bytes 32800 | tf_op jit(solution)/shard_map/ppermute | solution.py:29
  33.6 0.0 collective-permute-done.8
  33.6 1.8 %collective-permute-done.9 = f32[4,2048]{1,0:T(4,128)S(1)} collective-permute-done((f32[4,2048]{1,0:T(4,128)S(1)}, f32[4,2048]{1,0:T(4,128)S(1)}, u32[]{:S(2)}, u32[]{:S(2)}) %collective-permute-start.9) | collective-permute-done | bytes 32800 | tf_op jit(solution)/shard_map/ppermute | solution.py:29
  35.5 10.3 %psum.7 = f32[4,2048]{1,0:T(4,128)S(1)} all-reduce(f32[4,2048]{1,0:T(4,128)S(1)} %fusion.19), channel_id=1, replica_groups=mesh['comp'=4,'tile'=8] {'comp'}, use_global_device_ids=true, to_apply=%region_0.1 | all-reduce | flops 8192 | bytes 65536 | tf_op jit(solution)/shard_map/psum | solution.py:81
  45.8 0.1 add_dynamic-update-slice_fusion
  45.9 0.1 select_bitcast_fusion
  46.0 1.1 %copy.18 = f32[1,1,4,16,2048]{4,3,2,1,0:T(8,128)} copy(f32[1,1,4,16,2048]{4,2,3,1,0:T(4,128)S(1)} %select_bitcast_fusion) | data formatting | bytes 1048576 | tf_op jit(solution)/shard_map/broadcast_in_dim | solution.py:86
  (23 shorter events, 0.3 us)
Async XLA Ops:
  0.0 21.4 %copy-start = (bf16[1,1,16,128,128]{4,3,2,1,0:T(8,128)(2,1)S(1)}, bf16[1,1,16,128,128]{4,3,2,1,0:T(8,128)(2,1)}, u32[]{:S(2)}) copy-start(bf16[1,1,16,128,128]{4,3,2,1,0:T(8,128)(2,1)} %param.20) | copy-start | bytes 1572868
  1.5 9.5 %collective-permute-start = (f32[4,16,1]{2,0,1:T(4,128)S(1)}, f32[4,16,1]{2,0,1:T(4,128)S(1)}, u32[]{:S(2)}, u32[]{:S(2)}) collective-permute-start(f32[4,16,1]{2,0,1:T(4,128)S(1)} %get-tuple-element.35), channel_id=1, source_target_pairs={{0,1},{1,2},{2,3},{3,4},{4,5},{5,6},{6,7},{7,0},{8,9},{9,10},{10,1... | collective-permute-start | bytes 776 | tf_op jit(solution)/shard_map/ppermute | solution.py:17
  4.5 6.5 %collective-permute-start.1 = (f32[4,16,1]{2,0,1:T(4,128)S(1)}, f32[4,16,1]{2,0,1:T(4,128)S(1)}, u32[]{:S(2)}, u32[]{:S(2)}) collective-permute-start(f32[4,16,1]{2,0,1:T(4,128)S(1)} %get-tuple-element.36), channel_id=1, source_target_pairs={{1,0},{2,1},{3,2},{4,3},{5,4},{6,5},{7,6},{0,7},{9,8},{10,9},{11,1... | collective-permute-start | bytes 776 | tf_op jit(solution)/shard_map/ppermute | solution.py:19
  7.6 0.7 %copy-start.4 = (f32[2,4]{1,0:T(2,128)S(1)}, f32[2,4]{1,0:T(2,128)}, u32[]{:S(2)}) copy-start(f32[2,4]{1,0:T(2,128)} %param.16) | copy-start | bytes 100
  8.3 0.7 %copy-start.7 = (s32[1,1,16]{2,1,0:T(1,128)S(1)}, s32[1,1,16]{2,1,0:T(1,128)}, u32[]{:S(2)}) copy-start(s32[1,1,16]{2,1,0:T(1,128)} %param.17) | copy-start | bytes 196
  9.0 0.7 %copy-start.5 = (s32[1,1,16]{2,1,0:T(1,128)S(1)}, s32[1,1,16]{2,1,0:T(1,128)}, u32[]{:S(2)}) copy-start(s32[1,1,16]{2,1,0:T(1,128)} %param.18) | copy-start | bytes 196
  9.6 0.7 %copy-start.6 = (s32[1,1,16]{2,1,0:T(1,128)S(1)}, s32[1,1,16]{2,1,0:T(1,128)}, u32[]{:S(2)}) copy-start(s32[1,1,16]{2,1,0:T(1,128)} %param.19) | copy-start | bytes 196
  10.3 0.7 %copy-start.3 = (f32[2,4,16]{2,1,0:T(4,128)S(1)}, f32[2,4,16]{2,1,0:T(4,128)}, u32[]{:S(2)}) copy-start(f32[2,4,16]{2,1,0:T(4,128)} %param.14) | copy-start | bytes 1540
  11.8 6.6 %collective-permute-start.2 = (f32[4,16,1]{2,0,1:T(4,128)S(1)}, f32[4,16,1]{2,0,1:T(4,128)S(1)}, u32[]{:S(2)}, u32[]{:S(2)}) collective-permute-start(f32[4,16,1]{2,0,1:T(4,128)S(1)} %get-tuple-element.33), channel_id=1, source_target_pairs={{0,1},{1,2},{2,3},{3,4},{4,5},{5,6},{6,7},{7,0},{8,9},{9,10},{10,1... | collective-permute-start | bytes 776 | tf_op jit(solution)/shard_map/ppermute | solution.py:17
  11.8 6.6 %collective-permute-start.3 = (f32[4,16,1]{2,0,1:T(4,128)S(1)}, f32[4,16,1]{2,0,1:T(4,128)S(1)}, u32[]{:S(2)}, u32[]{:S(2)}) collective-permute-start(f32[4,16,1]{2,0,1:T(4,128)S(1)} %get-tuple-element.34), channel_id=1, source_target_pairs={{1,0},{2,1},{3,2},{4,3},{5,4},{6,5},{7,6},{0,7},{9,8},{10,9},{11,1... | collective-permute-start | bytes 776 | tf_op jit(solution)/shard_map/ppermute | solution.py:19
  16.5 2.5 %copy-start.2 = (f32[2,16,16]{2,1,0:T(8,128)S(1)}, f32[2,16,16]{2,1,0:T(8,128)}, u32[]{:S(2)}) copy-start(f32[2,16,16]{2,1,0:T(8,128)} %param.15) | copy-start | bytes 6148
  22.0 7.7 %collective-permute-start.4 = (f32[4,2048]{1,0:T(4,128)S(1)}, f32[4,2048]{1,0:T(4,128)S(1)}, u32[]{:S(2)}, u32[]{:S(2)}) collective-permute-start(f32[4,2048]{1,0:T(4,128)S(1)} %bitcast.117), channel_id=1, source_target_pairs={{0,5},{1,6},{2,7},{3,0},{4,1},{5,2},{6,3},{7,4},{8,13},{9,14},{10,... | collective-permute-start | bytes 98312 | tf_op jit(solution)/shard_map/ppermute | solution.py:29
  23.7 7.6 %collective-permute-start.5 = (f32[4,2048]{1,0:T(4,128)S(1)}, f32[4,2048]{1,0:T(4,128)S(1)}, u32[]{:S(2)}, u32[]{:S(2)}) collective-permute-start(f32[4,2048]{1,0:T(4,128)S(1)} %bitcast.115), channel_id=1, source_target_pairs={{0,6},{1,7},{2,0},{3,1},{4,2},{5,3},{6,4},{7,5},{8,14},{9,15},{10,... | collective-permute-start | bytes 98312 | tf_op jit(solution)/shard_map/ppermute | solution.py:29
  25.1 6.2 %collective-permute-start.6 = (f32[4,2048]{1,0:T(4,128)S(1)}, f32[4,2048]{1,0:T(4,128)S(1)}, u32[]{:S(2)}, u32[]{:S(2)}) collective-permute-start(f32[4,2048]{1,0:T(4,128)S(1)} %bitcast.116), channel_id=1, source_target_pairs={{0,7},{1,0},{2,1},{3,2},{4,3},{5,4},{6,5},{7,6},{8,15},{9,8},{10,9... | collective-permute-start | bytes 98312 | tf_op jit(solution)/shard_map/ppermute | solution.py:29
  27.0 6.7 %collective-permute-start.7 = (f32[4,2048]{1,0:T(4,128)S(1)}, f32[4,2048]{1,0:T(4,128)S(1)}, u32[]{:S(2)}, u32[]{:S(2)}) collective-permute-start(f32[4,2048]{1,0:T(4,128)S(1)} %bitcast.118), channel_id=1, source_target_pairs={{0,1},{1,2},{2,3},{3,4},{4,5},{5,6},{6,7},{7,0},{8,9},{9,10},{10,1... | collective-permute-start | bytes 98312 | tf_op jit(solution)/shard_map/ppermute | solution.py:29
  27.6 6.0 %collective-permute-start.8 = (f32[4,2048]{1,0:T(4,128)S(1)}, f32[4,2048]{1,0:T(4,128)S(1)}, u32[]{:S(2)}, u32[]{:S(2)}) collective-permute-start(f32[4,2048]{1,0:T(4,128)S(1)} %bitcast.119), channel_id=1, source_target_pairs={{0,2},{1,3},{2,4},{3,5},{4,6},{5,7},{6,0},{7,1},{8,10},{9,11},{10,... | collective-permute-start | bytes 98312 | tf_op jit(solution)/shard_map/ppermute | solution.py:29
  29.6 1.5 %copy-start.1 = (s32[1,2048]{1,0:T(1,128)S(1)}, s32[1,2048]{1,0:T(1,128)}, u32[]{:S(2)}) copy-start(s32[1,2048]{1,0:T(1,128)} %param.21) | copy-start | bytes 24580
  29.7 5.8 %collective-permute-start.9 = (f32[4,2048]{1,0:T(4,128)S(1)}, f32[4,2048]{1,0:T(4,128)S(1)}, u32[]{:S(2)}, u32[]{:S(2)}) collective-permute-start(f32[4,2048]{1,0:T(4,128)S(1)} %bitcast.120), channel_id=1, source_target_pairs={{0,3},{1,4},{2,5},{3,6},{4,7},{5,0},{6,1},{7,2},{8,11},{9,12},{10,... | collective-permute-start | bytes 98312 | tf_op jit(solution)/shard_map/ppermute | solution.py:29
where the time goes:
time: 47.4 us; the launch traced here: 47.1 us
  starting transfers between devices  19.9 us (42%)
  blocking collectives  10.3 us (22%)
  local copies, waits for them, and re-layouts  6.88 us (15%)
  waiting for transfers between devices  6.07 us (13%)
  other arithmetic  2.36 us (5%)
  matrix products  1.45 us (3%)
    psum x1, blocking collectives, local(): received = lax.psum(received, 'comp')  10.3 us
    ppermute x6, starting transfers between devices, passed_along(): return lax.ppermute(value, axis, pairs)  9.11 us
    ppermute x2, starting transfers between devices, extended(): lax.ppermute(head, axis, [((i + 1) % count, i) for i in range(count)])  7.81 us
    unnamed x26, local copies, waits for them, and re-layouts  4.92 us
    ppermute x6, waiting for transfers between devices, passed_along(): return lax.ppermute(value, axis, pairs)  4.18 us
    ppermute x2, starting transfers between devices, extended(): lax.ppermute(tail, axis, [(i, (i + 1) % count) for i in range(count)])  3.02 us
    ppermute x2, waiting for transfers between devices, extended(): lax.ppermute(tail, axis, [(i, (i + 1) % count) for i in range(count)])  1.88 us
    add x2, other arithmetic, local(): fields + rates * (padded[:, :, :-2] + padded[:, :, 2:] - 2.0 * fields)  1.28 us
  transfers between devices with their start and end apart: 10, of which 3 were waited for; matrix products, arithmetic and copies ran while one was open for 0% of the time, Pallas kernels for 0%

commit v1 on v0

--- a/solution.py
+++ b/solution.py
@@ -7,26 +7,23 @@
 SUB = 2
 
 
-def extended(cells, sides, width):
-    for axis, dim in sides:
-        count = lax.axis_size(axis)
-        head = lax.slice_in_dim(cells, 0, width, axis=dim)
-        tail = lax.slice_in_dim(cells, cells.shape[dim] - width, cells.shape[dim], axis=dim)
-        cells = jnp.concatenate(
-            [
-                lax.ppermute(tail, axis, [(i, (i + 1) % count) for i in range(count)]),
-                cells,
-                lax.ppermute(head, axis, [((i + 1) % count, i) for i in range(count)]),
-            ],
-            axis=dim,
-        )
-    return cells
+def moved(value, axis, steps):
+    count = lax.axis_size(axis)
+    return lax.ppermute(value, axis, [(i, (i + steps) % count) for i in range(count)])
 
 
-def passed_along(value, axis, steps):
+def swapped(value, axis, bit):
     count = lax.axis_size(axis)
-    pairs = [(source, (source + steps) % count) for source in range(count)]
-    return lax.ppermute(value, axis, pairs)
+    return lax.ppermute(value, axis, [(i, i ^ bit) for i in range(count)])
+
+
+def sideways(value, steps):
+    comps, tiles = lax.axis_size("comp"), lax.axis_size("tile")
+    pairs = []
+    for c in range(comps):
+        shift = steps if c % 2 else -steps
+        pairs += [(c * tiles + t, c * tiles + (t + shift) % tiles) for t in range(tiles)]
+    return lax.ppermute(value, ("comp", "tile"), pairs)
 
 
 def local(
@@ -49,12 +46,16 @@
     comp_index = lax.axis_index("comp")
     comp_count = lax.axis_size("comp")
     is_atmos = comp_index < comp_count - 1
+    right_core = (comp_index % 2) == 1
     group = jnp.where(is_atmos, 0, 1).astype(jnp.int32)
     rates = lax.dynamic_index_in_dim(mixing, group, 0, keepdims=False)[:, :, None]
     operator = lax.dynamic_index_in_dim(vertical, group, 0, keepdims=False)
+    from_left = moved(fields[:, :, cells - SUB :], "tile", 1)
+    from_right = moved(fields[:, :, :SUB], "tile", -1)
+    wide = jnp.concatenate([from_left, fields, from_right], axis=2)
     for sweep in range(SUB):
-        padded = extended(fields, (("tile", 2),), 1)
-        fields = fields + rates * (padded[:, :, :-2] + padded[:, :, 2:] - 2.0 * fields)
+        wide = wide[:, :, 1:-1] + rates * (wide[:, :, :-2] + wide[:, :, 2:] - 2.0 * wide[:, :, 1:-1])
+    fields = wide
     mixed = fields + jnp.einsum("lm,kmz->klz", operator, fields, precision=lax.Precision.HIGHEST)
     surface = jnp.tanh(flux_coef[0][:, None] * mixed[:, -1] + flux_coef[1][:, None] * mixed[:, -2])
     rounded = surface.astype(jnp.bfloat16)
@@ -74,11 +75,17 @@
     )
     buffers = buffers.reshape(spread, rounded.shape[0], cells)
     buffers = jnp.where(is_atmos, buffers, 0.0)
+    left = buffers[:REACH][::-1]
+    right = buffers[REACH + 1 :]
+    theirs = swapped(jnp.where(right_core, left, right), "comp", 1)
+    mine = jnp.where(right_core, right, left) + theirs
     received = buffers[REACH]
-    for offset in range(-REACH, REACH + 1):
-        if offset != 0:
-            received = received + passed_along(buffers[REACH + offset], "tile", offset)
-    received = lax.psum(received, "comp")
+    for step in range(1, REACH + 1):
+        received = received + sideways(mine[step - 1], step)
+    bit = 1
+    while bit < comp_count:
+        received = received + swapped(received, "comp", bit)
+        bit *= 2
     land = ocean_mask[0].astype(jnp.float32)
     atmosphere = mixed.at[:, -1].add(-0.5 * surface)
     ocean = mixed.at[:, 0].add(land[None, :] * received)

time: 47.4 us -> 32.8 us (0.69)
  blocking collectives: 10.3 us -> 0 us
  starting transfers between devices: 19.9 us -> 11.2 us
  waiting for transfers between devices: 6.07 us -> 9.63 us
  local copies, waits for them, and re-layouts: 6.88 us -> 7.55 us
    psum x1 -> x0, blocking collectives: 10.3 us -> none  [local(): received = lax.psum(received, 'comp')]
    ppermute x10 -> x8, starting transfers between devices: 19.9 us -> 11.2 us  [the longest x2 6.09 us: moved(): lax.ppermute(value, axis, [(i, (i + steps) % count) for i in range(count)])]
    ppermute x10 -> x8, waiting for transfers between devices: 6.07 us -> 9.63 us  [the longest x3 4.82 us: swapped(): return lax.ppermute(value, axis, [(i, i ^ bit) for i in range(count)])]
    concatenate x0 -> x1, local copies, waits for them, and re-layouts: none -> 0.71 us  [local(): wide = jnp.concatenate([from_left, fields, from_right], axis=2)]
    add x3 -> x5, other arithmetic: 1.32 us -> 1.42 us  [the longest x2 1.34 us: local(): wide[:, :, 1:-1]]
    unnamed x26 -> x20, local copies, waits for them, and re-layouts: 4.92 us -> 4.87 us
  transfers between devices with their start and end apart: 10 -> 8, of which waited for: 3 -> 6; matrix products, arithmetic and copies ran while one was open for 0% -> 0% of each run, Pallas kernels for 0% -> 0%
where the time goes in v1:
time: 32.8 us; the launch traced here: 32.5 us
  starting transfers between devices  11.2 us (34%)
  waiting for transfers between devices  9.63 us (29%)
  local copies, waits for them, and re-layouts  7.55 us (23%)
  other arithmetic  2.53 us (8%)
  matrix products  1.45 us (4%)
    ppermute x2, starting transfers between devices, moved(): lax.ppermute(value, axis, [(i, (i + steps) % count) for i in range(count)])  6.09 us
    unnamed x20, local copies, waits for them, and re-layouts  4.87 us
    ppermute x3, waiting for transfers between devices, swapped(): return lax.ppermute(value, axis, [(i, i ^ bit) for i in range(count)])  4.82 us
    ppermute x3, waiting for transfers between devices, sideways(): return lax.ppermute(value, ('comp', 'tile'), pairs)  4.81 us
    ppermute x3, starting transfers between devices, sideways(): return lax.ppermute(value, ('comp', 'tile'), pairs)  3.34 us
    ppermute x3, starting transfers between devices, swapped(): return lax.ppermute(value, axis, [(i, i ^ bit) for i in range(count)])  1.73 us
    add x2, other arithmetic, local(): wide[:, :, 1:-1]  1.34 us
    broadcast_in_dim x1, local copies, waits for them, and re-layouts, local(): return result[None, None]  1.1 us
  transfers between devices with their start and end apart: 8, of which 6 were waited for; matrix products, arithmetic and copies ran while one was open for 0% of the time, Pallas kernels for 0%

profile of v1, /device:TPU:0, one launch (start us, length us, event | category | flops | bytes accessed | tf_op | source)
XLA Modules:
  0.0 32.5 jit_solution(4103830644699598980)
XLA Ops:
  0.0 0.0 copy-start
  0.0 1.4 %copy.35 = f32[1,1,4,16,2048]{4,2,3,1,0:T(4,128)S(1)} copy(f32[1,1,4,16,2048]{4,3,2,1,0:T(8,128)} %param.13) | data formatting | bytes 1048576 | tf_op args[0]
  1.4 0.1 fusion.30
  1.5 3.0 %collective-permute-start = (f32[4,16,2]{2,0,1:T(4,128)S(1)}, f32[4,16,2]{2,0,1:T(4,128)S(1)}, u32[]{:S(2)}, u32[]{:S(2)}) collective-permute-start(f32[4,16,2]{2,0,1:T(4,128)S(1)} %get-tuple-element.34), channel_id=1, source_target_pairs={{0,1},{1,2},{2,3},{3,4},{4,5},{5,6},{6,7},{7,0},{8,9},{9,10},{10,1... | collective-permute-start | bytes 1544 | tf_op jit(solution)/shard_map/ppermute | solution.py:12
  4.5 3.1 %collective-permute-start.1 = (f32[4,16,2]{2,0,1:T(4,128)S(1)}, f32[4,16,2]{2,0,1:T(4,128)S(1)}, u32[]{:S(2)}, u32[]{:S(2)}) collective-permute-start(f32[4,16,2]{2,0,1:T(4,128)S(1)} %get-tuple-element.33), channel_id=1, source_target_pairs={{0,7},{1,0},{2,1},{3,2},{4,3},{5,4},{6,5},{7,6},{8,15},{9,8},{10,9... | collective-permute-start | bytes 1544 | tf_op jit(solution)/shard_map/ppermute | solution.py:12
  7.6 0.0 copy-start.4
  7.6 0.7 %copy-done.4 = f32[2,4]{1,0:T(2,128)S(1)} copy-done((f32[2,4]{1,0:T(2,128)S(1)}, f32[2,4]{1,0:T(2,128)}, u32[]{:S(2)}) %copy-start.4) | copy-done | bytes 56
  8.3 0.0 copy-start.7
  8.3 0.6 %copy-done.7 = s32[1,1,16]{2,1,0:T(1,128)S(1)} copy-done((s32[1,1,16]{2,1,0:T(1,128)S(1)}, s32[1,1,16]{2,1,0:T(1,128)}, u32[]{:S(2)}) %copy-start.7) | copy-done | bytes 88
  9.0 0.0 copy-start.5
  9.0 0.6 %copy-done.5 = s32[1,1,16]{2,1,0:T(1,128)S(1)} copy-done((s32[1,1,16]{2,1,0:T(1,128)S(1)}, s32[1,1,16]{2,1,0:T(1,128)}, u32[]{:S(2)}) %copy-start.5) | copy-done | bytes 88
  9.6 0.0 copy-start.6
  9.6 0.7 %copy-done.6 = s32[1,1,16]{2,1,0:T(1,128)S(1)} copy-done((s32[1,1,16]{2,1,0:T(1,128)S(1)}, s32[1,1,16]{2,1,0:T(1,128)}, u32[]{:S(2)}) %copy-start.6) | copy-done | bytes 88
  10.3 0.0 copy-start.3
  10.3 0.7 %copy-done.3 = f32[2,4,16]{2,1,0:T(4,128)S(1)} copy-done((f32[2,4,16]{2,1,0:T(4,128)S(1)}, f32[2,4,16]{2,1,0:T(4,128)}, u32[]{:S(2)}) %copy-start.3) | copy-done | bytes 536
  11.0 0.1 copy.13
  11.1 0.0 collective-permute-done
  11.1 0.0 collective-permute-done.1
  11.1 0.7 %concatenate.13 = f32[4,16,2052]{2,0,1:T(4,128)S(1)} concatenate(f32[4,16,2]{2,0,1:T(4,128)S(1)} %collective-permute-done, f32[4,16,2048]{2,0,1:T(4,128)S(1)} %bitcast.82, f32[4,16,2]{2,0,1:T(4,128)S(1)} %collective-permute-done.1), dimensions={2} | concatenate | bytes 1050624 | tf_op jit(solution)/shard_map/concatenate | solution.py:55
  11.8 0.7 %fusion.3 = f32[4,16,2050]{2,0,1:T(4,128)S(1)} fusion(f32[4,16,2048]{2,0,1:T(4,128)S(1)} %bitcast.83, f32[4,16,2]{2,0,1:T(4,128)S(1)} %collective-permute-done, f32[4,16,2]{2,0,1:T(4,128)S(1)} %collective-permute-done.1, f32[4,16,2052]{2,0,1:T(4,128)S(1)} %concatenate.13, f32[4,16]{0,1:T(8,128)S(1)} %copy.13), kind=kLoop, calls=%fused_computation.6 | loop fusion | flops 918400 | bytes 1575168 | tf_op jit(solution)/shard_map/add | solution.py:57
  12.5 0.0 copy-start.2
  12.5 0.6 %fusion.6 = f32[4,16,2048]{2,0,1:T(4,128)S(1)} fusion(f32[4,16,2050]{2,0,1:T(4,128)S(1)} %fusion.3, f32[4,16]{0,1:T(8,128)S(1)} %copy.13), kind=kLoop, calls=%fused_computation.10 | loop fusion | flops 655360 | bytes 2097408 | tf_op jit(solution)/shard_map/add | solution.py:57
  13.2 0.1 copy-done.2
  13.2 0.9 %fusion.9 = f32[4,2048,16]{1,2,0:T(8,128)S(1)} fusion(f32[4,16,2048]{2,0,1:T(4,128)S(1)} %fusion.6, f32[2,16,16]{2,1,0:T(8,128)S(1)} %copy-done.2, s32[]{:T(128)S(6)} %select_n.58), kind=kOutput, calls=%fused_computation.14 | convolution fusion | flops 25165824 | bytes 1056772 | tf_op jit(solution)/shard_map/lm,kmz->klz/dot_general | solution.py:59
  14.1 0.7 %bitcast_add_fusion = f32[4,16,2048]{2,0,1:T(4,128)S(1)} fusion(f32[4,2048,16]{1,2,0:T(8,128)S(1)} %fusion.9, f32[4,16,2050]{2,0,1:T(4,128)S(1)} %fusion.3, f32[4,16]{0,1:T(8,128)S(1)} %copy.13), kind=kLoop, calls=%fused_computation.13 | loop fusion | flops 786432 | bytes 2621696 | tf_op jit(solution)/shard_map/add | solution.py:59
  14.8 0.1 fusion.17
  14.9 0.6 %gather_fusion = bf16[16,4,128]{2,1,0:T(4,128)(2,1)S(1)} fusion(bf16[4,16,128]{2,0,1:T(4,128)(2,1)S(1)} %copy.17, s32[1024]{0:T(1024)S(1)} %pad_clamp_fusion), kind=kCustom, calls=%fused_computation | custom fusion | bytes 32832 | tf_op jit(solution)/shard_map/gather | solution.py:63
  15.5 0.0 copy-done
  15.5 0.2 fusion.7
  15.8 0.3 %fusion = f32[7,4,16,128]{3,2,1,0:T(8,128)S(1)} fusion(pred[]{:T(512)S(6)} %lt.23, f32[16,4,128]{2,1,0:T(4,128)S(1)} %fusion.7, f32[16,7]{0,1:T(8,128)S(1)} %fusion.27, f32[16,16]{0,1:T(8,128)S(1)} %fusion.26), kind=kOutput, calls=%fused_computation.2 | convolution fusion | flops 11069184 | bytes 263617 | tf_op jit(solution)/shard_map/nd,no,nkj->dkoj/dot_general | solution.py:73
  16.2 0.1 collective-permute-start.2
  16.3 1.3 %collective-permute-done.2 = f32[3,4,2048]{2,1,0:T(4,128)S(1)} collective-permute-done((f32[3,4,2048]{2,1,0:T(4,128)S(1)}, f32[3,4,2048]{2,1,0:T(4,128)S(1)}, u32[]{:S(2)}, u32[]{:S(2)}) %collective-permute-start.2) | collective-permute-done | bytes 98336 | tf_op jit(solution)/shard_map/ppermute | solution.py:17
  17.7 3.2 %collective-permute-start.3 = (f32[4,2048]{1,0:T(4,128)S(1)}, f32[4,2048]{1,0:T(4,128)S(1)}, u32[]{:S(2)}, u32[]{:S(2)}) collective-permute-start(f32[4,2048]{1,0:T(4,128)S(1)} %get-tuple-element.37), channel_id=1, source_target_pairs={{0,7},{1,0},{2,1},{3,2},{4,3},{5,4},{6,5},{7,6},{8,9},{9,10},{10,1... | collective-permute-start | bytes 98312 | tf_op jit(solution)/shard_map/ppermute | solution.py:26
  20.9 0.1 collective-permute-start.4
  21.0 0.0 collective-permute-start.5
  21.0 1.5 %collective-permute-done.3 = f32[4,2048]{1,0:T(4,128)S(1)} collective-permute-done((f32[4,2048]{1,0:T(4,128)S(1)}, f32[4,2048]{1,0:T(4,128)S(1)}, u32[]{:S(2)}, u32[]{:S(2)}) %collective-permute-start.3) | collective-permute-done | bytes 32800 | tf_op jit(solution)/shard_map/ppermute | solution.py:26
  22.5 2.3 %collective-permute-done.4 = f32[4,2048]{1,0:T(4,128)S(1)} collective-permute-done((f32[4,2048]{1,0:T(4,128)S(1)}, f32[4,2048]{1,0:T(4,128)S(1)}, u32[]{:S(2)}, u32[]{:S(2)}) %collective-permute-start.4) | collective-permute-done | bytes 32800 | tf_op jit(solution)/shard_map/ppermute | solution.py:26
  24.8 1.0 %collective-permute-done.5 = f32[4,2048]{1,0:T(4,128)S(1)} collective-permute-done((f32[4,2048]{1,0:T(4,128)S(1)}, f32[4,2048]{1,0:T(4,128)S(1)}, u32[]{:S(2)}, u32[]{:S(2)}) %collective-permute-start.5) | collective-permute-done | bytes 32800 | tf_op jit(solution)/shard_map/ppermute | solution.py:26
  25.9 0.0 copy-start.1
  25.9 0.1 collective-permute-start.6
  25.9 1.2 %collective-permute-done.6 = f32[4,2048]{1,0:T(4,128)S(1)} collective-permute-done((f32[4,2048]{1,0:T(4,128)S(1)}, f32[4,2048]{1,0:T(4,128)S(1)}, u32[]{:S(2)}, u32[]{:S(2)}) %collective-permute-start.6) | collective-permute-done | bytes 32800 | tf_op jit(solution)/shard_map/ppermute | solution.py:17
  27.2 1.6 %collective-permute-start.7 = (f32[4,2048]{1,0:T(4,128)S(1)}, f32[4,2048]{1,0:T(4,128)S(1)}, u32[]{:S(2)}, u32[]{:S(2)}) collective-permute-start(f32[4,2048]{1,0:T(4,128)S(1)} %add.86), channel_id=1, source_target_pairs={{0,16},{8,24},{16,0},{24,8},{1,17},{9,25},{17,1},{25,9},{2,18},{10... | collective-permute-start | bytes 98312 | tf_op jit(solution)/shard_map/ppermute | solution.py:17
  28.7 0.0 copy-done.1
  28.8 2.3 %collective-permute-done.7 = f32[4,2048]{1,0:T(4,128)S(1)} collective-permute-done((f32[4,2048]{1,0:T(4,128)S(1)}, f32[4,2048]{1,0:T(4,128)S(1)}, u32[]{:S(2)}, u32[]{:S(2)}) %collective-permute-start.7) | collective-permute-done | bytes 32800 | tf_op jit(solution)/shard_map/ppermute | solution.py:17
  31.2 0.1 add_dynamic-update-slice_fusion
  31.3 0.1 select_bitcast_fusion
  31.4 1.1 %copy.19 = f32[1,1,4,16,2048]{4,3,2,1,0:T(8,128)} copy(f32[1,1,4,16,2048]{4,2,3,1,0:T(4,128)S(1)} %select_bitcast_fusion) | data formatting | bytes 1048576 | tf_op jit(solution)/shard_map/broadcast_in_dim | solution.py:93
  (20 shorter events, 0.3 us)
Async XLA Ops:
  0.0 15.5 %copy-start = (bf16[1,1,16,128,128]{4,3,2,1,0:T(8,128)(2,1)S(1)}, bf16[1,1,16,128,128]{4,3,2,1,0:T(8,128)(2,1)}, u32[]{:S(2)}) copy-start(bf16[1,1,16,128,128]{4,3,2,1,0:T(8,128)(2,1)} %param.20) | copy-start | bytes 1572868
  1.5 9.5 %collective-permute-start = (f32[4,16,2]{2,0,1:T(4,128)S(1)}, f32[4,16,2]{2,0,1:T(4,128)S(1)}, u32[]{:S(2)}, u32[]{:S(2)}) collective-permute-start(f32[4,16,2]{2,0,1:T(4,128)S(1)} %get-tuple-element.34), channel_id=1, source_target_pairs={{0,1},{1,2},{2,3},{3,4},{4,5},{5,6},{6,7},{7,0},{8,9},{9,10},{10,1... | collective-permute-start | bytes 1544 | tf_op jit(solution)/shard_map/ppermute | solution.py:12
  4.5 6.6 %collective-permute-start.1 = (f32[4,16,2]{2,0,1:T(4,128)S(1)}, f32[4,16,2]{2,0,1:T(4,128)S(1)}, u32[]{:S(2)}, u32[]{:S(2)}) collective-permute-start(f32[4,16,2]{2,0,1:T(4,128)S(1)} %get-tuple-element.33), channel_id=1, source_target_pairs={{0,7},{1,0},{2,1},{3,2},{4,3},{5,4},{6,5},{7,6},{8,15},{9,8},{10,9... | collective-permute-start | bytes 1544 | tf_op jit(solution)/shard_map/ppermute | solution.py:12
  7.6 0.7 %copy-start.4 = (f32[2,4]{1,0:T(2,128)S(1)}, f32[2,4]{1,0:T(2,128)}, u32[]{:S(2)}) copy-start(f32[2,4]{1,0:T(2,128)} %param.16) | copy-start | bytes 100
  8.3 0.7 %copy-start.7 = (s32[1,1,16]{2,1,0:T(1,128)S(1)}, s32[1,1,16]{2,1,0:T(1,128)}, u32[]{:S(2)}) copy-start(s32[1,1,16]{2,1,0:T(1,128)} %param.17) | copy-start | bytes 196
  9.0 0.7 %copy-start.5 = (s32[1,1,16]{2,1,0:T(1,128)S(1)}, s32[1,1,16]{2,1,0:T(1,128)}, u32[]{:S(2)}) copy-start(s32[1,1,16]{2,1,0:T(1,128)} %param.18) | copy-start | bytes 196
  9.6 0.7 %copy-start.6 = (s32[1,1,16]{2,1,0:T(1,128)S(1)}, s32[1,1,16]{2,1,0:T(1,128)}, u32[]{:S(2)}) copy-start(s32[1,1,16]{2,1,0:T(1,128)} %param.19) | copy-start | bytes 196
  10.3 0.7 %copy-start.3 = (f32[2,4,16]{2,1,0:T(4,128)S(1)}, f32[2,4,16]{2,1,0:T(4,128)}, u32[]{:S(2)}) copy-start(f32[2,4,16]{2,1,0:T(4,128)} %param.14) | copy-start | bytes 1540
  12.5 0.7 %copy-start.2 = (f32[2,16,16]{2,1,0:T(8,128)S(1)}, f32[2,16,16]{2,1,0:T(8,128)}, u32[]{:S(2)}) copy-start(f32[2,16,16]{2,1,0:T(8,128)} %param.15) | copy-start | bytes 6148
  16.2 1.4 %collective-permute-start.2 = (f32[3,4,2048]{2,1,0:T(4,128)S(1)}, f32[3,4,2048]{2,1,0:T(4,128)S(1)}, u32[]{:S(2)}, u32[]{:S(2)}) collective-permute-start(f32[3,4,2048]{2,1,0:T(4,128)S(1)} %reverse_select_fusion), channel_id=1, source_target_pairs={{0,8},{8,0},{16,24},{24,16},{1,9},{9,1},{17,25},{25,17},{2,10},{10... | collective-permute-start | bytes 294920 | tf_op jit(solution)/shard_map/ppermute | solution.py:17
  17.7 4.8 %collective-permute-start.3 = (f32[4,2048]{1,0:T(4,128)S(1)}, f32[4,2048]{1,0:T(4,128)S(1)}, u32[]{:S(2)}, u32[]{:S(2)}) collective-permute-start(f32[4,2048]{1,0:T(4,128)S(1)} %get-tuple-element.37), channel_id=1, source_target_pairs={{0,7},{1,0},{2,1},{3,2},{4,3},{5,4},{6,5},{7,6},{8,9},{9,10},{10,1... | collective-permute-start | bytes 98312 | tf_op jit(solution)/shard_map/ppermute | solution.py:26
  20.9 3.9 %collective-permute-start.4 = (f32[4,2048]{1,0:T(4,128)S(1)}, f32[4,2048]{1,0:T(4,128)S(1)}, u32[]{:S(2)}, u32[]{:S(2)}) collective-permute-start(f32[4,2048]{1,0:T(4,128)S(1)} %get-tuple-element.39), channel_id=1, source_target_pairs={{0,6},{1,7},{2,0},{3,1},{4,2},{5,3},{6,4},{7,5},{8,10},{9,11},{10,... | collective-permute-start | bytes 98312 | tf_op jit(solution)/shard_map/ppermute | solution.py:26
  21.0 4.8 %collective-permute-start.5 = (f32[4,2048]{1,0:T(4,128)S(1)}, f32[4,2048]{1,0:T(4,128)S(1)}, u32[]{:S(2)}, u32[]{:S(2)}) collective-permute-start(f32[4,2048]{1,0:T(4,128)S(1)} %get-tuple-element.38), channel_id=1, source_target_pairs={{0,5},{1,6},{2,7},{3,0},{4,1},{5,2},{6,3},{7,4},{8,11},{9,12},{10,... | collective-permute-start | bytes 98312 | tf_op jit(solution)/shard_map/ppermute | solution.py:26
  25.9 2.9 %copy-start.1 = (s32[1,2048]{1,0:T(1,128)S(1)}, s32[1,2048]{1,0:T(1,128)}, u32[]{:S(2)}) copy-start(s32[1,2048]{1,0:T(1,128)} %param.21) | copy-start | bytes 24580
  25.9 1.3 %collective-permute-start.6 = (f32[4,2048]{1,0:T(4,128)S(1)}, f32[4,2048]{1,0:T(4,128)S(1)}, u32[]{:S(2)}, u32[]{:S(2)}) collective-permute-start(f32[4,2048]{1,0:T(4,128)S(1)} %fusion.14), channel_id=1, source_target_pairs={{0,8},{8,0},{16,24},{24,16},{1,9},{9,1},{17,25},{25,17},{2,10},{10... | collective-permute-start | bytes 98312 | tf_op jit(solution)/shard_map/ppermute | solution.py:17
  27.2 4.0 %collective-permute-start.7 = (f32[4,2048]{1,0:T(4,128)S(1)}, f32[4,2048]{1,0:T(4,128)S(1)}, u32[]{:S(2)}, u32[]{:S(2)}) collective-permute-start(f32[4,2048]{1,0:T(4,128)S(1)} %add.86), channel_id=1, source_target_pairs={{0,16},{8,24},{16,0},{24,8},{1,17},{9,25},{17,1},{25,9},{2,18},{10... | collective-permute-start | bytes 98312 | tf_op jit(solution)/shard_map/ppermute | solution.py:17

commit v2 on v1

v2 whole, which is shorter than its diff:
```python
import functools

import jax
import jax.numpy as jnp
from jax import lax
from jax.experimental import pallas as pl
from jax.experimental.pallas import tpu as pltpu
from jax.sharding import PartitionSpec as P

REACH = 3
SUB = 2
LANES = 128
ROWS = 8
MID = LANES // 2
EDGES = 2 * SUB
F32 = jnp.float32
BF16 = jnp.bfloat16
VMEM = pl.BlockSpec(memory_space=pltpu.VMEM)
ANY = pl.BlockSpec(memory_space=pl.ANY)


def moved(value, axis, steps):
    count = lax.axis_size(axis)
    return lax.ppermute(value, axis, [(i, (i + steps) % count) for i in range(count)])


def swapped(value, axis, bit):
    count = lax.axis_size(axis)
    return lax.ppermute(value, axis, [(i, i ^ bit) for i in range(count)])


def sideways(value, steps):
    comps, tiles = lax.axis_size("comp"), lax.axis_size("tile")
    pairs = []
    for c in range(comps):
        shift = steps if c % 2 else -steps
        pairs += [(c * tiles + t, c * tiles + (t + shift) % tiles) for t in range(tiles)]
    return lax.ppermute(value, ("comp", "tile"), pairs)


def lanes_of(shape):
    return lax.broadcasted_iota(jnp.int32, shape, len(shape) - 1)


def turned(value, steps):
    width = value.shape[-1]
    steps = steps % width
    return value if steps == 0 else pltpu.roll(value, steps, axis=value.ndim - 1)


def atmosphere(comps):
    return lax.axis_index("comp") < comps - 1


def split(value):
    high = value.astype(BF16)
    return high, (value - high.astype(F32)).astype(BF16)


def product(vh, vl, field):
    high, low = split(field)
    dot = functools.partial(jnp.dot, preferred_element_type=F32)
    return dot(vh, high) + dot(vl, high) + dot(vh, low)


def stencil(coef, x):
    near = turned(x, 1) + turned(x, -1)
    far = turned(x, 2) + turned(x, -2)
    return coef[0] * x + coef[1] * near + coef[2] * far


def edges_kernel(comps, state, mixing, vertical, own, to_right, to_left, mix, ver, head, tail, sems):
    group = jnp.where(atmosphere(comps), 0, 1)
    cells = state.shape[-1]
    first = pltpu.make_async_copy(state.at[0, 0, :, :, pl.ds(0, LANES)], head, sems.at[0])
    last = pltpu.make_async_copy(state.at[0, 0, :, :, pl.ds(cells - LANES, LANES)], tail, sems.at[1])
    others = [
        pltpu.make_async_copy(mixing.at[group], mix, sems.at[2]),
        pltpu.make_async_copy(vertical.at[group], ver, sems.at[3]),
    ]
    for copy in [first, last] + others:
        copy.start()
    first.wait()
    last.wait()
    lane = lanes_of((ROWS, LANES))
    right = jnp.zeros((ROWS, LANES), F32)
    left = jnp.zeros((ROWS, LANES), F32)
    number = 0
    for k in range(head.shape[0]):
        for h in range(0, head.shape[1], ROWS):
            a, b = head[k, h : h + ROWS, :], tail[k, h : h + ROWS, :]
            at = SUB * number
            here = (lane >= at) & (lane < at + SUB)
            left = jnp.where(here, turned(a, at), left)
            right = jnp.where(here, turned(b, at + SUB), right)
            own[k, h : h + ROWS, :] = jnp.where(lane < MID, turned(a, SUB), turned(b, MID + 2 * SUB))
            number += 1
    to_right[...] = right
    to_left[...] = left
    for copy in others:
        copy.wait()


def interior_kernel(
    comps,
    state,
    mix,
    ver,
    weights,
    flux,
    atm,
    ocean,
    offset,
    low,
    high,
    buf,
    wide,
    coef,
    parts,
    flux_out,
    flux_s,
    atm_s,
    ocean_s,
    offset_s,
    press,
    round_ref,
    rim,
    sems,
):
    fields, levels, cells = state.shape
    blocks = cells // LANES
    copies = [
        pltpu.make_async_copy(src, dst, sems.at[i])
        for i, (src, dst) in enumerate(
            ((flux, flux_s), (atm.at[0, 0], atm_s), (ocean.at[0, 0], ocean_s), (offset.at[0, 0], offset_s))
        )
    ]
    for copy in copies:
        copy.start()
    is_atmos = atmosphere(comps)
    right_core = lax.axis_index("comp") % 2
    buf[...] = jnp.zeros_like(buf)
    wide[...] = jnp.zeros_like(wide)
    vh, vl = split(ver[...])
    parts[0] = vh
    parts[1] = vl
    square = (levels, levels)
    eye = lax.broadcasted_iota(jnp.int32, square, 0) == lanes_of(square)
    copies[0].wait()
    for k in range(fields):
        rate = jnp.sum(
            jnp.where(eye, jnp.broadcast_to(mix[k : k + 1, :], square), 0.0), axis=1, keepdims=True
        )
        far = rate * rate
        near = 2.0 * rate - 4.0 * far
        mid = 1.0 - 4.0 * rate + 6.0 * far
        for i, c in enumerate((mid, near, far)):
            coef[i, k] = jnp.broadcast_to(c, (levels, LANES))
        field = stencil((mid, near, far), state[k])
        mixed = field + product(vh, vl, field)
        low[k] = mixed[:ROWS]
        high[k] = mixed[ROWS:]
        press[k : k + 1, :] = (
            flux_s[0, k] * mixed[levels - 1 : levels, :] + flux_s[1, k] * mixed[levels - 2 : levels - 1, :]
        )
        for i in range(2):
            flux_out[i, k : k + 1, :] = jnp.full((1, LANES), flux_s[i, k], F32)
    surface = jnp.tanh(press[...])
    press[...] = jnp.where(is_atmos, surface, 0.0)
    last = high.shape[1] - 1
    for k in range(fields):
        high[k, last : last + 1, :] = high[k, last : last + 1, :] - 0.5 * press[k : k + 1, :]
    lane = lanes_of((fields, LANES))
    for b in range(blocks):
        value = press[:, b * LANES : (b + 1) * LANES].astype(BF16).astype(F32)
        if b == 0:
            value = jnp.where(lane < SUB, 0.0, value)
        if b == blocks - 1:
            value = jnp.where(lane >= LANES - SUB, 0.0, value)
        round_ref[b] = jnp.zeros(round_ref.shape[1:], F32)
        round_ref[b, :fields, :] = value
    for copy in copies[1:]:
        copy.wait()
    side = lax.broadcasted_iota(jnp.int32, (EDGES, LANES), 0) < SUB
    for n in range(weights.shape[0]):
        block = jnp.clip(atm_s[n], 0, blocks - 1)
        place = jnp.clip(ocean_s[n], 0, blocks - 1)
        distance = jnp.clip(offset_s[n], 0, 2 * REACH) - REACH
        ahead = jnp.where(distance > 0, 1, 0)
        slot = jnp.abs(distance) - 1 + jnp.where(ahead == right_core, 0, REACH)
        slot = jnp.where(distance == 0, 2 * REACH, slot)
        term = jnp.dot(round_ref[block].astype(BF16), weights[n], preferred_element_type=F32)
        buf[slot, place] = buf[slot, place] + term[:fields]
        rim[:SUB, :] = weights[n, : 2 * ROWS, :].astype(F32)[:SUB]
        rim[SUB:, :] = weights[n, LANES - 2 * ROWS :, :].astype(F32)[2 * ROWS - SUB :]
        lead = jnp.where(block == 0, 1.0, 0.0)
        trail = jnp.where(block == blocks - 1, 1.0, 0.0)
        wide[slot, place] = wide[slot, place] + jnp.where(side, lead, trail) * rim[...]


def rim_kernel(
    comps, from_left, from_right, own, coef, parts, flux, buf, wide, mine, theirs, here, edge, press
):
    fields, levels, _ = own.shape
    is_atmos = atmosphere(comps)
    lane = lanes_of((ROWS, LANES))
    number = 0
    for k in range(fields):
        for h in range(0, levels, ROWS):
            at = SUB * number
            x = own[k, h : h + ROWS, :]
            x = jnp.where(lane < SUB, turned(from_left[...], -at), x)
            beyond = (lane >= MID + 2 * SUB) & (lane < MID + 3 * SUB)
            x = jnp.where(beyond, turned(from_right[...], MID + 2 * SUB - at), x)
            c = [coef[i, k, h : h + ROWS, :] for i in range(3)]
            edge[k, h : h + ROWS, :] = stencil(c, x)
            number += 1
    for k in range(fields):
        field = edge[k]
        mixed = field + product(parts[0], parts[1], field)
        edge[k] = mixed
        press[k : k + 1, :] = (
            flux[0, k : k + 1, :] * mixed[levels - 1 : levels, :]
            + flux[1, k : k + 1, :] * mixed[levels - 2 : levels - 1, :]
        )
    surface = jnp.where(is_atmos, jnp.tanh(press[...]), 0.0)
    press[...] = surface
    for k in range(fields):
        edge[k, levels - 1 : levels, :] = edge[k, levels - 1 : levels, :] - 0.5 * press[k : k + 1, :]
    value = surface.astype(BF16).astype(F32)
    spots = [SUB + i for i in range(SUB)] + [MID + SUB + i for i in range(SUB)]
    column = [jnp.broadcast_to(value[:, s : s + 1], (fields, LANES)) for s in spots]
    for slot in range(buf.shape[0]):
        for place in range(buf.shape[1]):
            total = buf[slot, place]
            for e in range(EDGES):
                total = total + column[e] * wide[slot, place, e : e + 1, :]
            if slot < REACH:
                mine[slot, place] = total
            elif slot < 2 * REACH:
                theirs[slot - REACH, place] = total
            else:
                here[place] = total


def finish_kernel(low_in, high_in, edge, low, high, out, sems):
    fields, _, cells = low.shape
    lane = lanes_of((ROWS, LANES))
    copies = []
    for k in range(fields):
        for half, start in ((low, 0), (high, ROWS)):
            source = low_in if start == 0 else high_in
            value = edge[k, start : start + ROWS, :]
            half[k, :, :LANES] = jnp.where(lane < SUB, turned(value, -SUB), source[k, :, :LANES])
            half[k, :, cells - LANES :] = jnp.where(
                lane >= LANES - SUB, turned(value, MID - 2 * SUB), source[k, :, cells - LANES :]
            )
        copies.append(
            pltpu.make_async_copy(high.at[k], out.at[0, 0, k, pl.ds(ROWS, high.shape[1]), :], sems.at[k])
        )
        copies[-1].start()
    for copy in copies:
        copy.wait()


def ocean_kernel(comps, out_in, low_in, received, mask, out, low, sems):
    fields, rows, cells = low.shape
    is_ocean = jnp.logical_not(atmosphere(comps))
    copies = []
    for k in range(fields):
        for b in range(cells // LANES):
            at = slice(b * LANES, (b + 1) * LANES)
            land = mask[:, at].astype(F32)
            gain = jnp.where(is_ocean, land * received[b, k : k + 1, :], 0.0)
            low[k, 0:1, at] = low_in[k, 0:1, at] + gain
        copies.append(pltpu.make_async_copy(low.at[k], out.at[0, 0, k, pl.ds(0, rows), :], sems.at[k]))
        copies[-1].start()
    for copy in copies:
        copy.wait()


def call(body, out_shape, in_specs, out_specs, scratch, flops, aliases=None, name=None):
    return pl.pallas_call(
        body,
        out_shape=out_shape,
        in_specs=in_specs,
        out_specs=out_specs,
        scratch_shapes=scratch,
        input_output_aliases=aliases or {},
        compiler_params=pltpu.CompilerParams(vmem_limit_bytes=16 << 20),
        cost_estimate=pl.CostEstimate(flops=flops, bytes_accessed=flops // 8, transcendentals=0),
        name=name,
    )


def local(
    column_state,
    mixing,
    vertical,
    flux_coef,
    atm_block,
    ocean_block,
    tile_offset,
    remap_weights,
    ocean_mask,
):
    _, _, fields, levels, cells = column_state.shape
    margins, across, ocean_cells = remap_weights.shape[2:]
    blocks = cells // LANES
    spread = 2 * REACH + 1
    comps = lax.axis_size("comp")
    groups = fields * levels // ROWS
    assert across == LANES and ocean_cells == LANES and levels == 2 * ROWS
    assert groups * SUB <= LANES and cells % LANES == 0

    def f32(*shape):
        return jax.ShapeDtypeStruct(shape, F32)

    own, to_right, to_left, mix, ver = call(
        functools.partial(edges_kernel, comps),
        (f32(fields, levels, LANES), f32(ROWS, LANES), f32(ROWS, LANES), f32(fields, levels), f32(levels, levels)),
        [ANY] * 3,
        [VMEM] * 5,
        [pltpu.VMEM((fields, levels, LANES), F32)] * 2 + [pltpu.SemaphoreType.DMA((4,))],
        10**5,
        name="edges",
    )(column_state, mixing, vertical)
    from_left = moved(to_right, "tile", 1)
    from_right = moved(to_left, "tile", -1)
    low, high, buf, wide, coef, parts, flux = call(
        functools.partial(interior_kernel, comps),
        (
            f32(fields, ROWS, cells),
            f32(fields, levels - ROWS, cells),
            f32(spread, blocks, fields, LANES),
            f32(spread, blocks, EDGES, LANES),
            f32(3, fields, levels, LANES),
            jax.ShapeDtypeStruct((2, levels, levels), BF16),
            f32(2, fields, LANES),
        ),
        [VMEM] * 4 + [ANY] * 4,
        [VMEM] * 7,
        [
            pltpu.SMEM(flux_coef.shape, F32),
            pltpu.SMEM((margins,), jnp.int32),
            pltpu.SMEM((margins,), jnp.int32),
            pltpu.SMEM((margins,), jnp.int32),
            pltpu.VMEM((fields, cells), F32),
            pltpu.VMEM((blocks, ROWS, LANES), F32),
            pltpu.VMEM((EDGES, LANES), F32),
            pltpu.SemaphoreType.DMA((4,)),
        ],
        10**7,
        name="interior",
    )(column_state[0, 0], mix, ver, remap_weights[0, 0], flux_coef, atm_block, ocean_block, tile_offset)
    mine, theirs, received, edge = call(
        functools.partial(rim_kernel, comps),
        (
            f32(REACH, blocks, fields, LANES),
            f32(REACH, blocks, fields, LANES),
            f32(blocks, fields, LANES),
            f32(fields, levels, LANES),
        ),
        [VMEM] * 8,
        [VMEM] * 4,
        [pltpu.VMEM((fields, LANES), F32)],
        10**6,
        name="rim",
    )(from_left, from_right, own, coef, parts, flux, buf, wide)
    mine = mine + swapped(theirs, "comp", 1)
    for step in range(1, REACH + 1):
        received = received + sideways(mine[step - 1], step)
    low, high, out = call(
        finish_kernel,
        (
            f32(fields, ROWS, cells),
            f32(fields, levels - ROWS, cells),
            jax.ShapeDtypeStruct(column_state.shape, F32),
        ),
        [VMEM] * 3,
        [VMEM, VMEM, ANY],
        [pltpu.SemaphoreType.DMA((fields,))],
        10**7,
        aliases={0: 0, 1: 1},
        name="finish",
    )(low, high, edge)
    bit = 1
    while bit < comps:
        received = received + swapped(received, "comp", bit)
        bit *= 2
    out, _ = call(
        functools.partial(ocean_kernel, comps),
        (jax.ShapeDtypeStruct(column_state.shape, F32), f32(fields, ROWS, cells)),
        [ANY, VMEM, VMEM, VMEM],
        [ANY, VMEM],
        [pltpu.SemaphoreType.DMA((fields,))],
        10**6,
        aliases={0: 0, 1: 1},
        name="ocean",
    )(out, low, received, ocean_mask)
    return out


def solution(mesh):
    placed = (
        P("comp", "tile", None, None, None),
        P(),
        P(),
        P(),
        P("comp", "tile", None),
        P("comp", "tile", None),
        P("comp", "tile", None),
        P("comp", "tile", None, None, None),
        P("tile", None),
    )
    return jax.shard_map(
        local,
        mesh=mesh,
        in_specs=placed,
        out_specs=P("comp", "tile", None, None, None),
        check_vma=False,
    )
```

time: 32.8 us -> 29 us (0.88)
  Pallas kernels: 0 us -> 4.17 us
  local copies, waits for them, and re-layouts: 7.55 us -> 3.84 us
  other arithmetic: 2.53 us -> 0.06 us
  matrix products: 1.45 us -> 0 us
  waiting for transfers between devices: 9.63 us -> 8.64 us
  starting transfers between devices: 11.2 us -> 11.8 us
    pallas_call x0 -> x5, Pallas kernels: none -> 4.17 us  [the longest x1 1.9 us: local(): call(functools.partial(interior_kernel, comps), (f32(fields, ROWS, cells)...]
    add x4 -> x1, other arithmetic: 2.09 us -> 0.03 us  [local(): mine = mine + swapped(theirs, 'comp', 1)]
    dot_general x3 -> x0, matrix products: 1.45 us -> none  [the longest x1 0.87 us: local(): jnp.einsum('lm,kmz->klz', operator, fields, precision=lax.Precision.HIGHEST)]
    broadcast_in_dim x1 -> x0, local copies, waits for them, and re-layouts: 1.1 us -> none  [local(): return result[None, None]]
    unnamed x20 -> x18, local copies, waits for them, and re-layouts: 4.87 us -> 3.83 us
    ppermute x3, waiting for transfers between devices: 4.82 us -> 3.95 us  [swapped(): return lax.ppermute(value, axis, [(i, i ^ bit) for i in range(count)])]
    concatenate x1 -> x0, local copies, waits for them, and re-layouts: 0.71 us -> none  [local(): wide = jnp.concatenate([from_left, fields, from_right], axis=2)]
    gather x1 -> x0, local copies, waits for them, and re-layouts: 0.59 us -> none  [local(): chosen = blocks[:, atm_block[0, 0], :]]
  transfers between devices with their start and end apart: 8 -> 8, of which waited for: 6 -> 5; matrix products, arithmetic and copies ran while one was open for 0% -> 0% of each run, Pallas kernels for 0% -> 9%
where the time goes in v2:
time: 29 us; the launch traced here: 28.6 us
  starting transfers between devices  11.8 us (41%)
  waiting for transfers between devices  8.64 us (30%)
  Pallas kernels  4.17 us (14%)
  local copies, waits for them, and re-layouts  3.84 us (13%)
    ppermute x2, starting transfers between devices, moved(): lax.ppermute(value, axis, [(i, (i + steps) % count) for i in range(count)])  6.12 us
    ppermute x3, waiting for transfers between devices, sideways(): return lax.ppermute(value, ('comp', 'tile'), pairs)  4.69 us
    ppermute x3, waiting for transfers between devices, swapped(): return lax.ppermute(value, axis, [(i, i ^ bit) for i in range(count)])  3.95 us
    ppermute x3, starting transfers between devices, sideways(): return lax.ppermute(value, ('comp', 'tile'), pairs)  3.85 us
    unnamed x18, local copies, waits for them, and re-layouts  3.83 us
    pallas_call x1, Pallas kernels, local(): call(functools.partial(interior_kernel, comps), (f32(fields, ROWS, cells)...  1.9 us
    ppermute x3, starting transfers between devices, swapped(): return lax.ppermute(value, axis, [(i, i ^ bit) for i in range(count)])  1.85 us
    pallas_call x1, Pallas kernels, local(): call(finish_kernel, (f32(fields, ROWS, cells), f32(fields, levels - ROWS,...  0.8 us
  transfers between devices with their start and end apart: 8, of which 5 were waited for; matrix products, arithmetic and copies ran while one was open for 0% of the time, Pallas kernels for 9%

profile of v2, /device:TPU:0, one launch (start us, length us, event | category | flops | bytes accessed | tf_op | source)
XLA Modules:
  0.0 28.6 jit_solution(1426254282110263647)
XLA Ops:
  0.0 0.0 copy-start
  0.0 1.0 %copy-done = f32[1,1,4,16,2048]{4,3,2,1,0:T(8,128)S(1)} copy-done((f32[1,1,4,16,2048]{4,3,2,1,0:T(8,128)S(1)}, f32[1,1,4,16,2048]{4,3,2,1,0:T(8,128)}, u32[]{:S(2)}) %copy-start) | copy-done | bytes 524312
  1.0 0.0 copy-start.2
  1.0 0.7 %copy-done.2 = f32[2,16,16]{2,1,0:T(8,128)S(1)} copy-done((f32[2,16,16]{2,1,0:T(8,128)S(1)}, f32[2,16,16]{2,1,0:T(8,128)}, u32[]{:S(2)}) %copy-start.2) | copy-done | bytes 2072
  1.8 0.0 copy-start.4
  1.8 0.7 %copy-done.4 = f32[2,4,16]{2,1,0:T(4,128)S(1)} copy-done((f32[2,4,16]{2,1,0:T(4,128)S(1)}, f32[2,4,16]{2,1,0:T(4,128)}, u32[]{:S(2)}) %copy-start.4) | copy-done | bytes 536
  2.4 0.0 copy-start.1
  2.5 0.2 edges.1
  2.6 3.0 %collective-permute-start = (f32[8,128]{1,0:T(8,128)S(1)}, f32[8,128]{1,0:T(8,128)S(1)}, u32[]{:S(2)}, u32[]{:S(2)}) collective-permute-start(f32[8,128]{1,0:T(8,128)S(1)} %get-tuple-element.28), channel_id=1, source_target_pairs={{0,1},{1,2},{2,3},{3,4},{4,5},{5,6},{6,7},{7,0},{8,9},{9,10},{10,1... | collective-permute-start | bytes 12296 | tf_op jit(solution)/shard_map/ppermute | solution.py:24
  5.6 3.1 %collective-permute-start.1 = (f32[8,128]{1,0:T(8,128)S(1)}, f32[8,128]{1,0:T(8,128)S(1)}, u32[]{:S(2)}, u32[]{:S(2)}) collective-permute-start(f32[8,128]{1,0:T(8,128)S(1)} %get-tuple-element.29), channel_id=1, source_target_pairs={{0,7},{1,0},{2,1},{3,2},{4,3},{5,4},{6,5},{7,6},{8,15},{9,8},{10,9... | collective-permute-start | bytes 12296 | tf_op jit(solution)/shard_map/ppermute | solution.py:24
  8.7 0.0 copy-start.7
  8.7 0.0 copy-start.8
  8.7 0.0 copy-start.5
  8.7 0.0 copy-start.6
  8.8 0.0 copy-done.1
  8.8 0.6 %copy-done.7 = s32[1,1,16]{2,1,0:T(1,128)S(1)} copy-done((s32[1,1,16]{2,1,0:T(1,128)S(1)}, s32[1,1,16]{2,1,0:T(1,128)}, u32[]{:S(2)}) %copy-start.7) | copy-done | bytes 88
  9.4 0.0 copy-done.8
  9.4 0.0 copy-done.5
  9.5 0.0 copy-done.6
  9.5 1.9 %interior.1 = (f32[4,8,2048]{2,1,0:T(8,128)S(1)}, f32[4,8,2048]{2,1,0:T(8,128)S(1)}, f32[7,16,4,128]{3,2,1,0:T(4,128)S(1)}, f32[7,16,4,128]{3,2,1,0:T(4,128)S(1)...) custom-call(f32[4,16,2048]{2,1,0:T(8,128)S(1)} %bitcast.13, ...), custom_call_target="tpu_custom_call" | custom-call | flops 10000000 | bytes 1250000 | tf_op jit(solution)/shard_map/interior/pallas_call | solution.py:330
  11.4 0.0 collective-permute-done.from_left
  11.4 0.0 collective-permute-done.1.from_right
  11.4 0.6 %rim.1 = (f32[3,16,4,128]{3,2,1,0:T(4,128)S(1)}, f32[3,16,4,128]{3,2,1,0:T(4,128)S(1)}, f32[16,4,128]{2,1,0:T(4,128)S(1)}, f32[4,16,128]{2,1,0:T(8,128)S(1)}) custom-call(f32[8,128]{1,0:T(8,128)S(1)} %collective-permute-done.from_left, f32[8,128]{1,0:T(8,128)S(1)} %collective-permute-done.1.from_right, f32[4,16,128]{2,1,0:T(8,128)S(1)} %get-tuple-element.30.own, ...), custom_call_target="tpu_custom_call" | custom-call | flops 1000000 | bytes 125000 | tf_op jit(solution)/shard_map/rim/pallas_call | solution.py:356
  12.0 0.1 collective-permute-start.2
  12.0 1.3 %collective-permute-done.2 = f32[3,16,4,128]{3,2,1,0:T(4,128)S(1)} collective-permute-done((f32[3,16,4,128]{3,2,1,0:T(4,128)S(1)}, f32[3,16,4,128]{3,2,1,0:T(4,128)S(1)}, u32[]{:S(2)}, u32[]{:S(2)}) %collective-permute-start.2) | collective-permute-done | bytes 98336 | tf_op jit(solution)/shard_map/ppermute | solution.py:29
  13.4 3.7 %collective-permute-start.3 = (f32[16,4,128]{2,1,0:T(4,128)S(1)}, f32[16,4,128]{2,1,0:T(4,128)S(1)}, u32[]{:S(2)}, u32[]{:S(2)}) collective-permute-start(f32[16,4,128]{2,1,0:T(4,128)S(1)} %get-tuple-element.43), channel_id=1, source_target_pairs={{0,7},{1,0},{2,1},{3,2},{4,3},{5,4},{6,5},{7,6},{8,9},{9,10},{10,1... | collective-permute-start | bytes 98312 | tf_op jit(solution)/shard_map/ppermute | solution.py:38
  17.1 0.0 collective-permute-start.5
  17.1 0.1 collective-permute-start.4
  17.2 1.5 %collective-permute-done.3 = f32[16,4,128]{2,1,0:T(4,128)S(1)} collective-permute-done((f32[16,4,128]{2,1,0:T(4,128)S(1)}, f32[16,4,128]{2,1,0:T(4,128)S(1)}, u32[]{:S(2)}, u32[]{:S(2)}) %collective-permute-start.3) | collective-permute-done | bytes 32800 | tf_op jit(solution)/shard_map/ppermute | solution.py:38
  18.7 3.2 %collective-permute-done.5 = f32[16,4,128]{2,1,0:T(4,128)S(1)} collective-permute-done((f32[16,4,128]{2,1,0:T(4,128)S(1)}, f32[16,4,128]{2,1,0:T(4,128)S(1)}, u32[]{:S(2)}, u32[]{:S(2)}) %collective-permute-start.5) | collective-permute-done | bytes 32800 | tf_op jit(solution)/shard_map/ppermute | solution.py:38
  21.9 0.0 collective-permute-done.4
  21.9 0.1 collective-permute-start.6
  22.0 1.2 %collective-permute-done.6 = f32[16,4,128]{2,1,0:T(4,128)S(1)} collective-permute-done((f32[16,4,128]{2,1,0:T(4,128)S(1)}, f32[16,4,128]{2,1,0:T(4,128)S(1)}, u32[]{:S(2)}, u32[]{:S(2)}) %collective-permute-start.6) | collective-permute-done | bytes 32800 | tf_op jit(solution)/shard_map/ppermute | solution.py:29
  23.2 1.7 %collective-permute-start.7 = (f32[16,4,128]{2,1,0:T(4,128)S(1)}, f32[16,4,128]{2,1,0:T(4,128)S(1)}, u32[]{:S(2)}, u32[]{:S(2)}) collective-permute-start(f32[16,4,128]{2,1,0:T(4,128)S(1)} %add.22), channel_id=1, source_target_pairs={{0,16},{8,24},{16,0},{24,8},{1,17},{9,25},{17,1},{25,9},{2,18},{10... | collective-permute-start | bytes 98312 | tf_op jit(solution)/shard_map/ppermute | solution.py:29
  24.9 0.8 %finish.1 = (f32[4,8,2048]{2,1,0:T(8,128)S(1)}, f32[4,8,2048]{2,1,0:T(8,128)S(1)}, f32[1,1,4,16,2048]{4,3,2,1,0:T(8,128)}) custom-call(f32[4,8,2048]{2,1,0:T(8,128)S(1)} %get-tuple-element.26.low_in, f32[4,8,2048]{2,1,0:T(8,128)S(1)} %get-tuple-element.27.high_in, f32[4,16,128]{2,1,0:T(8,128)S(1)} %get-tuple-element.36.edge), custom_call_target="tpu_custom_call", output_to_operand_aliasing={{0}: (0, {}), {1}: (1, {})} | custom-call | flops 10000000 | bytes 1250000 | tf_op jit(solution)/shard_map/finish/pallas_call | solution.py:373
  25.7 1.5 %collective-permute-done.7 = f32[16,4,128]{2,1,0:T(4,128)S(1)} collective-permute-done((f32[16,4,128]{2,1,0:T(4,128)S(1)}, f32[16,4,128]{2,1,0:T(4,128)S(1)}, u32[]{:S(2)}, u32[]{:S(2)}) %collective-permute-start.7) | collective-permute-done | bytes 32800 | tf_op jit(solution)/shard_map/ppermute | solution.py:29
  27.2 0.0 copy-start.3
  27.2 0.7 %copy-done.3 = s32[1,2048]{1,0:T(1,128)S(1)} copy-done((s32[1,2048]{1,0:T(1,128)S(1)}, s32[1,2048]{1,0:T(1,128)}, u32[]{:S(2)}) %copy-start.3) | copy-done | bytes 8216
  27.9 0.8 %ocean.3 = (f32[1,1,4,16,2048]{4,3,2,1,0:T(8,128)}, f32[4,8,2048]{2,1,0:T(8,128)S(1)}) custom-call(f32[1,1,4,16,2048]{4,3,2,1,0:T(8,128)} %get-tuple-element.37.out_in, f32[4,8,2048]{2,1,0:T(8,128)S(1)} %get-tuple-element.38.low_in, f32[16,4,128]{2,1,0:T(4,128)S(1)} %add.23.received, ...), custom_call_target="tpu_custom_call", output_to_operand_aliasing={{0}: (0, {}), {1}: (1, {})} | custom-call | flops 1000000 | bytes 125000 | tf_op jit(solution)/shard_map/ocean/pallas_call | solution.py:391
  (5 shorter events, 0.1 us)
Async XLA Ops:
  0.0 1.0 %copy-start = (f32[1,1,4,16,2048]{4,3,2,1,0:T(8,128)S(1)}, f32[1,1,4,16,2048]{4,3,2,1,0:T(8,128)}, u32[]{:S(2)}) copy-start(f32[1,1,4,16,2048]{4,3,2,1,0:T(8,128)} %state.1) | copy-start | bytes 1572868
  1.0 0.7 %copy-start.2 = (f32[2,16,16]{2,1,0:T(8,128)S(1)}, f32[2,16,16]{2,1,0:T(8,128)}, u32[]{:S(2)}) copy-start(f32[2,16,16]{2,1,0:T(8,128)} %vertical.1) | copy-start | bytes 6148
  1.8 0.7 %copy-start.4 = (f32[2,4,16]{2,1,0:T(4,128)S(1)}, f32[2,4,16]{2,1,0:T(4,128)}, u32[]{:S(2)}) copy-start(f32[2,4,16]{2,1,0:T(4,128)} %mixing.1) | copy-start | bytes 1540
  2.4 6.3 %copy-start.1 = (bf16[1,1,16,128,128]{4,3,2,1,0:T(8,128)(2,1)S(1)}, bf16[1,1,16,128,128]{4,3,2,1,0:T(8,128)(2,1)}, u32[]{:S(2)}) copy-start(bf16[1,1,16,128,128]{4,3,2,1,0:T(8,128)(2,1)} %param.16) | copy-start | bytes 1572868
  2.6 8.7 %collective-permute-start = (f32[8,128]{1,0:T(8,128)S(1)}, f32[8,128]{1,0:T(8,128)S(1)}, u32[]{:S(2)}, u32[]{:S(2)}) collective-permute-start(f32[8,128]{1,0:T(8,128)S(1)} %get-tuple-element.28), channel_id=1, source_target_pairs={{0,1},{1,2},{2,3},{3,4},{4,5},{5,6},{6,7},{7,0},{8,9},{9,10},{10,1... | collective-permute-start | bytes 12296 | tf_op jit(solution)/shard_map/ppermute | solution.py:24
  5.6 5.7 %collective-permute-start.1 = (f32[8,128]{1,0:T(8,128)S(1)}, f32[8,128]{1,0:T(8,128)S(1)}, u32[]{:S(2)}, u32[]{:S(2)}) collective-permute-start(f32[8,128]{1,0:T(8,128)S(1)} %get-tuple-element.29), channel_id=1, source_target_pairs={{0,7},{1,0},{2,1},{3,2},{4,3},{5,4},{6,5},{7,6},{8,15},{9,8},{10,9... | collective-permute-start | bytes 12296 | tf_op jit(solution)/shard_map/ppermute | solution.py:24
  8.7 0.7 %copy-start.7 = (s32[1,1,16]{2,1,0:T(1,128)S(1)}, s32[1,1,16]{2,1,0:T(1,128)}, u32[]{:S(2)}) copy-start(s32[1,1,16]{2,1,0:T(1,128)} %ocean.2) | copy-start | bytes 196
  8.7 0.7 %copy-start.8 = (s32[1,1,16]{2,1,0:T(1,128)S(1)}, s32[1,1,16]{2,1,0:T(1,128)}, u32[]{:S(2)}) copy-start(s32[1,1,16]{2,1,0:T(1,128)} %offset.1) | copy-start | bytes 196
  8.7 0.7 %copy-start.5 = (f32[2,4]{1,0:T(2,128)S(1)}, f32[2,4]{1,0:T(2,128)}, u32[]{:S(2)}) copy-start(f32[2,4]{1,0:T(2,128)} %flux.1) | copy-start | bytes 100
  8.7 0.7 %copy-start.6 = (s32[1,1,16]{2,1,0:T(1,128)S(1)}, s32[1,1,16]{2,1,0:T(1,128)}, u32[]{:S(2)}) copy-start(s32[1,1,16]{2,1,0:T(1,128)} %atm.1) | copy-start | bytes 196
  12.0 1.4 %collective-permute-start.2 = (f32[3,16,4,128]{3,2,1,0:T(4,128)S(1)}, f32[3,16,4,128]{3,2,1,0:T(4,128)S(1)}, u32[]{:S(2)}, u32[]{:S(2)}) collective-permute-start(f32[3,16,4,128]{3,2,1,0:T(4,128)S(1)} %get-tuple-element.41), channel_id=1, source_target_pairs={{0,8},{8,0},{16,24},{24,16},{1,9},{9,1},{17,25},{25,17},{2,10},{10... | collective-permute-start | bytes 294920 | tf_op jit(solution)/shard_map/ppermute | solution.py:29
  13.4 5.3 %collective-permute-start.3 = (f32[16,4,128]{2,1,0:T(4,128)S(1)}, f32[16,4,128]{2,1,0:T(4,128)S(1)}, u32[]{:S(2)}, u32[]{:S(2)}) collective-permute-start(f32[16,4,128]{2,1,0:T(4,128)S(1)} %get-tuple-element.43), channel_id=1, source_target_pairs={{0,7},{1,0},{2,1},{3,2},{4,3},{5,4},{6,5},{7,6},{8,9},{9,10},{10,1... | collective-permute-start | bytes 98312 | tf_op jit(solution)/shard_map/ppermute | solution.py:38
  17.1 4.8 %collective-permute-start.5 = (f32[16,4,128]{2,1,0:T(4,128)S(1)}, f32[16,4,128]{2,1,0:T(4,128)S(1)}, u32[]{:S(2)}, u32[]{:S(2)}) collective-permute-start(f32[16,4,128]{2,1,0:T(4,128)S(1)} %get-tuple-element.44), channel_id=1, source_target_pairs={{0,5},{1,6},{2,7},{3,0},{4,1},{5,2},{6,3},{7,4},{8,11},{9,12},{10,... | collective-permute-start | bytes 98312 | tf_op jit(solution)/shard_map/ppermute | solution.py:38
  17.1 4.8 %collective-permute-start.4 = (f32[16,4,128]{2,1,0:T(4,128)S(1)}, f32[16,4,128]{2,1,0:T(4,128)S(1)}, u32[]{:S(2)}, u32[]{:S(2)}) collective-permute-start(f32[16,4,128]{2,1,0:T(4,128)S(1)} %get-tuple-element.45), channel_id=1, source_target_pairs={{0,6},{1,7},{2,0},{3,1},{4,2},{5,3},{6,4},{7,5},{8,10},{9,11},{10,... | collective-permute-start | bytes 98312 | tf_op jit(solution)/shard_map/ppermute | solution.py:38
  21.9 1.3 %collective-permute-start.6 = (f32[16,4,128]{2,1,0:T(4,128)S(1)}, f32[16,4,128]{2,1,0:T(4,128)S(1)}, u32[]{:S(2)}, u32[]{:S(2)}) collective-permute-start(f32[16,4,128]{2,1,0:T(4,128)S(1)} %bitcast.16), channel_id=1, source_target_pairs={{0,8},{8,0},{16,24},{24,16},{1,9},{9,1},{17,25},{25,17},{2,10},{10... | collective-permute-start | bytes 98312 | tf_op jit(solution)/shard_map/ppermute | solution.py:29
  23.2 4.0 %collective-permute-start.7 = (f32[16,4,128]{2,1,0:T(4,128)S(1)}, f32[16,4,128]{2,1,0:T(4,128)S(1)}, u32[]{:S(2)}, u32[]{:S(2)}) collective-permute-start(f32[16,4,128]{2,1,0:T(4,128)S(1)} %add.22), channel_id=1, source_target_pairs={{0,16},{8,24},{16,0},{24,8},{1,17},{9,25},{17,1},{25,9},{2,18},{10... | collective-permute-start | bytes 98312 | tf_op jit(solution)/shard_map/ppermute | solution.py:29
  27.2 0.7 %copy-start.3 = (s32[1,2048]{1,0:T(1,128)S(1)}, s32[1,2048]{1,0:T(1,128)}, u32[]{:S(2)}) copy-start(s32[1,2048]{1,0:T(1,128)} %mask.1) | copy-start | bytes 24580

commit v3 on v2

--- a/solution.py
+++ b/solution.py
@@ -16,7 +16,7 @@
 F32 = jnp.float32
 BF16 = jnp.bfloat16
 VMEM = pl.BlockSpec(memory_space=pltpu.VMEM)
-ANY = pl.BlockSpec(memory_space=pl.ANY)
+HBM = pl.BlockSpec(memory_space=pltpu.HBM)
 
 
 def moved(value, axis, steps):
@@ -36,6 +36,10 @@
         shift = steps if c % 2 else -steps
         pairs += [(c * tiles + t, c * tiles + (t + shift) % tiles) for t in range(tiles)]
     return lax.ppermute(value, ("comp", "tile"), pairs)
+
+
+def in_hbm(*arrays):
+    return [pltpu.with_memory_space_constraint(a, pltpu.HBM) for a in arrays]
 
 
 def lanes_of(shape):
@@ -106,7 +110,7 @@
     state,
     mix,
     ver,
-    weights,
+    weights_hbm,
     flux,
     atm,
     ocean,
@@ -125,6 +129,7 @@
     press,
     round_ref,
     rim,
+    weights,
     sems,
 ):
     fields, levels, cells = state.shape
@@ -132,7 +137,13 @@
     copies = [
         pltpu.make_async_copy(src, dst, sems.at[i])
         for i, (src, dst) in enumerate(
-            ((flux, flux_s), (atm.at[0, 0], atm_s), (ocean.at[0, 0], ocean_s), (offset.at[0, 0], offset_s))
+            (
+                (flux, flux_s),
+                (atm.at[0, 0], atm_s),
+                (ocean.at[0, 0], ocean_s),
+                (offset.at[0, 0], offset_s),
+                (weights_hbm.at[0, 0], weights),
+            )
         )
     ]
     for copy in copies:
@@ -243,10 +254,11 @@
                 here[place] = total
 
 
-def finish_kernel(low_in, high_in, edge, low, high, out, sems):
+def finish_kernel(comps, low_in, high_in, edge, mask, low, high, land, out, raw, sems):
     fields, _, cells = low.shape
     lane = lanes_of((ROWS, LANES))
-    copies = []
+    copies = [pltpu.make_async_copy(mask, raw, sems.at[fields])]
+    copies[0].start()
     for k in range(fields):
         for half, start in ((low, 0), (high, ROWS)):
             source = low_in if start == 0 else high_in
@@ -261,25 +273,23 @@
         copies[-1].start()
     for copy in copies:
         copy.wait()
-
-
-def ocean_kernel(comps, out_in, low_in, received, mask, out, low, sems):
+    land[...] = jnp.where(atmosphere(comps), 0.0, raw[...].astype(F32))
+
+
+def ocean_kernel(out_in, low_in, received, land, out, low, sems):
     fields, rows, cells = low.shape
-    is_ocean = jnp.logical_not(atmosphere(comps))
     copies = []
     for k in range(fields):
         for b in range(cells // LANES):
             at = slice(b * LANES, (b + 1) * LANES)
-            land = mask[:, at].astype(F32)
-            gain = jnp.where(is_ocean, land * received[b, k : k + 1, :], 0.0)
-            low[k, 0:1, at] = low_in[k, 0:1, at] + gain
+            low[k, 0:1, at] = low_in[k, 0:1, at] + land[:, at] * received[b, k : k + 1, :]
         copies.append(pltpu.make_async_copy(low.at[k], out.at[0, 0, k, pl.ds(0, rows), :], sems.at[k]))
         copies[-1].start()
     for copy in copies:
         copy.wait()
 
 
-def call(body, out_shape, in_specs, out_specs, scratch, flops, aliases=None, name=None):
+def call(body, out_shape, in_specs, out_specs, scratch, flops, aliases=None):
     return pl.pallas_call(
         body,
         out_shape=out_shape,
@@ -289,11 +299,10 @@
         input_output_aliases=aliases or {},
         compiler_params=pltpu.CompilerParams(vmem_limit_bytes=16 << 20),
         cost_estimate=pl.CostEstimate(flops=flops, bytes_accessed=flops // 8, transcendentals=0),
-        name=name,
     )
 
 
-def local(
+def step(
     column_state,
     mixing,
     vertical,
@@ -319,12 +328,11 @@
     own, to_right, to_left, mix, ver = call(
         functools.partial(edges_kernel, comps),
         (f32(fields, levels, LANES), f32(ROWS, LANES), f32(ROWS, LANES), f32(fields, levels), f32(levels, levels)),
-        [ANY] * 3,
+        [HBM] * 3,
         [VMEM] * 5,
         [pltpu.VMEM((fields, levels, LANES), F32)] * 2 + [pltpu.SemaphoreType.DMA((4,))],
         10**5,
-        name="edges",
-    )(column_state, mixing, vertical)
+    )(*in_hbm(column_state, mixing, vertical))
     from_left = moved(to_right, "tile", 1)
     from_right = moved(to_left, "tile", -1)
     low, high, buf, wide, coef, parts, flux = call(
@@ -338,7 +346,7 @@
             jax.ShapeDtypeStruct((2, levels, levels), BF16),
             f32(2, fields, LANES),
         ),
-        [VMEM] * 4 + [ANY] * 4,
+        [VMEM] * 3 + [HBM] * 5,
         [VMEM] * 7,
         [
             pltpu.SMEM(flux_coef.shape, F32),
@@ -348,11 +356,11 @@
             pltpu.VMEM((fields, cells), F32),
             pltpu.VMEM((blocks, ROWS, LANES), F32),
             pltpu.VMEM((EDGES, LANES), F32),
-            pltpu.SemaphoreType.DMA((4,)),
+            pltpu.VMEM(remap_weights.shape[2:], BF16),
+            pltpu.SemaphoreType.DMA((5,)),
         ],
         10**7,
-        name="interior",
-    )(column_state[0, 0], mix, ver, remap_weights[0, 0], flux_coef, atm_block, ocean_block, tile_offset)
+    )(column_state[0, 0], mix, ver, *in_hbm(remap_weights, flux_coef, atm_block, ocean_block, tile_offset))
     mine, theirs, received, edge = call(
         functools.partial(rim_kernel, comps),
         (
@@ -365,39 +373,38 @@
         [VMEM] * 4,
         [pltpu.VMEM((fields, LANES), F32)],
         10**6,
-        name="rim",
     )(from_left, from_right, own, coef, parts, flux, buf, wide)
     mine = mine + swapped(theirs, "comp", 1)
-    for step in range(1, REACH + 1):
-        received = received + sideways(mine[step - 1], step)
-    low, high, out = call(
-        finish_kernel,
+    for step in range(REACH, 0, -1):
+        arrived = sideways(mine[step - 1], step)
+        received = received + arrived
+    low, high, land, out = call(
+        functools.partial(finish_kernel, comps),
         (
             f32(fields, ROWS, cells),
             f32(fields, levels - ROWS, cells),
+            f32(1, cells),
             jax.ShapeDtypeStruct(column_state.shape, F32),
         ),
-        [VMEM] * 3,
-        [VMEM, VMEM, ANY],
-        [pltpu.SemaphoreType.DMA((fields,))],
+        [VMEM] * 3 + [HBM],
+        [VMEM, VMEM, VMEM, HBM],
+        [pltpu.VMEM(ocean_mask.shape, jnp.int32), pltpu.SemaphoreType.DMA((fields + 1,))],
         10**7,
         aliases={0: 0, 1: 1},
-        name="finish",
-    )(low, high, edge)
+    )(low, high, edge, *in_hbm(ocean_mask))
     bit = 1
     while bit < comps:
         received = received + swapped(received, "comp", bit)
         bit *= 2
     out, _ = call(
-        functools.partial(ocean_kernel, comps),
+        ocean_kernel,
         (jax.ShapeDtypeStruct(column_state.shape, F32), f32(fields, ROWS, cells)),
-        [ANY, VMEM, VMEM, VMEM],
-        [ANY, VMEM],
+        [HBM, VMEM, VMEM, VMEM],
+        [HBM, VMEM],
         [pltpu.SemaphoreType.DMA((fields,))],
         10**6,
         aliases={0: 0, 1: 1},
-        name="ocean",
-    )(out, low, received, ocean_mask)
+    )(out, low, received, land)
     return out
 
 
@@ -414,7 +421,7 @@
         P("tile", None),
     )
     return jax.shard_map(
-        local,
+        step,
         mesh=mesh,
         in_specs=placed,
         out_specs=P("comp", "tile", None, None, None),

time: 29 us -> 25.7 us (0.89)
  local copies, waits for them, and re-layouts: 3.84 us -> 0.01 us
  Pallas kernels: 4.17 us -> 5.13 us
  waiting for transfers between devices: 8.64 us -> 7.71 us
  starting transfers between devices: 11.8 us -> 12.4 us
    unnamed x18 -> x2, local copies, waits for them, and re-layouts: 3.83 us -> 0.01 us
    pallas_call x5, Pallas kernels: 4.17 us -> 5.13 us  [the longest x1 2.05 us: step(): call(functools.partial(interior_kernel, comps), (f32(fields, ROWS, cells)...]
    ppermute x3, waiting for transfers between devices: 4.69 us -> 3.78 us  [sideways(): return lax.ppermute(value, ('comp', 'tile'), pairs)]
    ppermute x3, starting transfers between devices: 3.85 us -> 4.47 us  [sideways(): return lax.ppermute(value, ('comp', 'tile'), pairs)]
  transfers between devices with their start and end apart: 8 -> 8, of which waited for: 5 -> 6; matrix products, arithmetic and copies ran while one was open for 0% -> 0% of each run, Pallas kernels for 9% -> 11%
where the time goes in v3:
time: 25.7 us; the launch traced here: 25.5 us
  starting transfers between devices  12.4 us (48%)
  waiting for transfers between devices  7.71 us (30%)
  Pallas kernels  5.13 us (20%)
    ppermute x2, starting transfers between devices, moved(): lax.ppermute(value, axis, [(i, (i + steps) % count) for i in range(count)])  6.12 us
    ppermute x3, starting transfers between devices, sideways(): return lax.ppermute(value, ('comp', 'tile'), pairs)  4.47 us
    ppermute x3, waiting for transfers between devices, swapped(): return lax.ppermute(value, axis, [(i, i ^ bit) for i in range(count)])  3.93 us
    ppermute x3, waiting for transfers between devices, sideways(): return lax.ppermute(value, ('comp', 'tile'), pairs)  3.78 us
    pallas_call x1, Pallas kernels, step(): call(functools.partial(interior_kernel, comps), (f32(fields, ROWS, cells)...  2.05 us
    ppermute x3, starting transfers between devices, swapped(): return lax.ppermute(value, axis, [(i, i ^ bit) for i in range(count)])  1.85 us
    pallas_call x1, Pallas kernels, step(): call(functools.partial(edges_kernel, comps), (f32(fields, levels, LANES),...  0.97 us
    pallas_call x1, Pallas kernels, step(): call(functools.partial(finish_kernel, comps), (f32(fields, ROWS, cells),...  0.81 us
  transfers between devices with their start and end apart: 8, of which 6 were waited for; matrix products, arithmetic and copies ran while one was open for 0% of the time, Pallas kernels for 11%

profile of v3, /device:TPU:0, one launch (start us, length us, event | category | flops | bytes accessed | tf_op | source)
XLA Modules:
  0.0 25.5 jit_solution(9107415466960504384)
XLA Ops:
  0.0 0.0 copy-start
  0.0 1.0 %shard_map.91 = (f32[4,16,128]{2,1,0:T(8,128)S(1)}, f32[8,128]{1,0:T(8,128)S(1)}, f32[8,128]{1,0:T(8,128)S(1)}, f32[4,16]{1,0:T(4,128)S(1)}, f32[16,16]{1,0:T(8,128)S(1)}) custom-call(f32[1,1,4,16,2048]{4,3,2,1,0:T(8,128)} %state.1, f32[2,4,16]{2,1,0:T(4,128)} %mixing.1, f32[2,16,16]{2,1,0:T(8,128)} %vertical.1), custom_call_target="tpu_custom_call" | custom-call | flops 100000 | bytes 12500 | tf_op jit(solution)/shard_map/pallas_call | solution.py:328
  1.0 3.0 %collective-permute-start = (f32[8,128]{1,0:T(8,128)S(1)}, f32[8,128]{1,0:T(8,128)S(1)}, u32[]{:S(2)}, u32[]{:S(2)}) collective-permute-start(f32[8,128]{1,0:T(8,128)S(1)} %get-tuple-element.29), channel_id=1, source_target_pairs={{0,1},{1,2},{2,3},{3,4},{4,5},{5,6},{6,7},{7,0},{8,9},{9,10},{10,1... | collective-permute-start | bytes 12296 | tf_op jit(solution)/shard_map/ppermute | solution.py:24
  4.0 3.1 %collective-permute-start.1 = (f32[8,128]{1,0:T(8,128)S(1)}, f32[8,128]{1,0:T(8,128)S(1)}, u32[]{:S(2)}, u32[]{:S(2)}) collective-permute-start(f32[8,128]{1,0:T(8,128)S(1)} %get-tuple-element.30), channel_id=1, source_target_pairs={{0,7},{1,0},{2,1},{3,2},{4,3},{5,4},{6,5},{7,6},{8,15},{9,8},{10,9... | collective-permute-start | bytes 12296 | tf_op jit(solution)/shard_map/ppermute | solution.py:24
  7.1 0.0 copy-done
  7.1 2.0 %shard_map.92 = (f32[4,8,2048]{2,1,0:T(8,128)S(1)}, f32[4,8,2048]{2,1,0:T(8,128)S(1)}, f32[7,16,4,128]{3,2,1,0:T(4,128)S(1)}, f32[7,16,4,128]{3,2,1,0:T(4,128)S(...) custom-call(f32[4,16,2048]{2,1,0:T(8,128)S(1)} %bitcast.12, ...), custom_call_target="tpu_custom_call" | custom-call | flops 10000000 | bytes 1250000 | tf_op jit(solution)/shard_map/pallas_call | solution.py:338
  9.2 0.0 collective-permute-done.from_left
  9.2 0.0 collective-permute-done.1.from_right
  9.2 0.5 %shard_map.93 = (f32[3,16,4,128]{3,2,1,0:T(4,128)S(1)}, f32[3,16,4,128]{3,2,1,0:T(4,128)S(1)}, f32[16,4,128]{2,1,0:T(4,128)S(1)}, f32[4,16,128]{2,1,0:T(8,128)S(1)}) custom-call(f32[8,128]{1,0:T(8,128)S(1)} %collective-permute-done.from_left, f32[8,128]{1,0:T(8,128)S(1)} %collective-permute-done.1.from_right, f32[4,16,128]{2,1,0:T(8,128)S(1)} %get-tuple-element.31.own, ...), custom_call_target="tpu_custom_call" | custom-call | flops 1000000 | bytes 125000 | tf_op jit(solution)/shard_map/pallas_call | solution.py:364
  9.7 0.1 collective-permute-start.2
  9.8 1.3 %collective-permute-done.2 = f32[3,16,4,128]{3,2,1,0:T(4,128)S(1)} collective-permute-done((f32[3,16,4,128]{3,2,1,0:T(4,128)S(1)}, f32[3,16,4,128]{3,2,1,0:T(4,128)S(1)}, u32[]{:S(2)}, u32[]{:S(2)}) %collective-permute-start.2) | collective-permute-done | bytes 98336 | tf_op jit(solution)/shard_map/ppermute | solution.py:29
  11.1 2.9 %collective-permute-start.3 = (f32[16,4,128]{2,1,0:T(4,128)S(1)}, f32[16,4,128]{2,1,0:T(4,128)S(1)}, u32[]{:S(2)}, u32[]{:S(2)}) collective-permute-start(f32[16,4,128]{2,1,0:T(4,128)S(1)} %get-tuple-element.45), channel_id=1, source_target_pairs={{0,5},{1,6},{2,7},{3,0},{4,1},{5,2},{6,3},{7,4},{8,11},{9,12},{10,... | collective-permute-start | bytes 98312 | tf_op jit(solution)/shard_map/ppermute | solution.py:38
  14.1 1.4 %collective-permute-start.5 = (f32[16,4,128]{2,1,0:T(4,128)S(1)}, f32[16,4,128]{2,1,0:T(4,128)S(1)}, u32[]{:S(2)}, u32[]{:S(2)}) collective-permute-start(f32[16,4,128]{2,1,0:T(4,128)S(1)} %get-tuple-element.46), channel_id=1, source_target_pairs={{0,7},{1,0},{2,1},{3,2},{4,3},{5,4},{6,5},{7,6},{8,9},{9,10},{10,1... | collective-permute-start | bytes 98312 | tf_op jit(solution)/shard_map/ppermute | solution.py:38
  15.5 0.1 collective-permute-start.4
  15.6 0.6 %collective-permute-done.3 = f32[16,4,128]{2,1,0:T(4,128)S(1)} collective-permute-done((f32[16,4,128]{2,1,0:T(4,128)S(1)}, f32[16,4,128]{2,1,0:T(4,128)S(1)}, u32[]{:S(2)}, u32[]{:S(2)}) %collective-permute-start.3) | collective-permute-done | bytes 32800 | tf_op jit(solution)/shard_map/ppermute | solution.py:38
  16.3 1.7 %collective-permute-done.5 = f32[16,4,128]{2,1,0:T(4,128)S(1)} collective-permute-done((f32[16,4,128]{2,1,0:T(4,128)S(1)}, f32[16,4,128]{2,1,0:T(4,128)S(1)}, u32[]{:S(2)}, u32[]{:S(2)}) %collective-permute-start.5) | collective-permute-done | bytes 32800 | tf_op jit(solution)/shard_map/ppermute | solution.py:38
  18.0 1.4 %collective-permute-done.4 = f32[16,4,128]{2,1,0:T(4,128)S(1)} collective-permute-done((f32[16,4,128]{2,1,0:T(4,128)S(1)}, f32[16,4,128]{2,1,0:T(4,128)S(1)}, u32[]{:S(2)}, u32[]{:S(2)}) %collective-permute-start.4) | collective-permute-done | bytes 32800 | tf_op jit(solution)/shard_map/ppermute | solution.py:38
  19.4 0.1 collective-permute-start.6
  19.5 1.2 %collective-permute-done.6 = f32[16,4,128]{2,1,0:T(4,128)S(1)} collective-permute-done((f32[16,4,128]{2,1,0:T(4,128)S(1)}, f32[16,4,128]{2,1,0:T(4,128)S(1)}, u32[]{:S(2)}, u32[]{:S(2)}) %collective-permute-start.6) | collective-permute-done | bytes 32800 | tf_op jit(solution)/shard_map/ppermute | solution.py:29
  20.7 1.7 %collective-permute-start.7 = (f32[16,4,128]{2,1,0:T(4,128)S(1)}, f32[16,4,128]{2,1,0:T(4,128)S(1)}, u32[]{:S(2)}, u32[]{:S(2)}) collective-permute-start(f32[16,4,128]{2,1,0:T(4,128)S(1)} %add.22), channel_id=1, source_target_pairs={{0,16},{8,24},{16,0},{24,8},{1,17},{9,25},{17,1},{25,9},{2,18},{10... | collective-permute-start | bytes 98312 | tf_op jit(solution)/shard_map/ppermute | solution.py:29
  22.4 0.8 %shard_map.94 = (f32[4,8,2048]{2,1,0:T(8,128)S(1)}, f32[4,8,2048]{2,1,0:T(8,128)S(1)}, f32[1,2048]{1,0:T(1,128)S(1)}, f32[1,1,4,16,2048]{4,3,2,1,0:T(8,128)}) custom-call(f32[4,8,2048]{2,1,0:T(8,128)S(1)} %get-tuple-element.27.low_in, f32[4,8,2048]{2,1,0:T(8,128)S(1)} %get-tuple-element.28.high_in, ...), custom_call_target="tpu_custom_call", output_to_operand_aliasing={{0}: (0, {}), {1}: (1, {})} | custom-call | flops 10000000 | bytes 1250000 | tf_op jit(solution)/shard_map/pallas_call | solution.py:381
  23.2 1.4 %collective-permute-done.7 = f32[16,4,128]{2,1,0:T(4,128)S(1)} collective-permute-done((f32[16,4,128]{2,1,0:T(4,128)S(1)}, f32[16,4,128]{2,1,0:T(4,128)S(1)}, u32[]{:S(2)}, u32[]{:S(2)}) %collective-permute-start.7) | collective-permute-done | bytes 32800 | tf_op jit(solution)/shard_map/ppermute | solution.py:29
  24.7 0.8 %shard_map.95 = (f32[1,1,4,16,2048]{4,3,2,1,0:T(8,128)}, f32[4,8,2048]{2,1,0:T(8,128)S(1)}) custom-call(f32[1,1,4,16,2048]{4,3,2,1,0:T(8,128)} %get-tuple-element.38.out_in, f32[4,8,2048]{2,1,0:T(8,128)S(1)} %get-tuple-element.39.low_in, f32[16,4,128]{2,1,0:T(4,128)S(1)} %add.23.received, ...), custom_call_target="tpu_custom_call", output_to_operand_aliasing={{0}: (0, {}), {1}: (1, {})} | custom-call | flops 1000000 | bytes 125000 | tf_op jit(solution)/shard_map/pallas_call | solution.py:399
  (5 shorter events, 0.1 us)
Async XLA Ops:
  0.0 7.1 %copy-start = (f32[1,1,4,16,2048]{4,3,2,1,0:T(8,128)S(1)}, f32[1,1,4,16,2048]{4,3,2,1,0:T(8,128)}, u32[]{:S(2)}) copy-start(f32[1,1,4,16,2048]{4,3,2,1,0:T(8,128)} %state.1) | copy-start | bytes 1572868
  1.0 8.2 %collective-permute-start = (f32[8,128]{1,0:T(8,128)S(1)}, f32[8,128]{1,0:T(8,128)S(1)}, u32[]{:S(2)}, u32[]{:S(2)}) collective-permute-start(f32[8,128]{1,0:T(8,128)S(1)} %get-tuple-element.29), channel_id=1, source_target_pairs={{0,1},{1,2},{2,3},{3,4},{4,5},{5,6},{6,7},{7,0},{8,9},{9,10},{10,1... | collective-permute-start | bytes 12296 | tf_op jit(solution)/shard_map/ppermute | solution.py:24
  4.0 5.2 %collective-permute-start.1 = (f32[8,128]{1,0:T(8,128)S(1)}, f32[8,128]{1,0:T(8,128)S(1)}, u32[]{:S(2)}, u32[]{:S(2)}) collective-permute-start(f32[8,128]{1,0:T(8,128)S(1)} %get-tuple-element.30), channel_id=1, source_target_pairs={{0,7},{1,0},{2,1},{3,2},{4,3},{5,4},{6,5},{7,6},{8,15},{9,8},{10,9... | collective-permute-start | bytes 12296 | tf_op jit(solution)/shard_map/ppermute | solution.py:24
  9.7 1.4 %collective-permute-start.2 = (f32[3,16,4,128]{3,2,1,0:T(4,128)S(1)}, f32[3,16,4,128]{3,2,1,0:T(4,128)S(1)}, u32[]{:S(2)}, u32[]{:S(2)}) collective-permute-start(f32[3,16,4,128]{3,2,1,0:T(4,128)S(1)} %get-tuple-element.42), channel_id=1, source_target_pairs={{0,8},{8,0},{16,24},{24,16},{1,9},{9,1},{17,25},{25,17},{2,10},{10... | collective-permute-start | bytes 294920 | tf_op jit(solution)/shard_map/ppermute | solution.py:29
  11.1 5.1 %collective-permute-start.3 = (f32[16,4,128]{2,1,0:T(4,128)S(1)}, f32[16,4,128]{2,1,0:T(4,128)S(1)}, u32[]{:S(2)}, u32[]{:S(2)}) collective-permute-start(f32[16,4,128]{2,1,0:T(4,128)S(1)} %get-tuple-element.45), channel_id=1, source_target_pairs={{0,5},{1,6},{2,7},{3,0},{4,1},{5,2},{6,3},{7,4},{8,11},{9,12},{10,... | collective-permute-start | bytes 98312 | tf_op jit(solution)/shard_map/ppermute | solution.py:38
  14.1 3.9 %collective-permute-start.5 = (f32[16,4,128]{2,1,0:T(4,128)S(1)}, f32[16,4,128]{2,1,0:T(4,128)S(1)}, u32[]{:S(2)}, u32[]{:S(2)}) collective-permute-start(f32[16,4,128]{2,1,0:T(4,128)S(1)} %get-tuple-element.46), channel_id=1, source_target_pairs={{0,7},{1,0},{2,1},{3,2},{4,3},{5,4},{6,5},{7,6},{8,9},{9,10},{10,1... | collective-permute-start | bytes 98312 | tf_op jit(solution)/shard_map/ppermute | solution.py:38
  15.5 3.9 %collective-permute-start.4 = (f32[16,4,128]{2,1,0:T(4,128)S(1)}, f32[16,4,128]{2,1,0:T(4,128)S(1)}, u32[]{:S(2)}, u32[]{:S(2)}) collective-permute-start(f32[16,4,128]{2,1,0:T(4,128)S(1)} %get-tuple-element.47), channel_id=1, source_target_pairs={{0,6},{1,7},{2,0},{3,1},{4,2},{5,3},{6,4},{7,5},{8,10},{9,11},{10,... | collective-permute-start | bytes 98312 | tf_op jit(solution)/shard_map/ppermute | solution.py:38
  19.4 1.3 %collective-permute-start.6 = (f32[16,4,128]{2,1,0:T(4,128)S(1)}, f32[16,4,128]{2,1,0:T(4,128)S(1)}, u32[]{:S(2)}, u32[]{:S(2)}) collective-permute-start(f32[16,4,128]{2,1,0:T(4,128)S(1)} %bitcast.14), channel_id=1, source_target_pairs={{0,8},{8,0},{16,24},{24,16},{1,9},{9,1},{17,25},{25,17},{2,10},{10... | collective-permute-start | bytes 98312 | tf_op jit(solution)/shard_map/ppermute | solution.py:29
  20.7 4.0 %collective-permute-start.7 = (f32[16,4,128]{2,1,0:T(4,128)S(1)}, f32[16,4,128]{2,1,0:T(4,128)S(1)}, u32[]{:S(2)}, u32[]{:S(2)}) collective-permute-start(f32[16,4,128]{2,1,0:T(4,128)S(1)} %add.22), channel_id=1, source_target_pairs={{0,16},{8,24},{16,0},{24,8},{1,17},{9,25},{17,1},{25,9},{2,18},{10... | collective-permute-start | bytes 98312 | tf_op jit(solution)/shard_map/ppermute | solution.py:29

commit v4 on v3

--- a/solution.py
+++ b/solution.py
@@ -22,6 +22,22 @@
 def moved(value, axis, steps):
     count = lax.axis_size(axis)
     return lax.ppermute(value, axis, [(i, (i + steps) % count) for i in range(count)])
+
+
+def gathered(value):
+    comps = lax.axis_size("comp")
+    last = comps - 1
+    if comps == 4:
+        cycles = [(1, last, 2, 0), (0, last, 2, 1)]
+        paths = [list(zip(c, c[1:] + c[:1])) for c in cycles]
+        paths.append([(i, i ^ 1) for i in range(comps)])
+    else:
+        paths = [[(i, (i + s) % comps) for i in range(comps)] for s in range(1, comps)]
+    total = value
+    for pairs in paths:
+        arrived = lax.ppermute(value, "comp", pairs)
+        total = total + arrived
+    return total
 
 
 def swapped(value, axis, bit):
@@ -105,6 +121,11 @@
         copy.wait()
 
 
+def column_of(row, square):
+    eye = lax.broadcasted_iota(jnp.int32, square, 0) == lanes_of(square)
+    return jnp.sum(jnp.where(eye, jnp.broadcast_to(row, square), 0.0), axis=1, keepdims=True)
+
+
 def interior_kernel(
     comps,
     state,
@@ -115,13 +136,11 @@
     atm,
     ocean,
     offset,
-    low,
-    high,
+    spread_out,
     buf,
     wide,
     coef,
-    parts,
-    flux_out,
+    lean,
     flux_s,
     atm_s,
     ocean_s,
@@ -152,43 +171,33 @@
     right_core = lax.axis_index("comp") % 2
     buf[...] = jnp.zeros_like(buf)
     wide[...] = jnp.zeros_like(wide)
-    vh, vl = split(ver[...])
-    parts[0] = vh
-    parts[1] = vl
     square = (levels, levels)
-    eye = lax.broadcasted_iota(jnp.int32, square, 0) == lanes_of(square)
-    copies[0].wait()
+    lane = lanes_of((1, levels))
+    last = ver[levels - 1 : levels, :] + jnp.where(lane == levels - 1, 1.0, 0.0)
+    second = ver[levels - 2 : levels - 1, :] + jnp.where(lane == levels - 2, 1.0, 0.0)
+    last, second = column_of(last, square), column_of(second, square)
     for k in range(fields):
-        rate = jnp.sum(
-            jnp.where(eye, jnp.broadcast_to(mix[k : k + 1, :], square), 0.0), axis=1, keepdims=True
-        )
+        rate = column_of(mix[k : k + 1, :], square)
         far = rate * rate
         near = 2.0 * rate - 4.0 * far
         mid = 1.0 - 4.0 * rate + 6.0 * far
         for i, c in enumerate((mid, near, far)):
             coef[i, k] = jnp.broadcast_to(c, (levels, LANES))
-        field = stencil((mid, near, far), state[k])
-        mixed = field + product(vh, vl, field)
-        low[k] = mixed[:ROWS]
-        high[k] = mixed[ROWS:]
-        press[k : k + 1, :] = (
-            flux_s[0, k] * mixed[levels - 1 : levels, :] + flux_s[1, k] * mixed[levels - 2 : levels - 1, :]
-        )
-        for i in range(2):
-            flux_out[i, k : k + 1, :] = jnp.full((1, LANES), flux_s[i, k], F32)
-    surface = jnp.tanh(press[...])
-    press[...] = jnp.where(is_atmos, surface, 0.0)
-    last = high.shape[1] - 1
+        spread_out[k] = stencil((mid, near, far), state[k])
+    copies[0].wait()
     for k in range(fields):
-        high[k, last : last + 1, :] = high[k, last : last + 1, :] - 0.5 * press[k : k + 1, :]
+        pull = flux_s[0, k] * last + flux_s[1, k] * second
+        lean[k] = jnp.broadcast_to(pull, (levels, LANES))
+        press[k : k + 1, :] = jnp.sum(pull * spread_out[k], axis=0, keepdims=True)
+    surface = jnp.where(is_atmos, jnp.tanh(press[...]), 0.0).astype(BF16).astype(F32)
     lane = lanes_of((fields, LANES))
+    round_ref[...] = jnp.zeros_like(round_ref)
     for b in range(blocks):
-        value = press[:, b * LANES : (b + 1) * LANES].astype(BF16).astype(F32)
+        value = surface[:, b * LANES : (b + 1) * LANES]
         if b == 0:
             value = jnp.where(lane < SUB, 0.0, value)
         if b == blocks - 1:
             value = jnp.where(lane >= LANES - SUB, 0.0, value)
-        round_ref[b] = jnp.zeros(round_ref.shape[1:], F32)
         round_ref[b, :fields, :] = value
     for copy in copies[1:]:
         copy.wait()
@@ -202,43 +211,33 @@
         slot = jnp.where(distance == 0, 2 * REACH, slot)
         term = jnp.dot(round_ref[block].astype(BF16), weights[n], preferred_element_type=F32)
         buf[slot, place] = buf[slot, place] + term[:fields]
-        rim[:SUB, :] = weights[n, : 2 * ROWS, :].astype(F32)[:SUB]
-        rim[SUB:, :] = weights[n, LANES - 2 * ROWS :, :].astype(F32)[2 * ROWS - SUB :]
+        rim[n, :SUB, :] = weights[n, : 2 * ROWS, :].astype(F32)[:SUB]
+        rim[n, SUB:, :] = weights[n, LANES - 2 * ROWS :, :].astype(F32)[2 * ROWS - SUB :]
         lead = jnp.where(block == 0, 1.0, 0.0)
         trail = jnp.where(block == blocks - 1, 1.0, 0.0)
-        wide[slot, place] = wide[slot, place] + jnp.where(side, lead, trail) * rim[...]
+        wide[slot, place] = wide[slot, place] + jnp.where(side, lead, trail) * rim[n]
 
 
 def rim_kernel(
-    comps, from_left, from_right, own, coef, parts, flux, buf, wide, mine, theirs, here, edge, press
+    comps, from_left, from_right, own, coef, lean, buf, wide, mine, theirs, here, edge, press
 ):
     fields, levels, _ = own.shape
-    is_atmos = atmosphere(comps)
     lane = lanes_of((ROWS, LANES))
+    beyond = (lane >= MID + 2 * SUB) & (lane < MID + 3 * SUB)
     number = 0
     for k in range(fields):
+        total = jnp.zeros((ROWS, LANES), F32)
         for h in range(0, levels, ROWS):
             at = SUB * number
             x = own[k, h : h + ROWS, :]
             x = jnp.where(lane < SUB, turned(from_left[...], -at), x)
-            beyond = (lane >= MID + 2 * SUB) & (lane < MID + 3 * SUB)
             x = jnp.where(beyond, turned(from_right[...], MID + 2 * SUB - at), x)
-            c = [coef[i, k, h : h + ROWS, :] for i in range(3)]
-            edge[k, h : h + ROWS, :] = stencil(c, x)
+            field = stencil([coef[i, k, h : h + ROWS, :] for i in range(3)], x)
+            edge[k, h : h + ROWS, :] = field
+            total = total + lean[k, h : h + ROWS, :] * field
             number += 1
-    for k in range(fields):
-        field = edge[k]
-        mixed = field + product(parts[0], parts[1], field)
-        edge[k] = mixed
-        press[k : k + 1, :] = (
-            flux[0, k : k + 1, :] * mixed[levels - 1 : levels, :]
-            + flux[1, k : k + 1, :] * mixed[levels - 2 : levels - 1, :]
-        )
-    surface = jnp.where(is_atmos, jnp.tanh(press[...]), 0.0)
-    press[...] = surface
-    for k in range(fields):
-        edge[k, levels - 1 : levels, :] = edge[k, levels - 1 : levels, :] - 0.5 * press[k : k + 1, :]
-    value = surface.astype(BF16).astype(F32)
+        press[k : k + 1, :] = jnp.sum(total, axis=0, keepdims=True)
+    value = jnp.where(atmosphere(comps), jnp.tanh(press[...]), 0.0).astype(BF16).astype(F32)
     spots = [SUB + i for i in range(SUB)] + [MID + SUB + i for i in range(SUB)]
     column = [jnp.broadcast_to(value[:, s : s + 1], (fields, LANES)) for s in spots]
     for slot in range(buf.shape[0]):
@@ -254,39 +253,63 @@
                 here[place] = total
 
 
-def finish_kernel(comps, low_in, high_in, edge, mask, low, high, land, out, raw, sems):
-    fields, _, cells = low.shape
-    lane = lanes_of((ROWS, LANES))
-    copies = [pltpu.make_async_copy(mask, raw, sems.at[fields])]
-    copies[0].start()
+def finish_kernel(comps, field_in, edge, ver, flux, mask, low, land, out, high, press, raw, flux_s, sems):
+    fields, levels, cells = field_in.shape
+    copies = [
+        pltpu.make_async_copy(mask, raw, sems.at[2 * fields]),
+        pltpu.make_async_copy(flux, flux_s, sems.at[2 * fields + 1]),
+    ]
+    for copy in copies:
+        copy.start()
+    vh, vl = split(ver[...])
+    lane = lanes_of((levels, LANES))
+    is_atmos = atmosphere(comps)
+    copies[1].wait()
+    waits = [copies[0]]
     for k in range(fields):
-        for half, start in ((low, 0), (high, ROWS)):
-            source = low_in if start == 0 else high_in
-            value = edge[k, start : start + ROWS, :]
-            half[k, :, :LANES] = jnp.where(lane < SUB, turned(value, -SUB), source[k, :, :LANES])
-            half[k, :, cells - LANES :] = jnp.where(
-                lane >= LANES - SUB, turned(value, MID - 2 * SUB), source[k, :, cells - LANES :]
+        value = edge[k]
+        first = jnp.where(lane < SUB, turned(value, -SUB), field_in[k, :, :LANES])
+        last = jnp.where(lane >= LANES - SUB, turned(value, MID - 2 * SUB), field_in[k, :, cells - LANES :])
+        field = jnp.concatenate([first, field_in[k, :, LANES : cells - LANES], last], axis=1)
+        mixed = field + product(vh, vl, field)
+        low[k] = mixed[:ROWS]
+        high[k] = mixed[ROWS:]
+        press[k : k + 1, :] = (
+            flux_s[0, k] * mixed[levels - 1 : levels, :] + flux_s[1, k] * mixed[levels - 2 : levels - 1, :]
+        )
+        waits.append(pltpu.make_async_copy(low.at[k], out.at[0, 0, k, pl.ds(0, ROWS), :], sems.at[k]))
+        waits[-1].start()
+    press[...] = jnp.where(is_atmos, jnp.tanh(press[...]), 0.0)
+    end = high.shape[1] - 1
+    for k in range(fields):
+        high[k, end : end + 1, :] = high[k, end : end + 1, :] - 0.5 * press[k : k + 1, :]
+        waits.append(
+            pltpu.make_async_copy(
+                high.at[k], out.at[0, 0, k, pl.ds(ROWS, levels - ROWS), :], sems.at[fields + k]
             )
-        copies.append(
-            pltpu.make_async_copy(high.at[k], out.at[0, 0, k, pl.ds(ROWS, high.shape[1]), :], sems.at[k])
         )
-        copies[-1].start()
-    for copy in copies:
+        waits[-1].start()
+    for copy in waits:
         copy.wait()
-    land[...] = jnp.where(atmosphere(comps), 0.0, raw[...].astype(F32))
-
-
-def ocean_kernel(out_in, low_in, received, land, out, low, sems):
+    land[...] = raw[...].astype(F32)
+
+
+def ocean_kernel(comps, out_in, low_in, received, land, out, low, sems):
     fields, rows, cells = low.shape
-    copies = []
-    for k in range(fields):
-        for b in range(cells // LANES):
-            at = slice(b * LANES, (b + 1) * LANES)
-            low[k, 0:1, at] = low_in[k, 0:1, at] + land[:, at] * received[b, k : k + 1, :]
-        copies.append(pltpu.make_async_copy(low.at[k], out.at[0, 0, k, pl.ds(0, rows), :], sems.at[k]))
-        copies[-1].start()
-    for copy in copies:
-        copy.wait()
+
+    @pl.when(jnp.logical_not(atmosphere(comps)))
+    def _():
+        copies = []
+        for k in range(fields):
+            for b in range(cells // LANES):
+                at = slice(b * LANES, (b + 1) * LANES)
+                low[k, 0:1, at] = low_in[k, 0:1, at] + land[:, at] * received[b, k : k + 1, :]
+            copies.append(
+                pltpu.make_async_copy(low.at[k], out.at[0, 0, k, pl.ds(0, rows), :], sems.at[k])
+            )
+            copies[-1].start()
+        for copy in copies:
+            copy.wait()
 
 
 def call(body, out_shape, in_specs, out_specs, scratch, flops, aliases=None):
@@ -335,19 +358,17 @@
     )(*in_hbm(column_state, mixing, vertical))
     from_left = moved(to_right, "tile", 1)
     from_right = moved(to_left, "tile", -1)
-    low, high, buf, wide, coef, parts, flux = call(
+    field, buf, wide, coef, lean = call(
         functools.partial(interior_kernel, comps),
         (
-            f32(fields, ROWS, cells),
-            f32(fields, levels - ROWS, cells),
+            f32(fields, levels, cells),
             f32(spread, blocks, fields, LANES),
             f32(spread, blocks, EDGES, LANES),
             f32(3, fields, levels, LANES),
-            jax.ShapeDtypeStruct((2, levels, levels), BF16),
-            f32(2, fields, LANES),
+            f32(fields, levels, LANES),
         ),
         [VMEM] * 3 + [HBM] * 5,
-        [VMEM] * 7,
+        [VMEM] * 5,
         [
             pltpu.SMEM(flux_coef.shape, F32),
             pltpu.SMEM((margins,), jnp.int32),
@@ -355,7 +376,7 @@
             pltpu.SMEM((margins,), jnp.int32),
             pltpu.VMEM((fields, cells), F32),
             pltpu.VMEM((blocks, ROWS, LANES), F32),
-            pltpu.VMEM((EDGES, LANES), F32),
+            pltpu.VMEM((margins, EDGES, LANES), F32),
             pltpu.VMEM(remap_weights.shape[2:], BF16),
             pltpu.SemaphoreType.DMA((5,)),
         ],
@@ -369,35 +390,36 @@
             f32(blocks, fields, LANES),
             f32(fields, levels, LANES),
         ),
-        [VMEM] * 8,
+        [VMEM] * 7,
         [VMEM] * 4,
         [pltpu.VMEM((fields, LANES), F32)],
         10**6,
-    )(from_left, from_right, own, coef, parts, flux, buf, wide)
+    )(from_left, from_right, own, coef, lean, buf, wide)
     mine = mine + swapped(theirs, "comp", 1)
     for step in range(REACH, 0, -1):
         arrived = sideways(mine[step - 1], step)
         received = received + arrived
-    low, high, land, out = call(
+    low, land, out = call(
         functools.partial(finish_kernel, comps),
         (
             f32(fields, ROWS, cells),
-            f32(fields, levels - ROWS, cells),
             f32(1, cells),
             jax.ShapeDtypeStruct(column_state.shape, F32),
         ),
-        [VMEM] * 3 + [HBM],
-        [VMEM, VMEM, VMEM, HBM],
-        [pltpu.VMEM(ocean_mask.shape, jnp.int32), pltpu.SemaphoreType.DMA((fields + 1,))],
+        [VMEM] * 3 + [HBM] * 2,
+        [VMEM, VMEM, HBM],
+        [
+            pltpu.VMEM((fields, levels - ROWS, cells), F32),
+            pltpu.VMEM((fields, cells), F32),
+            pltpu.VMEM(ocean_mask.shape, jnp.int32),
+            pltpu.SMEM(flux_coef.shape, F32),
+            pltpu.SemaphoreType.DMA((2 * fields + 2,)),
+        ],
         10**7,
-        aliases={0: 0, 1: 1},
-    )(low, high, edge, *in_hbm(ocean_mask))
-    bit = 1
-    while bit < comps:
-        received = received + swapped(received, "comp", bit)
-        bit *= 2
+    )(field, edge, ver, *in_hbm(flux_coef, ocean_mask))
+    received = gathered(received)
     out, _ = call(
-        ocean_kernel,
+        functools.partial(ocean_kernel, comps),
         (jax.ShapeDtypeStruct(column_state.shape, F32), f32(fields, ROWS, cells)),
         [HBM, VMEM, VMEM, VMEM],
         [HBM, VMEM],

time: 25.7 us -> 25.3 us (0.984)
  waiting for transfers between devices: 7.71 us -> 6.92 us
  Pallas kernels: 5.13 us -> 5.49 us
    ppermute x3 -> x1, waiting for transfers between devices: 3.93 us -> 1.29 us  [swapped(): return lax.ppermute(value, axis, [(i, i ^ bit) for i in range(count)])]
    ppermute x0 -> x3, waiting for transfers between devices: none -> 1.84 us  [gathered(): arrived = lax.ppermute(value, 'comp', pairs)]
    ppermute x0 -> x3, starting transfers between devices: none -> 1.82 us  [gathered(): arrived = lax.ppermute(value, 'comp', pairs)]
    ppermute x3 -> x1, starting transfers between devices: 1.85 us -> 0.07 us  [swapped(): return lax.ppermute(value, axis, [(i, i ^ bit) for i in range(count)])]
    pallas_call x1, Pallas kernels: 0.81 us -> 2.04 us  [step(): call(functools.partial(finish_kernel, comps), (f32(fields, ROWS, cells),...]
    pallas_call x2, Pallas kernels: 2.81 us -> 2.05 us  [the longest x1 2 us: step(): call(functools.partial(interior_kernel, comps), (f32(fields, levels, cell...]
  transfers between devices with their start and end apart: 8 -> 9, of which waited for: 6 -> 5; matrix products, arithmetic and copies ran while one was open for 0% -> 0% of each run, Pallas kernels for 11% -> 16%
where the time goes in v4:
time: 25.3 us; the launch traced here: 25.1 us
  starting transfers between devices  12.5 us (49%)
  waiting for transfers between devices  6.92 us (27%)
  Pallas kernels  5.49 us (22%)
    ppermute x2, starting transfers between devices, moved(): lax.ppermute(value, axis, [(i, (i + steps) % count) for i in range(count)])  6.12 us
    ppermute x3, starting transfers between devices, sideways(): return lax.ppermute(value, ('comp', 'tile'), pairs)  4.52 us
    ppermute x3, waiting for transfers between devices, sideways(): return lax.ppermute(value, ('comp', 'tile'), pairs)  3.78 us
    pallas_call x1, Pallas kernels, step(): call(functools.partial(finish_kernel, comps), (f32(fields, ROWS, cells),...  2.04 us
    pallas_call x1, Pallas kernels, step(): call(functools.partial(interior_kernel, comps), (f32(fields, levels, cell...  2 us
    ppermute x3, waiting for transfers between devices, gathered(): arrived = lax.ppermute(value, 'comp', pairs)  1.84 us
    ppermute x3, starting transfers between devices, gathered(): arrived = lax.ppermute(value, 'comp', pairs)  1.82 us
    ppermute x1, waiting for transfers between devices, swapped(): return lax.ppermute(value, axis, [(i, i ^ bit) for i in range(count)])  1.29 us
  transfers between devices with their start and end apart: 9, of which 5 were waited for; matrix products, arithmetic and copies ran while one was open for 0% of the time, Pallas kernels for 16%

profile of v4, /device:TPU:0, one launch (start us, length us, event | category | flops | bytes accessed | tf_op | source)
XLA Modules:
  0.0 25.1 jit_solution(8566132447179595933)
XLA Ops:
  0.0 0.0 copy-start
  0.0 1.0 %shard_map.91 = (f32[4,16,128]{2,1,0:T(8,128)S(1)}, f32[8,128]{1,0:T(8,128)S(1)}, f32[8,128]{1,0:T(8,128)S(1)}, f32[4,16]{1,0:T(4,128)S(1)}, f32[16,16]{1,0:T(8,128)S(1)}) custom-call(f32[1,1,4,16,2048]{4,3,2,1,0:T(8,128)} %state.1, f32[2,4,16]{2,1,0:T(4,128)} %mixing.1, f32[2,16,16]{2,1,0:T(8,128)} %vertical.1), custom_call_target="tpu_custom_call" | custom-call | flops 100000 | bytes 12500 | tf_op jit(solution)/shard_map/pallas_call | solution.py:351
  1.0 3.0 %collective-permute-start = (f32[8,128]{1,0:T(8,128)S(1)}, f32[8,128]{1,0:T(8,128)S(1)}, u32[]{:S(2)}, u32[]{:S(2)}) collective-permute-start(f32[8,128]{1,0:T(8,128)S(1)} %get-tuple-element.26), channel_id=1, source_target_pairs={{0,1},{1,2},{2,3},{3,4},{4,5},{5,6},{6,7},{7,0},{8,9},{9,10},{10,1... | collective-permute-start | bytes 12296 | tf_op jit(solution)/shard_map/ppermute | solution.py:24
  4.0 3.1 %collective-permute-start.1 = (f32[8,128]{1,0:T(8,128)S(1)}, f32[8,128]{1,0:T(8,128)S(1)}, u32[]{:S(2)}, u32[]{:S(2)}) collective-permute-start(f32[8,128]{1,0:T(8,128)S(1)} %get-tuple-element.27), channel_id=1, source_target_pairs={{0,7},{1,0},{2,1},{3,2},{4,3},{5,4},{6,5},{7,6},{8,15},{9,8},{10,9... | collective-permute-start | bytes 12296 | tf_op jit(solution)/shard_map/ppermute | solution.py:24
  7.1 0.0 copy-done
  7.1 2.0 %shard_map.92 = (f32[4,16,2048]{2,1,0:T(8,128)S(1)}, f32[7,16,4,128]{3,2,1,0:T(4,128)S(1)}, f32[7,16,4,128]{3,2,1,0:T(4,128)S(1)}, f32[3,4,16,128]{3,2,1,0:T(8,128)S(1)}, f32[4,16,128]{2,1,0:T(8,128)S(1)}) custom-call(f32[4,16,2048]{2,1,0:T(8,128)S(1)} %bitcast.17, f32[4,16]{1,0:T(4,128)S(1)} %get-tuple-element.23.mix, f32[16,16]{1,0:T(8,128)S(1)} %get-tuple-element.24.ver, ...), custom_call_target="tpu_custom_call" | custom-call | flops 10000000 | bytes 1250000 | tf_op jit(solution)/shard_map/pallas_call | solution.py:361
  9.1 0.0 collective-permute-done.from_left
  9.1 0.0 collective-permute-done.1.from_right
  9.1 0.4 %shard_map.93 = (f32[3,16,4,128]{3,2,1,0:T(4,128)S(1)}, f32[3,16,4,128]{3,2,1,0:T(4,128)S(1)}, f32[16,4,128]{2,1,0:T(4,128)S(1)}, f32[4,16,128]{2,1,0:T(8,128)S(1)}) custom-call(f32[8,128]{1,0:T(8,128)S(1)} %collective-permute-done.from_left, f32[8,128]{1,0:T(8,128)S(1)} %collective-permute-done.1.from_right, f32[4,16,128]{2,1,0:T(8,128)S(1)} %get-tuple-element.28.own, ...), custom_call_target="tpu_custom_call" | custom-call | flops 1000000 | bytes 125000 | tf_op jit(solution)/shard_map/pallas_call | solution.py:385
  9.6 0.1 collective-permute-start.2
  9.6 1.3 %collective-permute-done.2 = f32[3,16,4,128]{3,2,1,0:T(4,128)S(1)} collective-permute-done((f32[3,16,4,128]{3,2,1,0:T(4,128)S(1)}, f32[3,16,4,128]{3,2,1,0:T(4,128)S(1)}, u32[]{:S(2)}, u32[]{:S(2)}) %collective-permute-start.2) | collective-permute-done | bytes 98336 | tf_op jit(solution)/shard_map/ppermute | solution.py:45
  11.0 3.0 %collective-permute-start.3 = (f32[16,4,128]{2,1,0:T(4,128)S(1)}, f32[16,4,128]{2,1,0:T(4,128)S(1)}, u32[]{:S(2)}, u32[]{:S(2)}) collective-permute-start(f32[16,4,128]{2,1,0:T(4,128)S(1)} %get-tuple-element.41), channel_id=1, source_target_pairs={{0,5},{1,6},{2,7},{3,0},{4,1},{5,2},{6,3},{7,4},{8,11},{9,12},{10,... | collective-permute-start | bytes 98312 | tf_op jit(solution)/shard_map/ppermute | solution.py:54
  14.0 1.4 %collective-permute-start.5 = (f32[16,4,128]{2,1,0:T(4,128)S(1)}, f32[16,4,128]{2,1,0:T(4,128)S(1)}, u32[]{:S(2)}, u32[]{:S(2)}) collective-permute-start(f32[16,4,128]{2,1,0:T(4,128)S(1)} %get-tuple-element.42), channel_id=1, source_target_pairs={{0,7},{1,0},{2,1},{3,2},{4,3},{5,4},{6,5},{7,6},{8,9},{9,10},{10,1... | collective-permute-start | bytes 98312 | tf_op jit(solution)/shard_map/ppermute | solution.py:54
  15.4 0.1 collective-permute-start.4
  15.5 0.6 %collective-permute-done.3 = f32[16,4,128]{2,1,0:T(4,128)S(1)} collective-permute-done((f32[16,4,128]{2,1,0:T(4,128)S(1)}, f32[16,4,128]{2,1,0:T(4,128)S(1)}, u32[]{:S(2)}, u32[]{:S(2)}) %collective-permute-start.3) | collective-permute-done | bytes 32800 | tf_op jit(solution)/shard_map/ppermute | solution.py:54
  16.1 1.8 %collective-permute-done.5 = f32[16,4,128]{2,1,0:T(4,128)S(1)} collective-permute-done((f32[16,4,128]{2,1,0:T(4,128)S(1)}, f32[16,4,128]{2,1,0:T(4,128)S(1)}, u32[]{:S(2)}, u32[]{:S(2)}) %collective-permute-start.5) | collective-permute-done | bytes 32800 | tf_op jit(solution)/shard_map/ppermute | solution.py:54
  17.9 1.4 %collective-permute-done.4 = f32[16,4,128]{2,1,0:T(4,128)S(1)} collective-permute-done((f32[16,4,128]{2,1,0:T(4,128)S(1)}, f32[16,4,128]{2,1,0:T(4,128)S(1)}, u32[]{:S(2)}, u32[]{:S(2)}) %collective-permute-start.4) | collective-permute-done | bytes 32800 | tf_op jit(solution)/shard_map/ppermute | solution.py:54
  19.3 0.1 collective-permute-start.8
  19.4 1.7 %collective-permute-start.7 = (f32[16,4,128]{2,1,0:T(4,128)S(1)}, f32[16,4,128]{2,1,0:T(4,128)S(1)}, u32[]{:S(2)}, u32[]{:S(2)}) collective-permute-start(f32[16,4,128]{2,1,0:T(4,128)S(1)} %bitcast.21), channel_id=1, source_target_pairs={{0,24},{24,16},{16,8},{8,0},{1,25},{25,17},{17,9},{9,1},{2,26},{26... | collective-permute-start | bytes 98312 | tf_op jit(solution)/shard_map/ppermute | solution.py:38
  21.1 0.0 collective-permute-start.6
  21.1 2.0 %shard_map.94 = (f32[4,8,2048]{2,1,0:T(8,128)S(1)}, f32[1,2048]{1,0:T(1,128)S(1)}, f32[1,1,4,16,2048]{4,3,2,1,0:T(8,128)}) custom-call(f32[4,16,2048]{2,1,0:T(8,128)S(1)} %get-tuple-element.25.field_in, f32[4,16,128]{2,1,0:T(8,128)S(1)} %get-tuple-element.33.edge, f32[16,16]{1,0:T(8,128)S(1)} %get-tuple-element.24.ver, f32[2,4]{1,0:T(2,128)} %flux.3, ...), custom_call_target="tpu_custom_call" | custom-call | flops 10000000 | bytes 1250000 | tf_op jit(solution)/shard_map/pallas_call | solution.py:402
  23.2 0.0 collective-permute-done.8
  23.2 0.0 collective-permute-done.7
  23.2 1.8 %collective-permute-done.6 = f32[16,4,128]{2,1,0:T(4,128)S(1)} collective-permute-done((f32[16,4,128]{2,1,0:T(4,128)S(1)}, f32[16,4,128]{2,1,0:T(4,128)S(1)}, u32[]{:S(2)}, u32[]{:S(2)}) %collective-permute-start.6) | collective-permute-done | bytes 32800 | tf_op jit(solution)/shard_map/ppermute | solution.py:38
  25.0 0.1 shard_map.95
  (4 shorter events, 0.1 us)
Async XLA Ops:
  0.0 7.1 %copy-start = (f32[1,1,4,16,2048]{4,3,2,1,0:T(8,128)S(1)}, f32[1,1,4,16,2048]{4,3,2,1,0:T(8,128)}, u32[]{:S(2)}) copy-start(f32[1,1,4,16,2048]{4,3,2,1,0:T(8,128)} %state.1) | copy-start | bytes 1572868
  1.0 8.1 %collective-permute-start = (f32[8,128]{1,0:T(8,128)S(1)}, f32[8,128]{1,0:T(8,128)S(1)}, u32[]{:S(2)}, u32[]{:S(2)}) collective-permute-start(f32[8,128]{1,0:T(8,128)S(1)} %get-tuple-element.26), channel_id=1, source_target_pairs={{0,1},{1,2},{2,3},{3,4},{4,5},{5,6},{6,7},{7,0},{8,9},{9,10},{10,1... | collective-permute-start | bytes 12296 | tf_op jit(solution)/shard_map/ppermute | solution.py:24
  4.0 5.1 %collective-permute-start.1 = (f32[8,128]{1,0:T(8,128)S(1)}, f32[8,128]{1,0:T(8,128)S(1)}, u32[]{:S(2)}, u32[]{:S(2)}) collective-permute-start(f32[8,128]{1,0:T(8,128)S(1)} %get-tuple-element.27), channel_id=1, source_target_pairs={{0,7},{1,0},{2,1},{3,2},{4,3},{5,4},{6,5},{7,6},{8,15},{9,8},{10,9... | collective-permute-start | bytes 12296 | tf_op jit(solution)/shard_map/ppermute | solution.py:24
  9.6 1.4 %collective-permute-start.2 = (f32[3,16,4,128]{3,2,1,0:T(4,128)S(1)}, f32[3,16,4,128]{3,2,1,0:T(4,128)S(1)}, u32[]{:S(2)}, u32[]{:S(2)}) collective-permute-start(f32[3,16,4,128]{3,2,1,0:T(4,128)S(1)} %get-tuple-element.38), channel_id=1, source_target_pairs={{0,8},{8,0},{16,24},{24,16},{1,9},{9,1},{17,25},{25,17},{2,10},{10... | collective-permute-start | bytes 294920 | tf_op jit(solution)/shard_map/ppermute | solution.py:45
  11.0 5.1 %collective-permute-start.3 = (f32[16,4,128]{2,1,0:T(4,128)S(1)}, f32[16,4,128]{2,1,0:T(4,128)S(1)}, u32[]{:S(2)}, u32[]{:S(2)}) collective-permute-start(f32[16,4,128]{2,1,0:T(4,128)S(1)} %get-tuple-element.41), channel_id=1, source_target_pairs={{0,5},{1,6},{2,7},{3,0},{4,1},{5,2},{6,3},{7,4},{8,11},{9,12},{10,... | collective-permute-start | bytes 98312 | tf_op jit(solution)/shard_map/ppermute | solution.py:54
  14.0 3.9 %collective-permute-start.5 = (f32[16,4,128]{2,1,0:T(4,128)S(1)}, f32[16,4,128]{2,1,0:T(4,128)S(1)}, u32[]{:S(2)}, u32[]{:S(2)}) collective-permute-start(f32[16,4,128]{2,1,0:T(4,128)S(1)} %get-tuple-element.42), channel_id=1, source_target_pairs={{0,7},{1,0},{2,1},{3,2},{4,3},{5,4},{6,5},{7,6},{8,9},{9,10},{10,1... | collective-permute-start | bytes 98312 | tf_op jit(solution)/shard_map/ppermute | solution.py:54
  15.4 3.9 %collective-permute-start.4 = (f32[16,4,128]{2,1,0:T(4,128)S(1)}, f32[16,4,128]{2,1,0:T(4,128)S(1)}, u32[]{:S(2)}, u32[]{:S(2)}) collective-permute-start(f32[16,4,128]{2,1,0:T(4,128)S(1)} %get-tuple-element.43), channel_id=1, source_target_pairs={{0,6},{1,7},{2,0},{3,1},{4,2},{5,3},{6,4},{7,5},{8,10},{9,11},{10,... | collective-permute-start | bytes 98312 | tf_op jit(solution)/shard_map/ppermute | solution.py:54
  19.3 3.9 %collective-permute-start.8 = (f32[16,4,128]{2,1,0:T(4,128)S(1)}, f32[16,4,128]{2,1,0:T(4,128)S(1)}, u32[]{:S(2)}, u32[]{:S(2)}) collective-permute-start(f32[16,4,128]{2,1,0:T(4,128)S(1)} %bitcast.20), channel_id=1, source_target_pairs={{0,8},{8,0},{16,24},{24,16},{1,9},{9,1},{17,25},{25,17},{2,10},{10... | collective-permute-start | bytes 98312 | tf_op jit(solution)/shard_map/ppermute | solution.py:38
  19.4 3.8 %collective-permute-start.7 = (f32[16,4,128]{2,1,0:T(4,128)S(1)}, f32[16,4,128]{2,1,0:T(4,128)S(1)}, u32[]{:S(2)}, u32[]{:S(2)}) collective-permute-start(f32[16,4,128]{2,1,0:T(4,128)S(1)} %bitcast.21), channel_id=1, source_target_pairs={{0,24},{24,16},{16,8},{8,0},{1,25},{25,17},{17,9},{9,1},{2,26},{26... | collective-permute-start | bytes 98312 | tf_op jit(solution)/shard_map/ppermute | solution.py:38
  21.1 3.9 %collective-permute-start.6 = (f32[16,4,128]{2,1,0:T(4,128)S(1)}, f32[16,4,128]{2,1,0:T(4,128)S(1)}, u32[]{:S(2)}, u32[]{:S(2)}) collective-permute-start(f32[16,4,128]{2,1,0:T(4,128)S(1)} %bitcast.22), channel_id=1, source_target_pairs={{8,24},{24,16},{16,0},{0,8},{9,25},{25,17},{17,1},{1,9},{10,26},{2... | collective-permute-start | bytes 98312 | tf_op jit(solution)/shard_map/ppermute | solution.py:38

commit v5 on v4

--- a/solution.py
+++ b/solution.py
@@ -9,6 +9,7 @@
 
 REACH = 3
 SUB = 2
+TURNS = ((2, 3, -1), (1, -3, -2))
 LANES = 128
 ROWS = 8
 MID = LANES // 2
@@ -28,7 +29,7 @@
     comps = lax.axis_size("comp")
     last = comps - 1
     if comps == 4:
-        cycles = [(1, last, 2, 0), (0, last, 2, 1)]
+        cycles = [(1, last, 0, 2), (0, last, 2, 1)]
         paths = [list(zip(c, c[1:] + c[:1])) for c in cycles]
         paths.append([(i, i ^ 1) for i in range(comps)])
     else:
@@ -45,11 +46,11 @@
     return lax.ppermute(value, axis, [(i, i ^ bit) for i in range(count)])
 
 
-def sideways(value, steps):
+def sideways(value, turn):
     comps, tiles = lax.axis_size("comp"), lax.axis_size("tile")
     pairs = []
     for c in range(comps):
-        shift = steps if c % 2 else -steps
+        shift = TURNS[c % 2][turn]
         pairs += [(c * tiles + t, c * tiles + (t + shift) % tiles) for t in range(tiles)]
     return lax.ppermute(value, ("comp", "tile"), pairs)
 
@@ -206,9 +207,11 @@
         block = jnp.clip(atm_s[n], 0, blocks - 1)
         place = jnp.clip(ocean_s[n], 0, blocks - 1)
         distance = jnp.clip(offset_s[n], 0, 2 * REACH) - REACH
-        ahead = jnp.where(distance > 0, 1, 0)
-        slot = jnp.abs(distance) - 1 + jnp.where(ahead == right_core, 0, REACH)
-        slot = jnp.where(distance == 0, 2 * REACH, slot)
+        slot = 2 * REACH
+        for core in range(2):
+            for turn in range(REACH):
+                spot = jnp.where(right_core == core, turn, REACH + turn)
+                slot = jnp.where(distance == TURNS[core][turn], spot, slot)
         term = jnp.dot(round_ref[block].astype(BF16), weights[n], preferred_element_type=F32)
         buf[slot, place] = buf[slot, place] + term[:fields]
         rim[n, :SUB, :] = weights[n, : 2 * ROWS, :].astype(F32)[:SUB]
@@ -396,8 +399,8 @@
         10**6,
     )(from_left, from_right, own, coef, lean, buf, wide)
     mine = mine + swapped(theirs, "comp", 1)
-    for step in range(REACH, 0, -1):
-        arrived = sideways(mine[step - 1], step)
+    for turn in range(REACH):
+        arrived = sideways(mine[turn], turn)
         received = received + arrived
     low, land, out = call(
         functools.partial(finish_kernel, comps),

time: 25.3 us -> 26.5 us (1.047)
  waiting for transfers between devices: 6.92 us -> 7.89 us
  starting transfers between devices: 12.5 us -> 12.8 us
    ppermute x3, waiting for transfers between devices: 3.78 us -> 5.71 us  [sideways(): return lax.ppermute(value, ('comp', 'tile'), pairs)]
    ppermute x3, waiting for transfers between devices: 1.84 us -> 0.89 us  [gathered(): arrived = lax.ppermute(value, 'comp', pairs)]
    ppermute x3, starting transfers between devices: 1.82 us -> 2.2 us  [gathered(): arrived = lax.ppermute(value, 'comp', pairs)]
  transfers between devices with their start and end apart: 9 -> 9, of which waited for: 5 -> 4; matrix products, arithmetic and copies ran while one was open for 0% -> 0% of each run, Pallas kernels for 16% -> 15%
where the time goes in v5:
time: 26.5 us; the launch traced here: 26.3 us
  starting transfers between devices  12.8 us (48%)
  waiting for transfers between devices  7.89 us (30%)
  Pallas kernels  5.51 us (21%)
    ppermute x2, starting transfers between devices, moved(): lax.ppermute(value, axis, [(i, (i + steps) % count) for i in range(count)])  6.12 us
    ppermute x3, waiting for transfers between devices, sideways(): return lax.ppermute(value, ('comp', 'tile'), pairs)  5.71 us
    ppermute x3, starting transfers between devices, sideways(): return lax.ppermute(value, ('comp', 'tile'), pairs)  4.37 us
    ppermute x3, starting transfers between devices, gathered(): arrived = lax.ppermute(value, 'comp', pairs)  2.2 us
    pallas_call x1, Pallas kernels, step(): call(functools.partial(finish_kernel, comps), (f32(fields, ROWS, cells),...  2.04 us
    pallas_call x1, Pallas kernels, step(): call(functools.partial(interior_kernel, comps), (f32(fields, levels, cell...  2.02 us
    ppermute x1, waiting for transfers between devices, swapped(): return lax.ppermute(value, axis, [(i, i ^ bit) for i in range(count)])  1.29 us
    pallas_call x1, Pallas kernels, step(): call(functools.partial(edges_kernel, comps), (f32(fields, levels, LANES),...  0.97 us
  transfers between devices with their start and end apart: 9, of which 4 were waited for; matrix products, arithmetic and copies ran while one was open for 0% of the time, Pallas kernels for 15%

profile of v5, /device:TPU:0, one launch (start us, length us, event | category | flops | bytes accessed | tf_op | source)
XLA Modules:
  0.0 26.3 jit_solution(5146737100204639710)
XLA Ops:
  0.0 0.0 copy-start
  0.0 1.0 %shard_map.91 = (f32[4,16,128]{2,1,0:T(8,128)S(1)}, f32[8,128]{1,0:T(8,128)S(1)}, f32[8,128]{1,0:T(8,128)S(1)}, f32[4,16]{1,0:T(4,128)S(1)}, f32[16,16]{1,0:T(8,128)S(1)}) custom-call(f32[1,1,4,16,2048]{4,3,2,1,0:T(8,128)} %state.1, f32[2,4,16]{2,1,0:T(4,128)} %mixing.1, f32[2,16,16]{2,1,0:T(8,128)} %vertical.1), custom_call_target="tpu_custom_call" | custom-call | flops 100000 | bytes 12500 | tf_op jit(solution)/shard_map/pallas_call | solution.py:354
  1.0 3.0 %collective-permute-start = (f32[8,128]{1,0:T(8,128)S(1)}, f32[8,128]{1,0:T(8,128)S(1)}, u32[]{:S(2)}, u32[]{:S(2)}) collective-permute-start(f32[8,128]{1,0:T(8,128)S(1)} %get-tuple-element.26), channel_id=1, source_target_pairs={{0,1},{1,2},{2,3},{3,4},{4,5},{5,6},{6,7},{7,0},{8,9},{9,10},{10,1... | collective-permute-start | bytes 12296 | tf_op jit(solution)/shard_map/ppermute | solution.py:25
  4.0 3.1 %collective-permute-start.1 = (f32[8,128]{1,0:T(8,128)S(1)}, f32[8,128]{1,0:T(8,128)S(1)}, u32[]{:S(2)}, u32[]{:S(2)}) collective-permute-start(f32[8,128]{1,0:T(8,128)S(1)} %get-tuple-element.27), channel_id=1, source_target_pairs={{0,7},{1,0},{2,1},{3,2},{4,3},{5,4},{6,5},{7,6},{8,15},{9,8},{10,9... | collective-permute-start | bytes 12296 | tf_op jit(solution)/shard_map/ppermute | solution.py:25
  7.1 0.0 copy-done
  7.1 2.0 %shard_map.92 = (f32[4,16,2048]{2,1,0:T(8,128)S(1)}, f32[7,16,4,128]{3,2,1,0:T(4,128)S(1)}, f32[7,16,4,128]{3,2,1,0:T(4,128)S(1)}, f32[3,4,16,128]{3,2,1,0:T(8,128)S(1)}, f32[4,16,128]{2,1,0:T(8,128)S(1)}) custom-call(f32[4,16,2048]{2,1,0:T(8,128)S(1)} %bitcast.17, f32[4,16]{1,0:T(4,128)S(1)} %get-tuple-element.23.mix, f32[16,16]{1,0:T(8,128)S(1)} %get-tuple-element.24.ver, ...), custom_call_target="tpu_custom_call" | custom-call | flops 10000000 | bytes 1250000 | tf_op jit(solution)/shard_map/pallas_call | solution.py:364
  9.1 0.0 collective-permute-done.from_left
  9.1 0.0 collective-permute-done.1.from_right
  9.2 0.4 %shard_map.93 = (f32[3,16,4,128]{3,2,1,0:T(4,128)S(1)}, f32[3,16,4,128]{3,2,1,0:T(4,128)S(1)}, f32[16,4,128]{2,1,0:T(4,128)S(1)}, f32[4,16,128]{2,1,0:T(8,128)S(1)}) custom-call(f32[8,128]{1,0:T(8,128)S(1)} %collective-permute-done.from_left, f32[8,128]{1,0:T(8,128)S(1)} %collective-permute-done.1.from_right, f32[4,16,128]{2,1,0:T(8,128)S(1)} %get-tuple-element.28.own, ...), custom_call_target="tpu_custom_call" | custom-call | flops 1000000 | bytes 125000 | tf_op jit(solution)/shard_map/pallas_call | solution.py:388
  9.6 0.1 collective-permute-start.2
  9.7 1.3 %collective-permute-done.2 = f32[3,16,4,128]{3,2,1,0:T(4,128)S(1)} collective-permute-done((f32[3,16,4,128]{3,2,1,0:T(4,128)S(1)}, f32[3,16,4,128]{3,2,1,0:T(4,128)S(1)}, u32[]{:S(2)}, u32[]{:S(2)}) %collective-permute-start.2) | collective-permute-done | bytes 98336 | tf_op jit(solution)/shard_map/ppermute | solution.py:46
  11.0 0.1 collective-permute-start.3
  11.1 4.3 %collective-permute-start.5 = (f32[16,4,128]{2,1,0:T(4,128)S(1)}, f32[16,4,128]{2,1,0:T(4,128)S(1)}, u32[]{:S(2)}, u32[]{:S(2)}) collective-permute-start(f32[16,4,128]{2,1,0:T(4,128)S(1)} %get-tuple-element.42), channel_id=1, source_target_pairs={{0,7},{1,0},{2,1},{3,2},{4,3},{5,4},{6,5},{7,6},{8,14},{9,15},{10,... | collective-permute-start | bytes 98312 | tf_op jit(solution)/shard_map/ppermute | solution.py:55
  15.4 0.0 collective-permute-start.4
  15.4 1.6 %collective-permute-done.3 = f32[16,4,128]{2,1,0:T(4,128)S(1)} collective-permute-done((f32[16,4,128]{2,1,0:T(4,128)S(1)}, f32[16,4,128]{2,1,0:T(4,128)S(1)}, u32[]{:S(2)}, u32[]{:S(2)}) %collective-permute-start.3) | collective-permute-done | bytes 32800 | tf_op jit(solution)/shard_map/ppermute | solution.py:55
  16.9 0.0 collective-permute-done.5
  17.0 4.1 %collective-permute-done.4 = f32[16,4,128]{2,1,0:T(4,128)S(1)} collective-permute-done((f32[16,4,128]{2,1,0:T(4,128)S(1)}, f32[16,4,128]{2,1,0:T(4,128)S(1)}, u32[]{:S(2)}, u32[]{:S(2)}) %collective-permute-start.4) | collective-permute-done | bytes 32800 | tf_op jit(solution)/shard_map/ppermute | solution.py:55
  21.1 0.1 collective-permute-start.8
  21.2 1.7 %collective-permute-start.7 = (f32[16,4,128]{2,1,0:T(4,128)S(1)}, f32[16,4,128]{2,1,0:T(4,128)S(1)}, u32[]{:S(2)}, u32[]{:S(2)}) collective-permute-start(f32[16,4,128]{2,1,0:T(4,128)S(1)} %bitcast.21), channel_id=1, source_target_pairs={{0,24},{24,16},{16,8},{8,0},{1,25},{25,17},{17,9},{9,1},{2,26},{26... | collective-permute-start | bytes 98312 | tf_op jit(solution)/shard_map/ppermute | solution.py:39
  22.9 0.4 %collective-permute-start.6 = (f32[16,4,128]{2,1,0:T(4,128)S(1)}, f32[16,4,128]{2,1,0:T(4,128)S(1)}, u32[]{:S(2)}, u32[]{:S(2)}) collective-permute-start(f32[16,4,128]{2,1,0:T(4,128)S(1)} %bitcast.22), channel_id=1, source_target_pairs={{8,24},{24,0},{0,16},{16,8},{9,25},{25,1},{1,17},{17,9},{10,26},{2... | collective-permute-start | bytes 98312 | tf_op jit(solution)/shard_map/ppermute | solution.py:39
  23.3 2.0 %shard_map.94 = (f32[4,8,2048]{2,1,0:T(8,128)S(1)}, f32[1,2048]{1,0:T(1,128)S(1)}, f32[1,1,4,16,2048]{4,3,2,1,0:T(8,128)}) custom-call(f32[4,16,2048]{2,1,0:T(8,128)S(1)} %get-tuple-element.25.field_in, f32[4,16,128]{2,1,0:T(8,128)S(1)} %get-tuple-element.33.edge, f32[16,16]{1,0:T(8,128)S(1)} %get-tuple-element.24.ver, f32[2,4]{1,0:T(2,128)} %flux.3, ...), custom_call_target="tpu_custom_call" | custom-call | flops 10000000 | bytes 1250000 | tf_op jit(solution)/shard_map/pallas_call | solution.py:405
  25.3 0.0 collective-permute-done.8
  25.4 0.0 collective-permute-done.7
  25.4 0.9 %collective-permute-done.6 = f32[16,4,128]{2,1,0:T(4,128)S(1)} collective-permute-done((f32[16,4,128]{2,1,0:T(4,128)S(1)}, f32[16,4,128]{2,1,0:T(4,128)S(1)}, u32[]{:S(2)}, u32[]{:S(2)}) %collective-permute-start.6) | collective-permute-done | bytes 32800 | tf_op jit(solution)/shard_map/ppermute | solution.py:39
  26.3 0.1 shard_map.95
  (4 shorter events, 0.1 us)
Async XLA Ops:
  0.0 7.1 %copy-start = (f32[1,1,4,16,2048]{4,3,2,1,0:T(8,128)S(1)}, f32[1,1,4,16,2048]{4,3,2,1,0:T(8,128)}, u32[]{:S(2)}) copy-start(f32[1,1,4,16,2048]{4,3,2,1,0:T(8,128)} %state.1) | copy-start | bytes 1572868
  1.0 8.2 %collective-permute-start = (f32[8,128]{1,0:T(8,128)S(1)}, f32[8,128]{1,0:T(8,128)S(1)}, u32[]{:S(2)}, u32[]{:S(2)}) collective-permute-start(f32[8,128]{1,0:T(8,128)S(1)} %get-tuple-element.26), channel_id=1, source_target_pairs={{0,1},{1,2},{2,3},{3,4},{4,5},{5,6},{6,7},{7,0},{8,9},{9,10},{10,1... | collective-permute-start | bytes 12296 | tf_op jit(solution)/shard_map/ppermute | solution.py:25
  4.0 5.2 %collective-permute-start.1 = (f32[8,128]{1,0:T(8,128)S(1)}, f32[8,128]{1,0:T(8,128)S(1)}, u32[]{:S(2)}, u32[]{:S(2)}) collective-permute-start(f32[8,128]{1,0:T(8,128)S(1)} %get-tuple-element.27), channel_id=1, source_target_pairs={{0,7},{1,0},{2,1},{3,2},{4,3},{5,4},{6,5},{7,6},{8,15},{9,8},{10,9... | collective-permute-start | bytes 12296 | tf_op jit(solution)/shard_map/ppermute | solution.py:25
  9.6 1.4 %collective-permute-start.2 = (f32[3,16,4,128]{3,2,1,0:T(4,128)S(1)}, f32[3,16,4,128]{3,2,1,0:T(4,128)S(1)}, u32[]{:S(2)}, u32[]{:S(2)}) collective-permute-start(f32[3,16,4,128]{3,2,1,0:T(4,128)S(1)} %get-tuple-element.38), channel_id=1, source_target_pairs={{0,8},{8,0},{16,24},{24,16},{1,9},{9,1},{17,25},{25,17},{2,10},{10... | collective-permute-start | bytes 294920 | tf_op jit(solution)/shard_map/ppermute | solution.py:46
  11.0 5.9 %collective-permute-start.3 = (f32[16,4,128]{2,1,0:T(4,128)S(1)}, f32[16,4,128]{2,1,0:T(4,128)S(1)}, u32[]{:S(2)}, u32[]{:S(2)}) collective-permute-start(f32[16,4,128]{2,1,0:T(4,128)S(1)} %get-tuple-element.41), channel_id=1, source_target_pairs={{0,2},{1,3},{2,4},{3,5},{4,6},{5,7},{6,0},{7,1},{8,9},{9,10},{10,1... | collective-permute-start | bytes 98312 | tf_op jit(solution)/shard_map/ppermute | solution.py:55
  11.1 5.9 %collective-permute-start.5 = (f32[16,4,128]{2,1,0:T(4,128)S(1)}, f32[16,4,128]{2,1,0:T(4,128)S(1)}, u32[]{:S(2)}, u32[]{:S(2)}) collective-permute-start(f32[16,4,128]{2,1,0:T(4,128)S(1)} %get-tuple-element.42), channel_id=1, source_target_pairs={{0,7},{1,0},{2,1},{3,2},{4,3},{5,4},{6,5},{7,6},{8,14},{9,15},{10,... | collective-permute-start | bytes 98312 | tf_op jit(solution)/shard_map/ppermute | solution.py:55
  15.4 5.7 %collective-permute-start.4 = (f32[16,4,128]{2,1,0:T(4,128)S(1)}, f32[16,4,128]{2,1,0:T(4,128)S(1)}, u32[]{:S(2)}, u32[]{:S(2)}) collective-permute-start(f32[16,4,128]{2,1,0:T(4,128)S(1)} %get-tuple-element.43), channel_id=1, source_target_pairs={{0,3},{1,4},{2,5},{3,6},{4,7},{5,0},{6,1},{7,2},{8,13},{9,14},{10,... | collective-permute-start | bytes 98312 | tf_op jit(solution)/shard_map/ppermute | solution.py:55
  21.1 4.3 %collective-permute-start.8 = (f32[16,4,128]{2,1,0:T(4,128)S(1)}, f32[16,4,128]{2,1,0:T(4,128)S(1)}, u32[]{:S(2)}, u32[]{:S(2)}) collective-permute-start(f32[16,4,128]{2,1,0:T(4,128)S(1)} %bitcast.20), channel_id=1, source_target_pairs={{0,8},{8,0},{16,24},{24,16},{1,9},{9,1},{17,25},{25,17},{2,10},{10... | collective-permute-start | bytes 98312 | tf_op jit(solution)/shard_map/ppermute | solution.py:39
  21.2 4.2 %collective-permute-start.7 = (f32[16,4,128]{2,1,0:T(4,128)S(1)}, f32[16,4,128]{2,1,0:T(4,128)S(1)}, u32[]{:S(2)}, u32[]{:S(2)}) collective-permute-start(f32[16,4,128]{2,1,0:T(4,128)S(1)} %bitcast.21), channel_id=1, source_target_pairs={{0,24},{24,16},{16,8},{8,0},{1,25},{25,17},{17,9},{9,1},{2,26},{26... | collective-permute-start | bytes 98312 | tf_op jit(solution)/shard_map/ppermute | solution.py:39
  22.9 3.3 %collective-permute-start.6 = (f32[16,4,128]{2,1,0:T(4,128)S(1)}, f32[16,4,128]{2,1,0:T(4,128)S(1)}, u32[]{:S(2)}, u32[]{:S(2)}) collective-permute-start(f32[16,4,128]{2,1,0:T(4,128)S(1)} %bitcast.22), channel_id=1, source_target_pairs={{8,24},{24,0},{0,16},{16,8},{9,25},{25,1},{1,17},{17,9},{10,26},{2... | collective-permute-start | bytes 98312 | tf_op jit(solution)/shard_map/ppermute | solution.py:39

commit v6 on v5

--- a/solution.py
+++ b/solution.py
@@ -222,7 +222,7 @@
 
 
 def rim_kernel(
-    comps, from_left, from_right, own, coef, lean, buf, wide, mine, theirs, here, edge, press
+    comps, from_left, from_right, own, coef, lean, buf, wide, theirs, edge, value, press
 ):
     fields, levels, _ = own.shape
     lane = lanes_of((ROWS, LANES))
@@ -240,20 +240,26 @@
             total = total + lean[k, h : h + ROWS, :] * field
             number += 1
         press[k : k + 1, :] = jnp.sum(total, axis=0, keepdims=True)
-    value = jnp.where(atmosphere(comps), jnp.tanh(press[...]), 0.0).astype(BF16).astype(F32)
+    surface = jnp.where(atmosphere(comps), jnp.tanh(press[...]), 0.0).astype(BF16).astype(F32)
+    value[...] = surface
+    added(surface, buf, wide, [(theirs, turn, REACH + turn) for turn in range(REACH)])
+
+
+def added(surface, buf, wide, moves):
+    fields, _ = surface.shape
     spots = [SUB + i for i in range(SUB)] + [MID + SUB + i for i in range(SUB)]
-    column = [jnp.broadcast_to(value[:, s : s + 1], (fields, LANES)) for s in spots]
-    for slot in range(buf.shape[0]):
+    column = [jnp.broadcast_to(surface[:, s : s + 1], (fields, LANES)) for s in spots]
+    for target, turn, slot in moves:
         for place in range(buf.shape[1]):
             total = buf[slot, place]
             for e in range(EDGES):
                 total = total + column[e] * wide[slot, place, e : e + 1, :]
-            if slot < REACH:
-                mine[slot, place] = total
-            elif slot < 2 * REACH:
-                theirs[slot - REACH, place] = total
-            else:
-                here[place] = total
+            target[turn, place] = total
+
+
+def mine_kernel(value, buf, wide, mine, here):
+    moves = [(mine, turn, turn) for turn in range(REACH)] + [(here, 0, 2 * REACH)]
+    added(value[...], buf, wide, moves)
 
 
 def finish_kernel(comps, field_in, edge, ver, flux, mask, low, land, out, high, press, raw, flux_s, sems):
@@ -297,8 +303,8 @@
     land[...] = raw[...].astype(F32)
 
 
-def ocean_kernel(comps, out_in, low_in, received, land, out, low, sems):
-    fields, rows, cells = low.shape
+def ocean_kernel(comps, out_in, low, received, land, out, row, sems):
+    fields, _, cells = low.shape
 
     @pl.when(jnp.logical_not(atmosphere(comps)))
     def _():
@@ -306,10 +312,8 @@
         for k in range(fields):
             for b in range(cells // LANES):
                 at = slice(b * LANES, (b + 1) * LANES)
-                low[k, 0:1, at] = low_in[k, 0:1, at] + land[:, at] * received[b, k : k + 1, :]
-            copies.append(
-                pltpu.make_async_copy(low.at[k], out.at[0, 0, k, pl.ds(0, rows), :], sems.at[k])
-            )
+                row[k, 0:1, at] = low[k, 0:1, at] + land[:, at] * received[b, k : k + 1, :]
+            copies.append(pltpu.make_async_copy(row.at[k], out.at[0, 0, k, pl.ds(0, 1), :], sems.at[k]))
             copies[-1].start()
         for copy in copies:
             copy.wait()
@@ -385,20 +389,25 @@
         ],
         10**7,
     )(column_state[0, 0], mix, ver, *in_hbm(remap_weights, flux_coef, atm_block, ocean_block, tile_offset))
-    mine, theirs, received, edge = call(
+    theirs, edge, value = call(
         functools.partial(rim_kernel, comps),
-        (
-            f32(REACH, blocks, fields, LANES),
-            f32(REACH, blocks, fields, LANES),
-            f32(blocks, fields, LANES),
-            f32(fields, levels, LANES),
-        ),
+        (f32(REACH, blocks, fields, LANES), f32(fields, levels, LANES), f32(fields, LANES)),
         [VMEM] * 7,
-        [VMEM] * 4,
+        [VMEM] * 3,
         [pltpu.VMEM((fields, LANES), F32)],
         10**6,
     )(from_left, from_right, own, coef, lean, buf, wide)
-    mine = mine + swapped(theirs, "comp", 1)
+    swap = swapped(theirs, "comp", 1)
+    mine, received = call(
+        mine_kernel,
+        (f32(REACH, blocks, fields, LANES), f32(1, blocks, fields, LANES)),
+        [VMEM] * 3,
+        [VMEM] * 2,
+        [],
+        10**6,
+    )(value, buf, wide)
+    mine = mine + swap
+    received = received[0]
     for turn in range(REACH):
         arrived = sideways(mine[turn], turn)
         received = received + arrived
@@ -421,16 +430,15 @@
         10**7,
     )(field, edge, ver, *in_hbm(flux_coef, ocean_mask))
     received = gathered(received)
-    out, _ = call(
+    return call(
         functools.partial(ocean_kernel, comps),
-        (jax.ShapeDtypeStruct(column_state.shape, F32), f32(fields, ROWS, cells)),
+        jax.ShapeDtypeStruct(column_state.shape, F32),
         [HBM, VMEM, VMEM, VMEM],
-        [HBM, VMEM],
-        [pltpu.SemaphoreType.DMA((fields,))],
+        HBM,
+        [pltpu.VMEM((fields, 1, cells), F32), pltpu.SemaphoreType.DMA((fields,))],
         10**6,
-        aliases={0: 0, 1: 1},
+        aliases={0: 0},
     )(out, low, received, land)
-    return out
 
 
 def solution(mesh):

time: 26.5 us -> 26.4 us (level)
  transfers between devices with their start and end apart: 9 -> 9, of which waited for: 4 -> 4; matrix products, arithmetic and copies ran while one was open for 0% -> 0% of each run, Pallas kernels for 15% -> 16%
where the time goes in v6:
time: 26.4 us; the launch traced here: 26.2 us
  starting transfers between devices  12.8 us (48%)
  waiting for transfers between devices  7.75 us (29%)
  Pallas kernels  5.56 us (21%)
    ppermute x2, starting transfers between devices, moved(): lax.ppermute(value, axis, [(i, (i + steps) % count) for i in range(count)])  6.12 us
    ppermute x3, waiting for transfers between devices, sideways(): return lax.ppermute(value, ('comp', 'tile'), pairs)  5.71 us
    ppermute x3, starting transfers between devices, sideways(): return lax.ppermute(value, ('comp', 'tile'), pairs)  4.37 us
    ppermute x3, starting transfers between devices, gathered(): arrived = lax.ppermute(value, 'comp', pairs)  2.2 us
    pallas_call x1, Pallas kernels, step(): call(functools.partial(finish_kernel, comps), (f32(fields, ROWS, cells),...  2.05 us
    pallas_call x1, Pallas kernels, step(): call(functools.partial(interior_kernel, comps), (f32(fields, levels, cell...  2.02 us
    ppermute x1, waiting for transfers between devices, swapped(): return lax.ppermute(value, axis, [(i, i ^ bit) for i in range(count)])  1.14 us
    pallas_call x1, Pallas kernels, step(): call(functools.partial(edges_kernel, comps), (f32(fields, levels, LANES),...  0.97 us
  transfers between devices with their start and end apart: 9, of which 4 were waited for; matrix products, arithmetic and copies ran while one was open for 0% of the time, Pallas kernels for 16%

profile of v6, /device:TPU:0, one launch (start us, length us, event | category | flops | bytes accessed | tf_op | source)
XLA Modules:
  0.0 26.2 jit_solution(873633694899936709)
XLA Ops:
  0.0 0.0 copy-start
  0.0 1.0 %shard_map.91 = (f32[4,16,128]{2,1,0:T(8,128)S(1)}, f32[8,128]{1,0:T(8,128)S(1)}, f32[8,128]{1,0:T(8,128)S(1)}, f32[4,16]{1,0:T(4,128)S(1)}, f32[16,16]{1,0:T(8,128)S(1)}) custom-call(f32[1,1,4,16,2048]{4,3,2,1,0:T(8,128)} %state.1, f32[2,4,16]{2,1,0:T(4,128)} %mixing.1, f32[2,16,16]{2,1,0:T(8,128)} %vertical.1), custom_call_target="tpu_custom_call" | custom-call | flops 100000 | bytes 12500 | tf_op jit(solution)/shard_map/pallas_call | solution.py:358
  1.0 3.0 %collective-permute-start = (f32[8,128]{1,0:T(8,128)S(1)}, f32[8,128]{1,0:T(8,128)S(1)}, u32[]{:S(2)}, u32[]{:S(2)}) collective-permute-start(f32[8,128]{1,0:T(8,128)S(1)} %get-tuple-element.26), channel_id=1, source_target_pairs={{0,1},{1,2},{2,3},{3,4},{4,5},{5,6},{6,7},{7,0},{8,9},{9,10},{10,1... | collective-permute-start | bytes 12296 | tf_op jit(solution)/shard_map/ppermute | solution.py:25
  4.0 3.1 %collective-permute-start.1 = (f32[8,128]{1,0:T(8,128)S(1)}, f32[8,128]{1,0:T(8,128)S(1)}, u32[]{:S(2)}, u32[]{:S(2)}) collective-permute-start(f32[8,128]{1,0:T(8,128)S(1)} %get-tuple-element.27), channel_id=1, source_target_pairs={{0,7},{1,0},{2,1},{3,2},{4,3},{5,4},{6,5},{7,6},{8,15},{9,8},{10,9... | collective-permute-start | bytes 12296 | tf_op jit(solution)/shard_map/ppermute | solution.py:25
  7.1 0.0 copy-done
  7.1 2.0 %shard_map.92 = (f32[4,16,2048]{2,1,0:T(8,128)S(1)}, f32[7,16,4,128]{3,2,1,0:T(4,128)S(1)}, f32[7,16,4,128]{3,2,1,0:T(4,128)S(1)}, f32[3,4,16,128]{3,2,1,0:T(8,128)S(1)}, f32[4,16,128]{2,1,0:T(8,128)S(1)}) custom-call(f32[4,16,2048]{2,1,0:T(8,128)S(1)} %bitcast.18, f32[4,16]{1,0:T(4,128)S(1)} %get-tuple-element.23.mix, f32[16,16]{1,0:T(8,128)S(1)} %get-tuple-element.24.ver, ...), custom_call_target="tpu_custom_call" | custom-call | flops 10000000 | bytes 1250000 | tf_op jit(solution)/shard_map/pallas_call | solution.py:368
  9.1 0.0 collective-permute-done.from_left
  9.1 0.0 collective-permute-done.1.from_right
  9.2 0.3 %shard_map.93 = (f32[3,16,4,128]{3,2,1,0:T(4,128)S(1)}, f32[4,16,128]{2,1,0:T(8,128)S(1)}, f32[4,128]{1,0:T(4,128)S(1)}) custom-call(f32[8,128]{1,0:T(8,128)S(1)} %collective-permute-done.from_left, f32[8,128]{1,0:T(8,128)S(1)} %collective-permute-done.1.from_right, f32[4,16,128]{2,1,0:T(8,128)S(1)} %get-tuple-element.28.own, ...), custom_call_target="tpu_custom_call" | custom-call | flops 1000000 | bytes 125000 | tf_op jit(solution)/shard_map/pallas_call | solution.py:392
  9.5 0.1 collective-permute-start.2
  9.6 0.1 shard_map.95
  9.7 1.1 %collective-permute-done.2 = f32[3,16,4,128]{3,2,1,0:T(4,128)S(1)} collective-permute-done((f32[3,16,4,128]{3,2,1,0:T(4,128)S(1)}, f32[3,16,4,128]{3,2,1,0:T(4,128)S(1)}, u32[]{:S(2)}, u32[]{:S(2)}) %collective-permute-start.2) | collective-permute-done | bytes 98336 | tf_op jit(solution)/shard_map/ppermute | solution.py:46
  10.9 0.1 collective-permute-start.3
  11.0 4.3 %collective-permute-start.5 = (f32[16,4,128]{2,1,0:T(4,128)S(1)}, f32[16,4,128]{2,1,0:T(4,128)S(1)}, u32[]{:S(2)}, u32[]{:S(2)}) collective-permute-start(f32[16,4,128]{2,1,0:T(4,128)S(1)} %get-tuple-element.42), channel_id=1, source_target_pairs={{0,7},{1,0},{2,1},{3,2},{4,3},{5,4},{6,5},{7,6},{8,14},{9,15},{10,... | collective-permute-start | bytes 98312 | tf_op jit(solution)/shard_map/ppermute | solution.py:55
  15.3 0.0 collective-permute-start.4
  15.3 1.6 %collective-permute-done.3 = f32[16,4,128]{2,1,0:T(4,128)S(1)} collective-permute-done((f32[16,4,128]{2,1,0:T(4,128)S(1)}, f32[16,4,128]{2,1,0:T(4,128)S(1)}, u32[]{:S(2)}, u32[]{:S(2)}) %collective-permute-start.3) | collective-permute-done | bytes 32800 | tf_op jit(solution)/shard_map/ppermute | solution.py:55
  16.8 0.0 collective-permute-done.5
  16.9 4.1 %collective-permute-done.4 = f32[16,4,128]{2,1,0:T(4,128)S(1)} collective-permute-done((f32[16,4,128]{2,1,0:T(4,128)S(1)}, f32[16,4,128]{2,1,0:T(4,128)S(1)}, u32[]{:S(2)}, u32[]{:S(2)}) %collective-permute-start.4) | collective-permute-done | bytes 32800 | tf_op jit(solution)/shard_map/ppermute | solution.py:55
  21.0 0.1 collective-permute-start.8
  21.1 1.7 %collective-permute-start.7 = (f32[16,4,128]{2,1,0:T(4,128)S(1)}, f32[16,4,128]{2,1,0:T(4,128)S(1)}, u32[]{:S(2)}, u32[]{:S(2)}) collective-permute-start(f32[16,4,128]{2,1,0:T(4,128)S(1)} %fusion.1), channel_id=1, source_target_pairs={{0,24},{24,16},{16,8},{8,0},{1,25},{25,17},{17,9},{9,1},{2,26},{26... | collective-permute-start | bytes 98312 | tf_op jit(solution)/shard_map/ppermute | solution.py:39
  22.8 0.4 %collective-permute-start.6 = (f32[16,4,128]{2,1,0:T(4,128)S(1)}, f32[16,4,128]{2,1,0:T(4,128)S(1)}, u32[]{:S(2)}, u32[]{:S(2)}) collective-permute-start(f32[16,4,128]{2,1,0:T(4,128)S(1)} %fusion.1), channel_id=1, source_target_pairs={{8,24},{24,0},{0,16},{16,8},{9,25},{25,1},{1,17},{17,9},{10,26},{2... | collective-permute-start | bytes 98312 | tf_op jit(solution)/shard_map/ppermute | solution.py:39
  23.2 2.0 %shard_map.94 = (f32[4,8,2048]{2,1,0:T(8,128)S(1)}, f32[1,2048]{1,0:T(1,128)S(1)}, f32[1,1,4,16,2048]{4,3,2,1,0:T(8,128)}) custom-call(f32[4,16,2048]{2,1,0:T(8,128)S(1)} %get-tuple-element.25.field_in, f32[4,16,128]{2,1,0:T(8,128)S(1)} %get-tuple-element.33.edge, f32[16,16]{1,0:T(8,128)S(1)} %get-tuple-element.24.ver, f32[2,4]{1,0:T(2,128)} %flux.3, ...), custom_call_target="tpu_custom_call" | custom-call | flops 10000000 | bytes 1250000 | tf_op jit(solution)/shard_map/pallas_call | solution.py:414
  25.3 0.0 collective-permute-done.8
  25.3 0.0 collective-permute-done.7
  25.3 0.9 %collective-permute-done.6 = f32[16,4,128]{2,1,0:T(4,128)S(1)} collective-permute-done((f32[16,4,128]{2,1,0:T(4,128)S(1)}, f32[16,4,128]{2,1,0:T(4,128)S(1)}, u32[]{:S(2)}, u32[]{:S(2)}) %collective-permute-start.6) | collective-permute-done | bytes 32800 | tf_op jit(solution)/shard_map/ppermute | solution.py:39
  26.2 0.1 shard_map.96
  (4 shorter events, 0.1 us)
Async XLA Ops:
  0.0 7.1 %copy-start = (f32[1,1,4,16,2048]{4,3,2,1,0:T(8,128)S(1)}, f32[1,1,4,16,2048]{4,3,2,1,0:T(8,128)}, u32[]{:S(2)}) copy-start(f32[1,1,4,16,2048]{4,3,2,1,0:T(8,128)} %state.1) | copy-start | bytes 1572868
  1.0 8.2 %collective-permute-start = (f32[8,128]{1,0:T(8,128)S(1)}, f32[8,128]{1,0:T(8,128)S(1)}, u32[]{:S(2)}, u32[]{:S(2)}) collective-permute-start(f32[8,128]{1,0:T(8,128)S(1)} %get-tuple-element.26), channel_id=1, source_target_pairs={{0,1},{1,2},{2,3},{3,4},{4,5},{5,6},{6,7},{7,0},{8,9},{9,10},{10,1... | collective-permute-start | bytes 12296 | tf_op jit(solution)/shard_map/ppermute | solution.py:25
  4.0 5.2 %collective-permute-start.1 = (f32[8,128]{1,0:T(8,128)S(1)}, f32[8,128]{1,0:T(8,128)S(1)}, u32[]{:S(2)}, u32[]{:S(2)}) collective-permute-start(f32[8,128]{1,0:T(8,128)S(1)} %get-tuple-element.27), channel_id=1, source_target_pairs={{0,7},{1,0},{2,1},{3,2},{4,3},{5,4},{6,5},{7,6},{8,15},{9,8},{10,9... | collective-permute-start | bytes 12296 | tf_op jit(solution)/shard_map/ppermute | solution.py:25
  9.5 1.4 %collective-permute-start.2 = (f32[3,16,4,128]{3,2,1,0:T(4,128)S(1)}, f32[3,16,4,128]{3,2,1,0:T(4,128)S(1)}, u32[]{:S(2)}, u32[]{:S(2)}) collective-permute-start(f32[3,16,4,128]{3,2,1,0:T(4,128)S(1)} %get-tuple-element.39), channel_id=1, source_target_pairs={{0,8},{8,0},{16,24},{24,16},{1,9},{9,1},{17,25},{25,17},{2,10},{10... | collective-permute-start | bytes 294920 | tf_op jit(solution)/shard_map/ppermute | solution.py:46
  10.9 5.9 %collective-permute-start.3 = (f32[16,4,128]{2,1,0:T(4,128)S(1)}, f32[16,4,128]{2,1,0:T(4,128)S(1)}, u32[]{:S(2)}, u32[]{:S(2)}) collective-permute-start(f32[16,4,128]{2,1,0:T(4,128)S(1)} %get-tuple-element.41), channel_id=1, source_target_pairs={{0,2},{1,3},{2,4},{3,5},{4,6},{5,7},{6,0},{7,1},{8,9},{9,10},{10,1... | collective-permute-start | bytes 98312 | tf_op jit(solution)/shard_map/ppermute | solution.py:55
  11.0 5.9 %collective-permute-start.5 = (f32[16,4,128]{2,1,0:T(4,128)S(1)}, f32[16,4,128]{2,1,0:T(4,128)S(1)}, u32[]{:S(2)}, u32[]{:S(2)}) collective-permute-start(f32[16,4,128]{2,1,0:T(4,128)S(1)} %get-tuple-element.42), channel_id=1, source_target_pairs={{0,7},{1,0},{2,1},{3,2},{4,3},{5,4},{6,5},{7,6},{8,14},{9,15},{10,... | collective-permute-start | bytes 98312 | tf_op jit(solution)/shard_map/ppermute | solution.py:55
  15.3 5.7 %collective-permute-start.4 = (f32[16,4,128]{2,1,0:T(4,128)S(1)}, f32[16,4,128]{2,1,0:T(4,128)S(1)}, u32[]{:S(2)}, u32[]{:S(2)}) collective-permute-start(f32[16,4,128]{2,1,0:T(4,128)S(1)} %get-tuple-element.43), channel_id=1, source_target_pairs={{0,3},{1,4},{2,5},{3,6},{4,7},{5,0},{6,1},{7,2},{8,13},{9,14},{10,... | collective-permute-start | bytes 98312 | tf_op jit(solution)/shard_map/ppermute | solution.py:55
  21.0 4.3 %collective-permute-start.8 = (f32[16,4,128]{2,1,0:T(4,128)S(1)}, f32[16,4,128]{2,1,0:T(4,128)S(1)}, u32[]{:S(2)}, u32[]{:S(2)}) collective-permute-start(f32[16,4,128]{2,1,0:T(4,128)S(1)} %fusion.1), channel_id=1, source_target_pairs={{0,8},{8,0},{16,24},{24,16},{1,9},{9,1},{17,25},{25,17},{2,10},{10... | collective-permute-start | bytes 98312 | tf_op jit(solution)/shard_map/ppermute | solution.py:39
  21.1 4.2 %collective-permute-start.7 = (f32[16,4,128]{2,1,0:T(4,128)S(1)}, f32[16,4,128]{2,1,0:T(4,128)S(1)}, u32[]{:S(2)}, u32[]{:S(2)}) collective-permute-start(f32[16,4,128]{2,1,0:T(4,128)S(1)} %fusion.1), channel_id=1, source_target_pairs={{0,24},{24,16},{16,8},{8,0},{1,25},{25,17},{17,9},{9,1},{2,26},{26... | collective-permute-start | bytes 98312 | tf_op jit(solution)/shard_map/ppermute | solution.py:39
  22.8 3.3 %collective-permute-start.6 = (f32[16,4,128]{2,1,0:T(4,128)S(1)}, f32[16,4,128]{2,1,0:T(4,128)S(1)}, u32[]{:S(2)}, u32[]{:S(2)}) collective-permute-start(f32[16,4,128]{2,1,0:T(4,128)S(1)} %fusion.1), channel_id=1, source_target_pairs={{8,24},{24,0},{0,16},{16,8},{9,25},{25,1},{1,17},{17,9},{10,26},{2... | collective-permute-start | bytes 98312 | tf_op jit(solution)/shard_map/ppermute | solution.py:39

commit v7 on v6

--- a/solution.py
+++ b/solution.py
@@ -9,7 +9,7 @@
 
 REACH = 3
 SUB = 2
-TURNS = ((2, 3, -1), (1, -3, -2))
+TURNS = ((('R', 2), ('R', 1), ('R', -1)), (('A', 3), ('B', 3), ('R', -2)))
 LANES = 128
 ROWS = 8
 MID = LANES // 2
@@ -46,12 +46,22 @@
     return lax.ppermute(value, axis, [(i, i ^ bit) for i in range(count)])
 
 
+def displaced(kind, distance, tile):
+    if kind == "R":
+        return distance
+    step = distance & -distance
+    flip = (tile // step) % 2
+    sign = 1 - 2 * flip if kind == "A" else 2 * flip - 1
+    return sign * distance
+
+
 def sideways(value, turn):
     comps, tiles = lax.axis_size("comp"), lax.axis_size("tile")
     pairs = []
     for c in range(comps):
-        shift = TURNS[c % 2][turn]
-        pairs += [(c * tiles + t, c * tiles + (t + shift) % tiles) for t in range(tiles)]
+        turns = [displaced(*TURNS[c % 2][turn], t) for t in range(tiles)]
+        pairs += [(c * tiles + t, c * tiles + (t + turns[t]) % tiles) for t in range(tiles)]
+    assert len({target for _, target in pairs}) == len(pairs)
     return lax.ppermute(value, ("comp", "tile"), pairs)
 
 
@@ -170,6 +180,7 @@
         copy.start()
     is_atmos = atmosphere(comps)
     right_core = lax.axis_index("comp") % 2
+    tile = lax.axis_index("tile")
     buf[...] = jnp.zeros_like(buf)
     wide[...] = jnp.zeros_like(wide)
     square = (levels, levels)
@@ -211,7 +222,7 @@
         for core in range(2):
             for turn in range(REACH):
                 spot = jnp.where(right_core == core, turn, REACH + turn)
-                slot = jnp.where(distance == TURNS[core][turn], spot, slot)
+                slot = jnp.where(distance == displaced(*TURNS[core][turn], tile), spot, slot)
         term = jnp.dot(round_ref[block].astype(BF16), weights[n], preferred_element_type=F32)
         buf[slot, place] = buf[slot, place] + term[:fields]
         rim[n, :SUB, :] = weights[n, : 2 * ROWS, :].astype(F32)[:SUB]

time: 26.4 us -> 27.3 us (1.034)
  waiting for transfers between devices: 7.75 us -> 8.65 us
    ppermute x3, waiting for transfers between devices: 5.71 us -> 6.61 us  [sideways(): return lax.ppermute(value, ('comp', 'tile'), pairs)]
  transfers between devices with their start and end apart: 9 -> 9, of which waited for: 4 -> 5; matrix products, arithmetic and copies ran while one was open for 0% -> 0% of each run, Pallas kernels for 16% -> 15%
where the time goes in v7:
time: 27.3 us; the launch traced here: 27.1 us
  starting transfers between devices  12.8 us (47%)
  waiting for transfers between devices  8.65 us (32%)
  Pallas kernels  5.5 us (20%)
    ppermute x3, waiting for transfers between devices, sideways(): return lax.ppermute(value, ('comp', 'tile'), pairs)  6.61 us
    ppermute x2, starting transfers between devices, moved(): lax.ppermute(value, axis, [(i, (i + steps) % count) for i in range(count)])  6.12 us
    ppermute x3, starting transfers between devices, sideways(): return lax.ppermute(value, ('comp', 'tile'), pairs)  4.42 us
    ppermute x3, starting transfers between devices, gathered(): arrived = lax.ppermute(value, 'comp', pairs)  2.2 us
    pallas_call x1, Pallas kernels, step(): call(functools.partial(finish_kernel, comps), (f32(fields, ROWS, cells),...  2.04 us
    pallas_call x1, Pallas kernels, step(): call(functools.partial(interior_kernel, comps), (f32(fields, levels, cell...  1.97 us
    ppermute x1, waiting for transfers between devices, swapped(): return lax.ppermute(value, axis, [(i, i ^ bit) for i in range(count)])  1.14 us
    pallas_call x1, Pallas kernels, step(): call(functools.partial(edges_kernel, comps), (f32(fields, levels, LANES),...  0.97 us
  transfers between devices with their start and end apart: 9, of which 5 were waited for; matrix products, arithmetic and copies ran while one was open for 0% of the time, Pallas kernels for 15%

profile of v7, /device:TPU:0, one launch (start us, length us, event | category | flops | bytes accessed | tf_op | source)
XLA Modules:
  0.0 27.1 jit_solution(12788753480368071510)
XLA Ops:
  0.0 0.0 copy-start
  0.0 1.0 %shard_map.91 = (f32[4,16,128]{2,1,0:T(8,128)S(1)}, f32[8,128]{1,0:T(8,128)S(1)}, f32[8,128]{1,0:T(8,128)S(1)}, f32[4,16]{1,0:T(4,128)S(1)}, f32[16,16]{1,0:T(8,128)S(1)}) custom-call(f32[1,1,4,16,2048]{4,3,2,1,0:T(8,128)} %state.1, f32[2,4,16]{2,1,0:T(4,128)} %mixing.1, f32[2,16,16]{2,1,0:T(8,128)} %vertical.1), custom_call_target="tpu_custom_call" | custom-call | flops 100000 | bytes 12500 | tf_op jit(solution)/shard_map/pallas_call | solution.py:369
  1.0 3.0 %collective-permute-start = (f32[8,128]{1,0:T(8,128)S(1)}, f32[8,128]{1,0:T(8,128)S(1)}, u32[]{:S(2)}, u32[]{:S(2)}) collective-permute-start(f32[8,128]{1,0:T(8,128)S(1)} %get-tuple-element.26), channel_id=1, source_target_pairs={{0,1},{1,2},{2,3},{3,4},{4,5},{5,6},{6,7},{7,0},{8,9},{9,10},{10,1... | collective-permute-start | bytes 12296 | tf_op jit(solution)/shard_map/ppermute | solution.py:25
  4.0 3.1 %collective-permute-start.1 = (f32[8,128]{1,0:T(8,128)S(1)}, f32[8,128]{1,0:T(8,128)S(1)}, u32[]{:S(2)}, u32[]{:S(2)}) collective-permute-start(f32[8,128]{1,0:T(8,128)S(1)} %get-tuple-element.27), channel_id=1, source_target_pairs={{0,7},{1,0},{2,1},{3,2},{4,3},{5,4},{6,5},{7,6},{8,15},{9,8},{10,9... | collective-permute-start | bytes 12296 | tf_op jit(solution)/shard_map/ppermute | solution.py:25
  7.1 0.0 copy-done
  7.1 2.0 %shard_map.92 = (f32[4,16,2048]{2,1,0:T(8,128)S(1)}, f32[7,16,4,128]{3,2,1,0:T(4,128)S(1)}, f32[7,16,4,128]{3,2,1,0:T(4,128)S(1)}, f32[3,4,16,128]{3,2,1,0:T(8,128)S(1)}, f32[4,16,128]{2,1,0:T(8,128)S(1)}) custom-call(f32[4,16,2048]{2,1,0:T(8,128)S(1)} %bitcast.18, f32[4,16]{1,0:T(4,128)S(1)} %get-tuple-element.23.mix, f32[16,16]{1,0:T(8,128)S(1)} %get-tuple-element.24.ver, ...), custom_call_target="tpu_custom_call" | custom-call | flops 10000000 | bytes 1250000 | tf_op jit(solution)/shard_map/pallas_call | solution.py:379
  9.1 0.0 collective-permute-done.from_left
  9.1 0.0 collective-permute-done.1.from_right
  9.1 0.3 %shard_map.93 = (f32[3,16,4,128]{3,2,1,0:T(4,128)S(1)}, f32[4,16,128]{2,1,0:T(8,128)S(1)}, f32[4,128]{1,0:T(4,128)S(1)}) custom-call(f32[8,128]{1,0:T(8,128)S(1)} %collective-permute-done.from_left, f32[8,128]{1,0:T(8,128)S(1)} %collective-permute-done.1.from_right, f32[4,16,128]{2,1,0:T(8,128)S(1)} %get-tuple-element.28.own, ...), custom_call_target="tpu_custom_call" | custom-call | flops 1000000 | bytes 125000 | tf_op jit(solution)/shard_map/pallas_call | solution.py:403
  9.4 0.1 collective-permute-start.2
  9.5 0.1 shard_map.95
  9.7 1.1 %collective-permute-done.2 = f32[3,16,4,128]{3,2,1,0:T(4,128)S(1)} collective-permute-done((f32[3,16,4,128]{3,2,1,0:T(4,128)S(1)}, f32[3,16,4,128]{3,2,1,0:T(4,128)S(1)}, u32[]{:S(2)}, u32[]{:S(2)}) %collective-permute-start.2) | collective-permute-done | bytes 98336 | tf_op jit(solution)/shard_map/ppermute | solution.py:46
  10.9 0.1 collective-permute-start.3
  11.0 4.3 %collective-permute-start.5 = (f32[16,4,128]{2,1,0:T(4,128)S(1)}, f32[16,4,128]{2,1,0:T(4,128)S(1)}, u32[]{:S(2)}, u32[]{:S(2)}) collective-permute-start(f32[16,4,128]{2,1,0:T(4,128)S(1)} %get-tuple-element.42), channel_id=1, source_target_pairs={{0,7},{1,0},{2,1},{3,2},{4,3},{5,4},{6,5},{7,6},{8,14},{9,15},{10,... | collective-permute-start | bytes 98312 | tf_op jit(solution)/shard_map/ppermute | solution.py:65
  15.3 0.0 collective-permute-start.4
  15.3 1.4 %collective-permute-done.3 = f32[16,4,128]{2,1,0:T(4,128)S(1)} collective-permute-done((f32[16,4,128]{2,1,0:T(4,128)S(1)}, f32[16,4,128]{2,1,0:T(4,128)S(1)}, u32[]{:S(2)}, u32[]{:S(2)}) %collective-permute-start.3) | collective-permute-done | bytes 32800 | tf_op jit(solution)/shard_map/ppermute | solution.py:65
  16.6 0.2 collective-permute-done.5
  16.9 5.0 %collective-permute-done.4 = f32[16,4,128]{2,1,0:T(4,128)S(1)} collective-permute-done((f32[16,4,128]{2,1,0:T(4,128)S(1)}, f32[16,4,128]{2,1,0:T(4,128)S(1)}, u32[]{:S(2)}, u32[]{:S(2)}) %collective-permute-start.4) | collective-permute-done | bytes 32800 | tf_op jit(solution)/shard_map/ppermute | solution.py:65
  21.9 0.1 collective-permute-start.8
  22.0 1.7 %collective-permute-start.7 = (f32[16,4,128]{2,1,0:T(4,128)S(1)}, f32[16,4,128]{2,1,0:T(4,128)S(1)}, u32[]{:S(2)}, u32[]{:S(2)}) collective-permute-start(f32[16,4,128]{2,1,0:T(4,128)S(1)} %fusion.1), channel_id=1, source_target_pairs={{0,24},{24,16},{16,8},{8,0},{1,25},{25,17},{17,9},{9,1},{2,26},{26... | collective-permute-start | bytes 98312 | tf_op jit(solution)/shard_map/ppermute | solution.py:39
  23.7 0.4 %collective-permute-start.6 = (f32[16,4,128]{2,1,0:T(4,128)S(1)}, f32[16,4,128]{2,1,0:T(4,128)S(1)}, u32[]{:S(2)}, u32[]{:S(2)}) collective-permute-start(f32[16,4,128]{2,1,0:T(4,128)S(1)} %fusion.1), channel_id=1, source_target_pairs={{8,24},{24,0},{0,16},{16,8},{9,25},{25,1},{1,17},{17,9},{10,26},{2... | collective-permute-start | bytes 98312 | tf_op jit(solution)/shard_map/ppermute | solution.py:39
  24.1 2.0 %shard_map.94 = (f32[4,8,2048]{2,1,0:T(8,128)S(1)}, f32[1,2048]{1,0:T(1,128)S(1)}, f32[1,1,4,16,2048]{4,3,2,1,0:T(8,128)}) custom-call(f32[4,16,2048]{2,1,0:T(8,128)S(1)} %get-tuple-element.25.field_in, f32[4,16,128]{2,1,0:T(8,128)S(1)} %get-tuple-element.33.edge, f32[16,16]{1,0:T(8,128)S(1)} %get-tuple-element.24.ver, f32[2,4]{1,0:T(2,128)} %flux.3, ...), custom_call_target="tpu_custom_call" | custom-call | flops 10000000 | bytes 1250000 | tf_op jit(solution)/shard_map/pallas_call | solution.py:425
  26.2 0.0 collective-permute-done.8
  26.2 0.0 collective-permute-done.7
  26.2 0.9 %collective-permute-done.6 = f32[16,4,128]{2,1,0:T(4,128)S(1)} collective-permute-done((f32[16,4,128]{2,1,0:T(4,128)S(1)}, f32[16,4,128]{2,1,0:T(4,128)S(1)}, u32[]{:S(2)}, u32[]{:S(2)}) %collective-permute-start.6) | collective-permute-done | bytes 32800 | tf_op jit(solution)/shard_map/ppermute | solution.py:39
  27.1 0.1 shard_map.96
  (4 shorter events, 0.1 us)
Async XLA Ops:
  0.0 7.1 %copy-start = (f32[1,1,4,16,2048]{4,3,2,1,0:T(8,128)S(1)}, f32[1,1,4,16,2048]{4,3,2,1,0:T(8,128)}, u32[]{:S(2)}) copy-start(f32[1,1,4,16,2048]{4,3,2,1,0:T(8,128)} %state.1) | copy-start | bytes 1572868
  1.0 8.1 %collective-permute-start = (f32[8,128]{1,0:T(8,128)S(1)}, f32[8,128]{1,0:T(8,128)S(1)}, u32[]{:S(2)}, u32[]{:S(2)}) collective-permute-start(f32[8,128]{1,0:T(8,128)S(1)} %get-tuple-element.26), channel_id=1, source_target_pairs={{0,1},{1,2},{2,3},{3,4},{4,5},{5,6},{6,7},{7,0},{8,9},{9,10},{10,1... | collective-permute-start | bytes 12296 | tf_op jit(solution)/shard_map/ppermute | solution.py:25
  4.0 5.1 %collective-permute-start.1 = (f32[8,128]{1,0:T(8,128)S(1)}, f32[8,128]{1,0:T(8,128)S(1)}, u32[]{:S(2)}, u32[]{:S(2)}) collective-permute-start(f32[8,128]{1,0:T(8,128)S(1)} %get-tuple-element.27), channel_id=1, source_target_pairs={{0,7},{1,0},{2,1},{3,2},{4,3},{5,4},{6,5},{7,6},{8,15},{9,8},{10,9... | collective-permute-start | bytes 12296 | tf_op jit(solution)/shard_map/ppermute | solution.py:25
  9.4 1.4 %collective-permute-start.2 = (f32[3,16,4,128]{3,2,1,0:T(4,128)S(1)}, f32[3,16,4,128]{3,2,1,0:T(4,128)S(1)}, u32[]{:S(2)}, u32[]{:S(2)}) collective-permute-start(f32[3,16,4,128]{3,2,1,0:T(4,128)S(1)} %get-tuple-element.39), channel_id=1, source_target_pairs={{0,8},{8,0},{16,24},{24,16},{1,9},{9,1},{17,25},{25,17},{2,10},{10... | collective-permute-start | bytes 294920 | tf_op jit(solution)/shard_map/ppermute | solution.py:46
  10.9 5.8 %collective-permute-start.3 = (f32[16,4,128]{2,1,0:T(4,128)S(1)}, f32[16,4,128]{2,1,0:T(4,128)S(1)}, u32[]{:S(2)}, u32[]{:S(2)}) collective-permute-start(f32[16,4,128]{2,1,0:T(4,128)S(1)} %get-tuple-element.41), channel_id=1, source_target_pairs={{0,2},{1,3},{2,4},{3,5},{4,6},{5,7},{6,0},{7,1},{8,11},{9,14},{10,... | collective-permute-start | bytes 98312 | tf_op jit(solution)/shard_map/ppermute | solution.py:65
  11.0 5.9 %collective-permute-start.5 = (f32[16,4,128]{2,1,0:T(4,128)S(1)}, f32[16,4,128]{2,1,0:T(4,128)S(1)}, u32[]{:S(2)}, u32[]{:S(2)}) collective-permute-start(f32[16,4,128]{2,1,0:T(4,128)S(1)} %get-tuple-element.42), channel_id=1, source_target_pairs={{0,7},{1,0},{2,1},{3,2},{4,3},{5,4},{6,5},{7,6},{8,14},{9,15},{10,... | collective-permute-start | bytes 98312 | tf_op jit(solution)/shard_map/ppermute | solution.py:65
  15.3 6.6 %collective-permute-start.4 = (f32[16,4,128]{2,1,0:T(4,128)S(1)}, f32[16,4,128]{2,1,0:T(4,128)S(1)}, u32[]{:S(2)}, u32[]{:S(2)}) collective-permute-start(f32[16,4,128]{2,1,0:T(4,128)S(1)} %get-tuple-element.43), channel_id=1, source_target_pairs={{0,1},{1,2},{2,3},{3,4},{4,5},{5,6},{6,7},{7,0},{8,13},{9,12},{10,... | collective-permute-start | bytes 98312 | tf_op jit(solution)/shard_map/ppermute | solution.py:65
  21.9 4.3 %collective-permute-start.8 = (f32[16,4,128]{2,1,0:T(4,128)S(1)}, f32[16,4,128]{2,1,0:T(4,128)S(1)}, u32[]{:S(2)}, u32[]{:S(2)}) collective-permute-start(f32[16,4,128]{2,1,0:T(4,128)S(1)} %fusion.1), channel_id=1, source_target_pairs={{0,8},{8,0},{16,24},{24,16},{1,9},{9,1},{17,25},{25,17},{2,10},{10... | collective-permute-start | bytes 98312 | tf_op jit(solution)/shard_map/ppermute | solution.py:39
  22.0 4.2 %collective-permute-start.7 = (f32[16,4,128]{2,1,0:T(4,128)S(1)}, f32[16,4,128]{2,1,0:T(4,128)S(1)}, u32[]{:S(2)}, u32[]{:S(2)}) collective-permute-start(f32[16,4,128]{2,1,0:T(4,128)S(1)} %fusion.1), channel_id=1, source_target_pairs={{0,24},{24,16},{16,8},{8,0},{1,25},{25,17},{17,9},{9,1},{2,26},{26... | collective-permute-start | bytes 98312 | tf_op jit(solution)/shard_map/ppermute | solution.py:39
  23.7 3.3 %collective-permute-start.6 = (f32[16,4,128]{2,1,0:T(4,128)S(1)}, f32[16,4,128]{2,1,0:T(4,128)S(1)}, u32[]{:S(2)}, u32[]{:S(2)}) collective-permute-start(f32[16,4,128]{2,1,0:T(4,128)S(1)} %fusion.1), channel_id=1, source_target_pairs={{8,24},{24,0},{0,16},{16,8},{9,25},{25,1},{1,17},{17,9},{10,26},{2... | collective-permute-start | bytes 98312 | tf_op jit(solution)/shard_map/ppermute | solution.py:39
